TPU v7x, 32 devices: a whole 2x2x4 slice. The times are simulated.
32 devices in a mesh: wide: 8 (over z, y), narrow: 4 (over x, core).
Axes of the slice: x: 2, y: 2, z: 4, core: 2. Of those that a mesh axis runs over, the one named last changes fastest.
Arguments:
- tokens: bfloat16 [12288, 768], P(('wide', 'narrow')), may hold values from -6 to 6
- buckets: int32 [12288], P(('wide', 'narrow')), may hold values from 0 to 255
- lengths: int32 [8, 3], P('wide'), may hold values from 1 to 1024, 1536 in all within a row
- type_table: bfloat16 [256, 768], replicated, may hold values from -3 to 3
- query_weight: bfloat16 [2, 768, 768], P(None, None, 'narrow'), may hold values from -0.3125 to 0.3125
- query_bias: bfloat16 [2, 768], P(None, 'narrow'), may hold values from -2 to 2
- key_weight: bfloat16 [2, 768, 768], P(None, None, 'narrow'), may hold values from -0.21875 to 0.21875
- value_weight: bfloat16 [2, 768, 768], P(None, None, 'narrow'), may hold values from -0.21875 to 0.21875
- value_bias: bfloat16 [2, 768], P(None, 'narrow'), may hold values from -2 to 2
- output_weight: bfloat16 [2, 768, 768], P(None, 'narrow'), may hold values from -1.25 to 1.25
- output_bias: bfloat16 [2, 768], replicated, may hold values from -2 to 2
- attention_gain: bfloat16 [2, 768], replicated, may hold values from 0.5 to 1.5
- attention_shift: bfloat16 [2, 768], replicated, may hold values from -2 to 2
- up_weight: bfloat16 [2, 768, 3072], P(None, None, 'narrow'), may hold values from -0.21875 to 0.21875
- up_bias: bfloat16 [2, 3072], P(None, 'narrow'), may hold values from -2 to 2
- down_weight: bfloat16 [2, 3072, 768], P(None, 'narrow'), may hold values from -0.109375 to 0.109375
- down_bias: bfloat16 [2, 768], replicated, may hold values from -2 to 2
- feed_gain: bfloat16 [2, 768], replicated, may hold values from 0.5 to 1.5
- feed_shift: bfloat16 [2, 768], replicated, may hold values from -2 to 2
- cotangent: bfloat16 [12288, 768], P(('wide', 'narrow')), may hold values from -6 to 6
Outputs:
- encoded: bfloat16 [12288, 768], P(('wide', 'narrow'))
- tokens_grad: float32 [12288, 768], P(('wide', 'narrow'))
- table_grad: float32 [256, 768], replicated
- query_weight_grad: float32 [2, 768, 768], P(None, None, 'narrow')
- query_bias_grad: float32 [2, 768], P(None, 'narrow')
- key_weight_grad: float32 [2, 768, 768], P(None, None, 'narrow')
- value_weight_grad: float32 [2, 768, 768], P(None, None, 'narrow')
- value_bias_grad: float32 [2, 768], P(None, 'narrow')
- output_weight_grad: float32 [2, 768, 768], P(None, 'narrow')
- output_bias_grad: float32 [2, 768], replicated
- attention_gain_grad: float32 [2, 768], replicated
- attention_shift_grad: float32 [2, 768], replicated
- up_weight_grad: float32 [2, 768, 3072], P(None, None, 'narrow')
- up_bias_grad: float32 [2, 3072], P(None, 'narrow')
- down_weight_grad: float32 [2, 3072, 768], P(None, 'narrow')
- down_bias_grad: float32 [2, 768], replicated
- feed_gain_grad: float32 [2, 768], replicated
- feed_shift_grad: float32 [2, 768], replicated
Inputs may be any that keep to these rules, and one draw needn't show every extreme that they name: In each row the lengths sum to 1536 and the largest is exactly 1024.
All inputs are finite; a program needn't handle non-finite values.
Results may differ from a plain program's by a relative error of at most 0.035.
Values may be sent and summed in bfloat16 or wider, within the bound.
No kernel may reach another device: no remote copies, remote signals or barrier semaphores. Data moves between devices by JAX's collectives and lax.ppermute only.
A program may use at most 128 MiB of HBM per device.

v0:
```python
import jax
import jax.numpy as jnp
from jax import lax
from jax.sharding import PartitionSpec as P

HEAD_DIM = 64
LAYERS = 2
QUERY_BLOCK = 512


EPS = 1e-12
ROOT_HALF = 0.7071067811865476
DENSITY = 0.3989422804014327
NEG = -1e30


def contract(matrix_left, matrix_right, left_axis, right_axis):
    return lax.dot_general(
        matrix_left,
        matrix_right,
        (((left_axis,), (right_axis,)), ((), ())),
        preferred_element_type=jnp.float32,
    )


def norm_rows(summed, gain_row, shift_row):
    row_mean = jnp.mean(summed, -1, keepdims=True)
    centred = summed - row_mean
    spread = jnp.mean(centred * centred, -1, keepdims=True)
    inverse = lax.rsqrt(spread + EPS)
    unit_rows = centred * inverse
    return (unit_rows * gain_row + shift_row, unit_rows, inverse)


def norm_back(upstream, unit_rows, inverse, gain_row):
    scaled = upstream * gain_row
    downstream = inverse * (
        scaled
        - jnp.mean(scaled, -1, keepdims=True)
        - unit_rows * jnp.mean(scaled * unit_rows, -1, keepdims=True)
    )
    return (downstream, jnp.sum(upstream * unit_rows, 0), jnp.sum(upstream, 0))


def gelu_parts(preact):
    normal_cdf = 0.5 * (1.0 + jax.scipy.special.erf(preact * ROOT_HALF))
    return (preact * normal_cdf, normal_cdf + preact * DENSITY * jnp.exp(-0.5 * preact * preact))


def item_labels(lengths, row_count):
    item_ends = jnp.cumsum(lengths[0], dtype=jnp.int32)
    places = lax.iota(jnp.int32, row_count)
    return jnp.sum((places[:, None] >= item_ends[None, :]).astype(jnp.int32), 1, dtype=jnp.int32)


def masked_scores(query_block, key_rows, label_block, labels):
    scores = jnp.einsum("qhd,khd->hqk", query_block, key_rows, preferred_element_type=jnp.float32)
    same_item = label_block[:, None] == labels[None, :]
    return jnp.where(same_item[None], scores, NEG)


def attend_forward(queries, key_rows, values, labels):
    row_count, head_count, head_width = queries.shape
    blocks = row_count // QUERY_BLOCK

    def one_block(pieces):
        query_block, label_block = pieces
        scores = masked_scores(query_block, key_rows, label_block, labels)
        row_max = jnp.max(scores, -1, keepdims=True)
        weights = jnp.exp(scores - row_max)
        totals = jnp.sum(weights, -1, keepdims=True)
        probability = (weights / totals).astype(jnp.bfloat16)
        context = jnp.einsum(
            "hqk,khd->qhd", probability, values, preferred_element_type=jnp.float32
        )
        return (context, (row_max + jnp.log(totals))[..., 0])

    context, logsum = lax.map(
        one_block,
        (
            queries.reshape(blocks, QUERY_BLOCK, head_count, head_width),
            labels.reshape(blocks, QUERY_BLOCK),
        ),
    )
    return (context.reshape(row_count, head_count * head_width), logsum)


def attend_backward(queries, key_rows, values, labels, logsum, upstream):
    row_count, head_count, head_width = queries.shape
    blocks = row_count // QUERY_BLOCK

    def one_block(carry, pieces):
        key_grad, value_grad = carry
        query_block, label_block, logsum_block, upstream_block = pieces
        scores = masked_scores(query_block, key_rows, label_block, labels)
        probability = jnp.exp(scores - logsum_block[..., None])
        value_grad = value_grad + jnp.einsum(
            "hqk,qhd->khd",
            probability.astype(jnp.bfloat16),
            upstream_block,
            preferred_element_type=jnp.float32,
        )
        prob_grad = jnp.einsum(
            "qhd,khd->hqk", upstream_block, values, preferred_element_type=jnp.float32
        )
        centre = jnp.sum(probability * prob_grad, -1, keepdims=True)
        score_grad = (probability * (prob_grad - centre)).astype(jnp.bfloat16)
        query_grad = jnp.einsum(
            "hqk,khd->qhd", score_grad, key_rows, preferred_element_type=jnp.float32
        )
        key_grad = key_grad + jnp.einsum(
            "hqk,qhd->khd", score_grad, query_block, preferred_element_type=jnp.float32
        )
        return ((key_grad, value_grad), query_grad)

    zero_grads = jnp.zeros((row_count, head_count, head_width), jnp.float32)
    shaped = (
        queries.reshape(blocks, QUERY_BLOCK, head_count, head_width),
        labels.reshape(blocks, QUERY_BLOCK),
        logsum,
        upstream.reshape(blocks, QUERY_BLOCK, head_count, head_width),
    )
    (key_grad, value_grad), query_grad = lax.scan(one_block, (zero_grads, zero_grads), shaped)
    return (query_grad.reshape(row_count, head_count, head_width), key_grad, value_grad)


def layer_parts(stream, weights, labels):
    (
        joint_weight,
        joint_bias,
        out_weight,
        out_bias,
        first_gain,
        first_shift,
        up_weight,
        up_bias,
        down_weight,
        down_bias,
        second_gain,
        second_shift,
    ) = weights
    local_width = out_weight.shape[0]
    head_count = local_width // HEAD_DIM
    query_scale = HEAD_DIM ** (-0.5)
    full_rows = lax.all_gather(stream.astype(jnp.bfloat16), "narrow", axis=0, tiled=True)
    row_count = full_rows.shape[0]
    projected = jnp.dot(full_rows, joint_weight, preferred_element_type=jnp.float32) + joint_bias
    queries = (
        (projected[:, :local_width] * query_scale)
        .astype(jnp.bfloat16)
        .reshape(row_count, head_count, HEAD_DIM)
    )
    key_rows = (
        projected[:, local_width : 2 * local_width]
        .astype(jnp.bfloat16)
        .reshape(row_count, head_count, HEAD_DIM)
    )
    values = (
        projected[:, 2 * local_width :]
        .astype(jnp.bfloat16)
        .reshape(row_count, head_count, HEAD_DIM)
    )
    context, logsum = attend_forward(queries, key_rows, values, labels)
    low_context = context.astype(jnp.bfloat16)
    attention = lax.psum_scatter(
        jnp.dot(low_context, out_weight, preferred_element_type=jnp.float32).astype(jnp.bfloat16),
        "narrow",
        scatter_dimension=0,
        tiled=True,
    ).astype(jnp.float32)
    middle, first_unit, first_inverse = norm_rows(
        stream + attention + out_bias, first_gain, first_shift
    )
    middle_rows = lax.all_gather(middle.astype(jnp.bfloat16), "narrow", axis=0, tiled=True)
    up_values = jnp.dot(middle_rows, up_weight, preferred_element_type=jnp.float32) + up_bias
    activation, slope = gelu_parts(up_values)
    low_activation = activation.astype(jnp.bfloat16)
    feed = lax.psum_scatter(
        jnp.dot(low_activation, down_weight, preferred_element_type=jnp.float32).astype(
            jnp.bfloat16
        ),
        "narrow",
        scatter_dimension=0,
        tiled=True,
    ).astype(jnp.float32)
    result, second_unit, second_inverse = norm_rows(
        middle + feed + down_bias, second_gain, second_shift
    )
    kept_parts = (
        full_rows,
        queries,
        key_rows,
        values,
        logsum,
        low_context,
        first_unit,
        first_inverse,
        middle_rows,
        slope,
        low_activation,
        second_unit,
        second_inverse,
    )
    return (result, kept_parts, (full_rows, attention, middle_rows, feed))


def layer_backward(upstream, kept_parts, weights, labels):
    (
        joint_weight,
        joint_bias,
        out_weight,
        out_bias,
        first_gain,
        first_shift,
        up_weight,
        up_bias,
        down_weight,
        down_bias,
        second_gain,
        second_shift,
    ) = weights
    (
        full_rows,
        queries,
        key_rows,
        values,
        logsum,
        low_context,
        first_unit,
        first_inverse,
        middle_rows,
        slope,
        low_activation,
        second_unit,
        second_inverse,
    ) = kept_parts
    row_count, head_count, head_width = queries.shape
    local_width = head_count * head_width
    second_total, second_gain_grad, second_shift_grad = norm_back(
        upstream, second_unit, second_inverse, second_gain
    )
    down_bias_grad = jnp.sum(second_total, 0)
    second_rows = lax.all_gather(second_total.astype(jnp.bfloat16), "narrow", axis=0, tiled=True)
    activation_grad = contract(second_rows, down_weight, 1, 1)
    down_weight_grad = contract(low_activation, second_rows, 0, 0)
    up_grad = (activation_grad * slope).astype(jnp.bfloat16)
    up_weight_grad = contract(middle_rows, up_grad, 0, 0)
    up_bias_grad = jnp.sum(up_grad, 0, dtype=jnp.float32)
    middle_grad = second_total + lax.psum_scatter(
        contract(up_grad, up_weight, 1, 1).astype(jnp.bfloat16),
        "narrow",
        scatter_dimension=0,
        tiled=True,
    ).astype(jnp.float32)
    first_total, first_gain_grad, first_shift_grad = norm_back(
        middle_grad, first_unit, first_inverse, first_gain
    )
    out_bias_grad = jnp.sum(first_total, 0)
    first_rows = lax.all_gather(first_total.astype(jnp.bfloat16), "narrow", axis=0, tiled=True)
    context_grad = contract(first_rows, out_weight, 1, 1).astype(jnp.bfloat16)
    out_weight_grad = contract(low_context, first_rows, 0, 0)
    query_grad, key_grad, value_grad = attend_backward(
        queries,
        key_rows,
        values,
        labels,
        logsum,
        context_grad.reshape(row_count, head_count, head_width),
    )
    query_scale = HEAD_DIM ** (-0.5)
    joint_grad = jnp.concatenate(
        [
            (query_grad.astype(jnp.bfloat16) * query_scale).reshape(row_count, local_width),
            key_grad.astype(jnp.bfloat16).reshape(row_count, local_width),
            value_grad.astype(jnp.bfloat16).reshape(row_count, local_width),
        ],
        1,
    )
    joint_weight_grad = contract(full_rows, joint_grad, 0, 0)
    joint_bias_grad = jnp.sum(joint_grad, 0, dtype=jnp.float32)
    downstream = first_total + lax.psum_scatter(
        contract(joint_grad, joint_weight, 1, 1).astype(jnp.bfloat16),
        "narrow",
        scatter_dimension=0,
        tiled=True,
    ).astype(jnp.float32)
    sharded = (
        joint_weight_grad[:, :local_width],
        joint_bias_grad[:local_width],
        joint_weight_grad[:, local_width : 2 * local_width],
        joint_weight_grad[:, 2 * local_width :],
        joint_bias_grad[2 * local_width :],
        out_weight_grad,
        up_weight_grad,
        up_bias_grad,
        down_weight_grad,
    )
    shared = (
        out_bias_grad,
        first_gain_grad,
        first_shift_grad,
        down_bias_grad,
        second_gain_grad,
        second_shift_grad,
    )
    return (downstream, sharded, shared)


def on_device(
    tokens,
    buckets,
    lengths,
    type_table,
    query_weight,
    query_bias,
    key_weight,
    value_weight,
    value_bias,
    output_weight,
    output_bias,
    attention_gain,
    attention_shift,
    up_weight,
    up_bias,
    down_weight,
    down_bias,
    feed_gain,
    feed_shift,
    cotangent,
):
    share_rows = tokens.shape[0]
    labels = item_labels(lengths, share_rows * lax.axis_size("narrow"))
    selector = (buckets[:, None] == lax.iota(jnp.int32, type_table.shape[0])[None, :]).astype(
        jnp.float32
    )
    stream = tokens.astype(jnp.float32) + jnp.dot(
        selector.astype(jnp.bfloat16), type_table, preferred_element_type=jnp.float32
    )
    local_width = query_bias.shape[1]
    layers = []
    whole_outs = []
    for layer_index in range(LAYERS):
        joint_weight = jnp.concatenate(
            [query_weight[layer_index], key_weight[layer_index], value_weight[layer_index]], 1
        )
        joint_bias = jnp.concatenate(
            [
                query_bias[layer_index].astype(jnp.float32),
                jnp.zeros((local_width,), jnp.float32),
                value_bias[layer_index].astype(jnp.float32),
            ]
        )
        layers.append(
            (
                joint_weight,
                joint_bias,
                output_weight[layer_index],
                output_bias[layer_index].astype(jnp.float32),
                attention_gain[layer_index].astype(jnp.float32),
                attention_shift[layer_index].astype(jnp.float32),
                up_weight[layer_index],
                up_bias[layer_index].astype(jnp.float32),
                down_weight[layer_index],
                down_bias[layer_index].astype(jnp.float32),
                feed_gain[layer_index].astype(jnp.float32),
                feed_shift[layer_index].astype(jnp.float32),
            )
        )
        whole_outs.append(None)
    inputs = []
    stored_all = []
    for layer_index in range(LAYERS):
        inputs.append(stream)
        stream, unused_parts, stored = layer_parts(stream, layers[layer_index], labels)
        stored_all.append(stored)
    encoded = stream.astype(jnp.bfloat16)
    upstream = cotangent.astype(jnp.float32)
    sharded_all = [None] * LAYERS
    shared_all = [None] * LAYERS
    for layer_index in reversed(range(LAYERS)):
        ignored, kept_parts, unused = layer_parts(inputs[layer_index], layers[layer_index], labels)
        upstream, sharded, shared = layer_backward(
            upstream, kept_parts, layers[layer_index], labels
        )
        sharded_all[layer_index] = sharded
        shared_all[layer_index] = shared
    table_grad = lax.dot_general(
        selector,
        upstream,
        (((0,), (0,)), ((), ())),
        precision=lax.Precision.HIGHEST,
        preferred_element_type=jnp.float32,
    )
    stacked = [
        jnp.stack([sharded_all[layer_index][member] for layer_index in range(LAYERS)])
        for member in range(9)
    ]
    common = [
        jnp.stack([shared_all[layer_index][member] for layer_index in range(LAYERS)])
        for member in range(6)
    ]
    summed = lax.psum(
        (
            stacked[0],
            stacked[1],
            stacked[2],
            stacked[3],
            stacked[4],
            stacked[5],
            stacked[6],
            stacked[7],
            stacked[8],
        ),
        "wide",
    )
    totals = lax.psum(
        (table_grad, common[0], common[1], common[2], common[3], common[4], common[5]),
        ("wide", "narrow"),
    )
    return (
        encoded,
        upstream,
        totals[0],
        summed[0],
        summed[1],
        summed[2],
        summed[3],
        summed[4],
        summed[5],
        totals[1],
        totals[2],
        totals[3],
        summed[6],
        summed[7],
        summed[8],
        totals[4],
        totals[5],
        totals[6],
    )


def solution(mesh):
    in_specs = (
        P(("wide", "narrow"), None),
        P(("wide", "narrow")),
        P("wide", None),
        P(),
        P(None, None, "narrow"),
        P(None, "narrow"),
        P(None, None, "narrow"),
        P(None, None, "narrow"),
        P(None, "narrow"),
        P(None, "narrow", None),
        P(),
        P(),
        P(),
        P(None, None, "narrow"),
        P(None, "narrow"),
        P(None, "narrow", None),
        P(),
        P(),
        P(),
        P(("wide", "narrow"), None),
    )
    out_specs = (
        P(("wide", "narrow"), None),
        P(("wide", "narrow"), None),
        P(),
        P(None, None, "narrow"),
        P(None, "narrow"),
        P(None, None, "narrow"),
        P(None, None, "narrow"),
        P(None, "narrow"),
        P(None, "narrow", None),
        P(),
        P(),
        P(),
        P(None, None, "narrow"),
        P(None, "narrow"),
        P(None, "narrow", None),
        P(),
        P(),
        P(),
    )
    return jax.shard_map(
        on_device, mesh=mesh, in_specs=in_specs, out_specs=out_specs, check_vma=False
    )
```

profile of v0, /device:TPU:1, one launch (start us, length us, event | category | flops | bytes accessed | tf_op | source)
XLA Modules:
  0.0 1561.6 jit_solution(9326111932193779432)
XLA Ops:
  13.6 24.0 %all-gather.11.cloned.1.call-done = bf16[1536,768]{1,0:T(8,128)(2,1)} async-done(((bf16[384,768]{1,0:T(8,128)(2,1)}), bf16[1536,768]{1,0:T(8,128)(2,1)}) %all-gather.11.cloned.1.call-update) | async-done | bytes 2359312 | tf_op jit(solution)/shard_map/all_gather | solution.py:145
  42.5 39.7 %while.74 = (s32[]{:T(128)}, bf16[3,512,3,64]{1,3,2,0:T(8,128)(2,1)}, s32[3,512]{1,0:T(4,128)S(1)}, s32[1536]{0:T(1024)S(1)}, bf16[3,512,3,64]{1,3,2,0:T(8,128)(...) while((s32[]{:T(128)}, bf16[3,512,3,64]{1,3,2,0:T(8,128)(2,1)}, ...), condition=%wide.region_5.6_spmd, body=%wide.region_2.5_spmd.sunk | while | flops 616564224 | bytes 22241384 | solution.py:78
  120.4 35.0 %reduce-scatter.21.cloned.1.call-done = bf16[384,768]{1,0:T(8,128)(2,1)} async-done(((bf16[1536,768]{1,0:T(8,128)(2,1)}), bf16[384,768]{1,0:T(8,128)(2,1)}) %reduce-scatter.21.cloned.1.call-update) | async-done | bytes 589840 | tf_op jit(solution)/shard_map/reduce_scatter | solution.py:165
  160.3 23.4 %all-gather.13.cloned.1.call-done = bf16[1536,768]{1,0:T(8,128)(2,1)} async-done(((bf16[384,768]{1,0:T(8,128)(2,1)}), bf16[1536,768]{1,0:T(8,128)(2,1)}) %all-gather.13.cloned.1.call-update) | async-done | bytes 2359312 | tf_op jit(solution)/shard_map/all_gather | solution.py:174
  244.9 36.4 %reduce-scatter.23.cloned.1.call-done = bf16[384,768]{1,0:T(8,128)(2,1)} async-done(((bf16[1536,768]{1,0:T(8,128)(2,1)}), bf16[384,768]{1,0:T(8,128)(2,1)}) %reduce-scatter.23.cloned.1.call-update) | async-done | bytes 589840 | tf_op jit(solution)/shard_map/reduce_scatter | solution.py:178
  287.3 24.4 %all-gather.15.cloned.1.call-done = bf16[1536,768]{1,0:T(8,128)(2,1)} async-done(((bf16[384,768]{1,0:T(8,128)(2,1)}), bf16[1536,768]{1,0:T(8,128)(2,1)}) %all-gather.15.cloned.1.call-update) | async-done | bytes 2359312 | tf_op jit(solution)/shard_map/all_gather | solution.py:145
  316.6 39.7 %while.75 = (s32[]{:T(128)}, bf16[3,512,3,64]{1,3,2,0:T(8,128)(2,1)}, s32[3,512]{1,0:T(4,128)S(1)}, s32[1536]{0:T(1024)S(1)}, bf16[3,512,3,64]{1,3,2,0:T(8,128)(...) while((s32[]{:T(128)}, ...), condition=%wide.region_15.16_spmd, body=%wide.region_12.15_spmd.sunk | while | flops 616564224 | bytes 22241384 | solution.py:78
  393.2 36.3 %reduce-scatter.25.cloned.1.call-done = bf16[384,768]{1,0:T(8,128)(2,1)} async-done(((bf16[1536,768]{1,0:T(8,128)(2,1)}), bf16[384,768]{1,0:T(8,128)(2,1)}) %reduce-scatter.25.cloned.1.call-update) | async-done | bytes 589840 | tf_op jit(solution)/shard_map/reduce_scatter | solution.py:165
  434.6 24.0 %all-gather.17.cloned.1.call-done = bf16[1536,768]{1,0:T(8,128)(2,1)} async-done(((bf16[384,768]{1,0:T(8,128)(2,1)}), bf16[1536,768]{1,0:T(8,128)(2,1)}) %all-gather.17.cloned.1.call-update) | async-done | bytes 2359312 | tf_op jit(solution)/shard_map/all_gather | solution.py:174
  496.4 23.5 %reduce-scatter.19.cloned.1.call-done = bf16[384,768]{1,0:T(8,128)(2,1)} async-done(((bf16[1536,768]{1,0:T(8,128)(2,1)}), bf16[384,768]{1,0:T(8,128)(2,1)}) %reduce-scatter.19.cloned.1.call-update) | async-done | bytes 589840 | tf_op jit(solution)/shard_map/reduce_scatter | solution.py:178
  519.9 35.7 %reduce-scatter.27.cloned.1.call-done = bf16[384,768]{1,0:T(8,128)(2,1)} async-done(((bf16[1536,768]{1,0:T(8,128)(2,1)}), bf16[384,768]{1,0:T(8,128)(2,1)}) %reduce-scatter.27.cloned.1.call-update) | async-done | bytes 589840 | tf_op jit(solution)/shard_map/reduce_scatter | solution.py:178
  562.0 24.6 %all-gather.23.cloned.1.call-done = bf16[1536,768]{1,0:T(8,128)(2,1)} async-done(((bf16[384,768]{1,0:T(8,128)(2,1)}), bf16[1536,768]{1,0:T(8,128)(2,1)}) %all-gather.23.cloned.1.call-update) | async-done | bytes 2359312 | tf_op jit(solution)/shard_map/all_gather | solution.py:243
  599.1 32.7 %reduce-scatter.29.cloned.1.call-done = bf16[384,768]{1,0:T(8,128)(2,1)} async-done(((bf16[1536,768]{1,0:T(8,128)(2,1)}), bf16[384,768]{1,0:T(8,128)(2,1)}) %reduce-scatter.29.cloned.1.call-update) | async-done | bytes 589840 | tf_op jit(solution)/shard_map/reduce_scatter | solution.py:249
  636.2 24.4 %all-gather.25.cloned.1.call-done = bf16[1536,768]{1,0:T(8,128)(2,1)} async-done(((bf16[384,768]{1,0:T(8,128)(2,1)}), bf16[1536,768]{1,0:T(8,128)(2,1)}) %all-gather.25.cloned.1.call-update) | async-done | bytes 2359312 | tf_op jit(solution)/shard_map/all_gather | solution.py:259
  669.1 48.9 %while.78 = (s32[]{:T(128)}, f32[1536,3,64]{0,2,1:T(8,128)S(1)}, f32[1536,3,64]{0,2,1:T(8,128)S(1)}, bf16[3,512,3,64]{1,3,2,0:T(8,128)(2,1)}, bf16[3,512,3,64]{1...) while((s32[]{:T(128)}, f32[1536,3,64]{0,2,1:T(8,128)S(1)}, ...), condition=%wide.region_49.50_spmd.clone, body=%wide.region_47.49_spmd.clone.sunk | while | flops 1540225536 | bytes 88729848 | solution.py:123
  725.9 31.3 %reduce-scatter.31.cloned.1.call-done = bf16[384,768]{1,0:T(8,128)(2,1)} async-done(((bf16[1536,768]{1,0:T(8,128)(2,1)}), bf16[384,768]{1,0:T(8,128)(2,1)}) %reduce-scatter.31.cloned.1.call-update) | async-done | bytes 589840 | tf_op jit(solution)/shard_map/reduce_scatter | solution.py:281
  761.6 24.6 %all-gather.27.cloned.1.call-done = bf16[1536,768]{1,0:T(8,128)(2,1)} async-done(((bf16[384,768]{1,0:T(8,128)(2,1)}), bf16[1536,768]{1,0:T(8,128)(2,1)}) %all-gather.27.cloned.1.call-update) | async-done | bytes 2359312 | tf_op jit(solution)/shard_map/all_gather | solution.py:243
  798.7 32.8 %reduce-scatter.33.cloned.1.call-done = bf16[384,768]{1,0:T(8,128)(2,1)} async-done(((bf16[1536,768]{1,0:T(8,128)(2,1)}), bf16[384,768]{1,0:T(8,128)(2,1)}) %reduce-scatter.33.cloned.1.call-update) | async-done | bytes 589840 | tf_op jit(solution)/shard_map/reduce_scatter | solution.py:249
  836.9 24.6 %all-gather.29.cloned.1.call-done = bf16[1536,768]{1,0:T(8,128)(2,1)} async-done(((bf16[384,768]{1,0:T(8,128)(2,1)}), bf16[1536,768]{1,0:T(8,128)(2,1)}) %all-gather.29.cloned.1.call-update) | async-done | bytes 2359312 | tf_op jit(solution)/shard_map/all_gather | solution.py:259
  870.3 48.7 %while.79 = (s32[]{:T(128)}, f32[1536,3,64]{0,2,1:T(8,128)S(1)}, f32[1536,3,64]{0,2,1:T(8,128)S(1)}, bf16[3,512,3,64]{1,3,2,0:T(8,128)(2,1)}, bf16[3,512,3,64]{1...) while((s32[]{:T(128)}, f32[1536,3,64]{0,2,1:T(8,128)S(1)}, ...), condition=%wide.region_58.59_spmd.clone, body=%wide.region_56.58_spmd.clone.sunk | while | flops 1540225536 | bytes 88729848 | solution.py:123
  975.3 40.0 %all-reduce = (f32[2,768]{1,0:T(2,128)}, f32[2,768]{1,0:T(2,128)}, f32[2,768]{1,0:T(2,128)}, f32[2,768]{1,0:T(2,128)}, f32[2,768]{1,0:T(2,128)}, /*index=5*/f32[2,768]{1,0:T(2,128)}) all-reduce(f32[2,768]{1,0:T(2,128)S(1)} %pad_maximum_fusion.14, ...), channel_id=1, replica_groups=mesh['wide'=8,'narrow'=4] {'wide','narrow'}, use_global_device_ids=true, to_apply=%region_71.72 | all-reduce | flops 9216 | bytes 73728 | tf_op jit(solution)/shard_map/psum | solution.py:416
  1015.7 29.6 %all-reduce.1 = (f32[2,192]{1,0:T(2,128)}, f32[2,192]{1,0:T(2,128)}, f32[2,768]{1,0:T(2,128)}) all-reduce(f32[2,192]{1,0:T(2,128)S(1)} %pad_maximum_fusion.23, f32[2,192]{1,0:T(2,128)S(1)} %pad_maximum_fusion.24, f32[2,768]{1,0:T(2,128)S(1)} %pad_maximum_fusion.17), channel_id=1, replica_groups=mesh['wide'=8,'narrow'=4] {'wide'}, use_global_device_ids=true, to_apply=%region_64.65 | all-reduce | flops 2304 | bytes 18432 | tf_op jit(solution)/shard_map/psum | solution.py:402
  1045.3 47.0 %all-reduce.6.cloned.1.call-done = f32[256,768]{1,0:T(8,128)} async-done(((f32[256,768]{1,0:T(8,128)}), f32[256,768]{1,0:T(8,128)}) %all-reduce.6.cloned.1.call-update) | async-done | bytes 786448 | tf_op jit(solution)/shard_map/psum | solution.py:416
  1092.2 449.3 %all-reduce.8.cloned.1.call-done = (f32[2,768,192]{1,2,0:T(8,128)}, f32[2,768,192]{1,2,0:T(8,128)}, f32[2,768,192]{1,2,0:T(8,128)}, f32[2,192,768]{2,1,0:T(8,128...) async-done(((f32[2,768,192]{1,2,0:T(8,128)}, f32[2,768,192]{1,2,0:T(8,128)}, f32[2,768,192]{1,2,0:T(8,128)}, f32[2,192,768]{2,1,0:T(8,128)}, f32[2,768,768]{2,1,0:T(8,128)}, ...) | async-done | bytes 14155792 | tf_op jit(solution)/shard_map/psum | solution.py:402
  (650 shorter events, 567.3 us)
Async XLA Ops:
  7.3 30.3 %all-gather.11.cloned.1.call-start = ((), (), s32[]{:S(2)}) async-start(), calls=%async_computation.12 | async-start | bytes 2949120 | tf_op jit(solution)/shard_map/all_gather | solution.py:145
  10.9 108.2 %reduce-scatter.13.cloned.1.call-start = ((), (), s32[]{:S(2)}) async-start(), calls=%async_computation.13 | async-start | bytes 2949120 | tf_op jit(solution)/shard_map/reduce_scatter | solution.py:165
  86.3 69.1 %reduce-scatter.21.cloned.1.call-start = ((), (), s32[]{:S(2)}) async-start(), calls=%async_computation.20 | async-start | bytes 2949120 | tf_op jit(solution)/shard_map/reduce_scatter | solution.py:165
  116.7 67.0 %all-gather.13.cloned.1.call-start = ((), (), s32[]{:S(2)}) async-start(), calls=%async_computation.14 | async-start | bytes 2949120 | tf_op jit(solution)/shard_map/all_gather | solution.py:174
  159.1 50.7 %all-gather.19.cloned.1.call-start = ((), (), s32[]{:S(2)}) async-start(), calls=%async_computation.21 | async-start | bytes 2949120 | tf_op jit(solution)/shard_map/all_gather | solution.py:174
  159.7 85.2 %reduce-scatter.15.cloned.1.call-start = ((), (), s32[]{:S(2)}) async-start(), calls=%async_computation.15 | async-start | bytes 2949120 | tf_op jit(solution)/shard_map/reduce_scatter | solution.py:178
  191.0 90.2 %reduce-scatter.23.cloned.1.call-start = ((), (), s32[]{:S(2)}) async-start(), calls=%async_computation.22 | async-start | bytes 2949120 | tf_op jit(solution)/shard_map/reduce_scatter | solution.py:178
  221.3 90.4 %all-gather.15.cloned.1.call-start = ((), (), s32[]{:S(2)}) async-start(), calls=%async_computation.16 | async-start | bytes 2949120 | tf_op jit(solution)/shard_map/all_gather | solution.py:145
  287.1 106.1 %reduce-scatter.17.cloned.1.call-start = ((), (), s32[]{:S(2)}) async-start(), calls=%async_computation.17 | async-start | bytes 2949120 | tf_op jit(solution)/shard_map/reduce_scatter | solution.py:165
  360.4 69.0 %reduce-scatter.25.cloned.1.call-start = ((), (), s32[]{:S(2)}) async-start(), calls=%async_computation.23 | async-start | bytes 2949120 | tf_op jit(solution)/shard_map/reduce_scatter | solution.py:165
  390.4 68.2 %all-gather.17.cloned.1.call-start = ((), (), s32[]{:S(2)}) async-start(), calls=%async_computation.18 | async-start | bytes 2949120 | tf_op jit(solution)/shard_map/all_gather | solution.py:174
  434.0 50.7 %all-gather.21.cloned.1.call-start = ((), (), s32[]{:S(2)}) async-start(), calls=%async_computation.24 | async-start | bytes 2949120 | tf_op jit(solution)/shard_map/all_gather | solution.py:174
  434.6 85.3 %reduce-scatter.19.cloned.1.call-start = ((), (), s32[]{:S(2)}) async-start(), calls=%async_computation.19 | async-start | bytes 2949120 | tf_op jit(solution)/shard_map/reduce_scatter | solution.py:178
  466.0 89.6 %reduce-scatter.27.cloned.1.call-start = ((), (), s32[]{:S(2)}) async-start(), calls=%async_computation.25 | async-start | bytes 2949120 | tf_op jit(solution)/shard_map/reduce_scatter | solution.py:178
  496.4 90.2 %all-gather.23.cloned.1.call-start = ((), (), s32[]{:S(2)}) async-start(), calls=%async_computation.26 | async-start | bytes 2949120 | tf_op jit(solution)/shard_map/all_gather | solution.py:243
  561.9 69.9 %reduce-scatter.29.cloned.1.call-start = ((), (), s32[]{:S(2)}) async-start(), calls=%async_computation.27 | async-start | bytes 2949120 | tf_op jit(solution)/shard_map/reduce_scatter | solution.py:249
  599.1 61.5 %all-gather.25.cloned.1.call-start = ((), (), s32[]{:S(2)}) async-start(), calls=%async_computation.28 | async-start | bytes 2949120 | tf_op jit(solution)/shard_map/all_gather | solution.py:259
  636.0 121.2 %reduce-scatter.31.cloned.1.call-start = ((), (), s32[]{:S(2)}) async-start(), calls=%async_computation.29 | async-start | bytes 2949120 | tf_op jit(solution)/shard_map/reduce_scatter | solution.py:281
  724.4 61.8 %all-gather.27.cloned.1.call-start = ((), (), s32[]{:S(2)}) async-start(), calls=%async_computation.30 | async-start | bytes 2949120 | tf_op jit(solution)/shard_map/all_gather | solution.py:243
  761.5 69.9 %reduce-scatter.33.cloned.1.call-start = ((), (), s32[]{:S(2)}) async-start(), calls=%async_computation.31 | async-start | bytes 2949120 | tf_op jit(solution)/shard_map/reduce_scatter | solution.py:249
  798.6 62.8 %all-gather.29.cloned.1.call-start = ((), (), s32[]{:S(2)}) async-start(), calls=%async_computation.32 | async-start | bytes 2949120 | tf_op jit(solution)/shard_map/all_gather | solution.py:259
  836.8 121.4 %reduce-scatter.35.cloned.1.call-start = ((), (), s32[]{:S(2)}) async-start(), calls=%async_computation.33 | async-start | bytes 2949120 | tf_op jit(solution)/shard_map/reduce_scatter | solution.py:281
  925.5 166.7 %all-reduce.6.cloned.1.call-start = ((), (), s32[]{:S(2)}) async-start(), calls=%async_computation.34 | async-start | bytes 1572864 | tf_op jit(solution)/shard_map/psum | solution.py:416
  961.5 580.0 %all-reduce.8.cloned.1.call-start = ((), (), s32[]{:S(2)}) async-start(), calls=%async_computation.35 | async-start | bytes 28311552 | tf_op jit(solution)/shard_map/psum | solution.py:402
  (151 other events, 1797.2 us)
Sparse Core Ops, SparseCore 0:
  11.0 26.5 all-gather.10
  86.4 32.6 reduce-scatter.12
  122.4 33.0 reduce-scatter.20
  159.2 24.4 all-gather.12
  185.7 24.0 all-gather.18
  212.2 32.6 reduce-scatter.14
  248.1 33.0 reduce-scatter.22
  287.2 24.4 all-gather.14
  360.5 32.6 reduce-scatter.16
  396.3 33.0 reduce-scatter.24
  434.1 24.4 all-gather.16
  460.6 24.0 all-gather.20
  487.2 32.6 reduce-scatter.18
  522.5 33.0 reduce-scatter.26
  562.1 24.4 all-gather.22
  599.2 32.6 reduce-scatter.28
  636.1 24.4 all-gather.24
  724.5 32.6 reduce-scatter.30
  761.7 24.4 all-gather.26
  798.8 32.6 reduce-scatter.32
  836.9 24.4 all-gather.28
  925.6 32.6 reduce-scatter.34
  964.0 128.1 all-reduce.5
  1099.4 442.0 all-reduce.7
where the time goes:
time: 1570 us; the launch traced here: 1560 us
  waiting for transfers between devices  1020 us (65%)
  matrix products  282 us (18%)
  other arithmetic  94.6 us (6%)
  local copies, waits for them, and re-layouts  74.5 us (5%)
  blocking collectives  69.6 us (4%)
  between operations  16.1 us (1%)
    psum x1, waiting for transfers between devices, on_device(): lax.psum((stacked[0], stacked[1], stacked[2], stacked[3], stacked[4], sta...  449 us
    reduce_scatter x4, waiting for transfers between devices, layer_parts(): lax.psum_scatter(jnp.dot(low_activation, down_weight, preferred_element_t...  117 us
    all_gather x4, waiting for transfers between devices, layer_parts(): lax.all_gather(middle.astype(jnp.bfloat16), 'narrow', axis=0, tiled=True)  84.2 us
    reduce_scatter x4, waiting for transfers between devices, layer_parts(): lax.psum_scatter(jnp.dot(low_context, out_weight, preferred_element_type=...  75.1 us
    reduce_scatter x2, waiting for transfers between devices, layer_backward(): lax.psum_scatter(contract(up_grad, up_weight, 1, 1).astype(jnp.bfloat16),...  65.5 us
    dot_general x12, matrix products, one_block(): jnp.einsum('hqk,khd->qhd', probability, values, preferred_element_type=jn...  52.6 us
    dot_general x16, matrix products, contract(): lax.dot_general(matrix_left, matrix_right, (((left_axis,), (right_axis,))...  50.8 us
    all_gather x2, waiting for transfers between devices, layer_backward(): lax.all_gather(second_total.astype(jnp.bfloat16), 'narrow', axis=0, tiled...  49.2 us
  transfers between devices with their start and end apart: 24, of which 24 were waited for; matrix products, arithmetic and copies ran while one was open for 9% of the time, Pallas kernels for 0%

commit v1 on v0

v1 whole, which is shorter than its diff:
```python
import functools

import jax
import jax.numpy as jnp
from jax import lax
from jax.experimental import pallas as pl
from jax.experimental.pallas import tpu as pltpu
from jax.sharding import PartitionSpec as P

HEAD_DIM = 64
LAYERS = 2
CHUNK = 256
EPS = 1e-12
ROOT_HALF = 0.7071067811865476
DENSITY = 0.3989422804014327
NEG = -1e30
F32 = jnp.float32
BF16 = jnp.bfloat16
MIB = 1 << 20
CORE_SWAP = [(0, 1), (1, 0), (2, 3), (3, 2)]
CHIP_SWAP = [(0, 2), (2, 0), (1, 3), (3, 1)]


def over_core(value):
    return lax.ppermute(value, "narrow", CORE_SWAP)


def over_chip(value):
    return lax.ppermute(value, "narrow", CHIP_SWAP)


def dot(left, right, left_axis=1, right_axis=0):
    return lax.dot_general(
        left, right, (((left_axis,), (right_axis,)), ((), ())), preferred_element_type=F32
    )


def norm_parts(summed):
    row_mean = jnp.mean(summed, -1, keepdims=True)
    centred = summed - row_mean
    spread = jnp.mean(centred * centred, -1, keepdims=True)
    inverse = lax.rsqrt(spread + EPS)
    return centred * inverse, inverse


def norm_back(upstream, unit_rows, inverse, gain_row):
    scaled = upstream * gain_row
    return inverse * (
        scaled
        - jnp.mean(scaled, -1, keepdims=True)
        - unit_rows * jnp.mean(scaled * unit_rows, -1, keepdims=True)
    )


def gelu_parts(preact):
    size = jnp.abs(preact) * ROOT_HALF
    bell = jnp.exp(-(size * size))
    step = 1.0 / (1.0 + 0.3275911 * size)
    series = step * (
        0.254829592
        + step * (-0.284496736 + step * (1.421413741 + step * (-1.453152027 + step * 1.061405429)))
    )
    tail = 0.5 * series * bell
    cdf = jnp.where(preact >= 0.0, 1.0 - tail, tail)
    return preact * cdf, cdf + preact * DENSITY * bell


def whole(shape):
    zeros = (0,) * len(shape)
    return pl.BlockSpec(shape, lambda *ids: zeros)


def call(kernel, grid, inputs, outputs, scratch=(), flops=0, moved=0, limit=40):
    arrays = [array for array, spec in inputs]
    specs = [spec for array, spec in inputs]
    aliases = {}
    for place, (shape, dtype, spec, buffer) in enumerate(outputs):
        if buffer is not None:
            aliases[len(arrays)] = place
            arrays.append(buffer)
            specs.append(pl.BlockSpec(memory_space=pl.ANY))
    given, extra, out_count = len(inputs), len(aliases), len(outputs)

    def body(*refs):
        kernel(*refs[:given], *refs[given + extra :])

    return pl.pallas_call(
        body,
        grid=grid,
        in_specs=specs,
        out_specs=[spec for shape, dtype, spec, buffer in outputs],
        out_shape=[
            jax.ShapeDtypeStruct(shape, dtype) for shape, dtype, spec, buffer in outputs
        ],
        scratch_shapes=list(scratch),
        input_output_aliases=aliases,
        compiler_params=pltpu.CompilerParams(vmem_limit_bytes=limit * MIB),
        cost_estimate=pl.CostEstimate(flops=flops, bytes_accessed=moved, transcendentals=0),
    )(*arrays)


def gather_kernel(own_ref, other_ref, rows_ref, turned_ref):
    place = pl.program_id(0)
    half = pl.num_programs(0) // 2

    def put(source):
        tile = source[0]
        rows_ref[0] = tile
        turned_ref[0] = tile.astype(F32).T.astype(BF16)

    @pl.when(place < half)
    def _():
        put(own_ref)

    @pl.when(place >= half)
    def _():
        put(other_ref)


def split_pairs(pair_block, target, head_count):
    lanes = lax.broadcasted_iota(jnp.int32, (CHUNK, 2 * HEAD_DIM), 1)
    low_half = lanes < HEAD_DIM
    for head in range(head_count):
        pair = pair_block[:, (head // 2) * 128 : (head // 2) * 128 + 128]
        keep = low_half if head % 2 == 0 else jnp.logical_not(low_half)
        target[head] = jnp.where(keep, pair, jnp.zeros_like(pair))


def attend_kernel(
    head_count,
    place,
    bits_ref,
    q_ref,
    kv_ref,
    turned_ref,
    q_label_ref,
    k_label_ref,
    out_weight_ref,
    context_ref,
    exact_ref,
    logsum_ref,
    share_ref,
    masked_q,
    total,
    top,
    mass,
):
    width = head_count * HEAD_DIM
    split_pairs(q_ref[...], masked_q, head_count)
    top[...] = jnp.full_like(top, NEG)
    mass[...] = jnp.zeros_like(mass)
    total[...] = jnp.zeros_like(total)
    tiles = kv_ref.shape[0]
    q_bits = bits_ref[tiles + place]

    def one_tile(tile, carry):
        @pl.when((bits_ref[tile] & q_bits) != 0)
        def _():
            hide = jnp.where(k_label_ref[tile] == q_label_ref[...], 0.0, NEG)
            for head in range(head_count):
                pair = (head // 2) * 128
                scores = dot(kv_ref[tile, :, pair : pair + 128], masked_q[head], 1, 1) + hide
                old_top = top[head : head + 1, :]
                new_top = jnp.maximum(old_top, jnp.max(scores, 0, keepdims=True))
                weights = jnp.exp(scores - new_top)
                fade = jnp.exp(old_top - new_top)
                top[head : head + 1, :] = new_top
                mass[head : head + 1, :] = mass[head : head + 1, :] * fade + jnp.sum(
                    weights, 0, keepdims=True
                )
                rows = slice(head * HEAD_DIM, (head + 1) * HEAD_DIM)
                total[rows, :] = total[rows, :] * fade + dot(
                    turned_ref[tile, width + head * HEAD_DIM : width + (head + 1) * HEAD_DIM, :],
                    weights.astype(BF16),
                )

        return carry

    lax.fori_loop(0, tiles, one_tile, 0)
    for head in range(head_count):
        rows = slice(head * HEAD_DIM, (head + 1) * HEAD_DIM)
        total[rows, :] = total[rows, :] / mass[head : head + 1, :]
    exact = total[...].T
    exact_ref[...] = exact
    context = exact.astype(BF16)
    context_ref[...] = context
    live = slice(0, head_count)
    logsum_ref[0] = jnp.zeros_like(logsum_ref[0])
    logsum_ref[0, live, :] = top[live, :] + jnp.log(mass[live, :])
    share_ref[...] = dot(context, out_weight_ref[0]).astype(BF16)


def attend_back_kernel(
    head_count,
    bits_ref,
    q_ref,
    kv_ref,
    turned_ref,
    q_label_ref,
    k_label_ref,
    grad_ref,
    exact_ref,
    logsum_ref,
    q_grad_ref,
    own_ref,
    other_ref,
    masked_q,
    masked_grad,
    centre,
    q_total,
    kv_total,
):
    place = pl.program_id(0)
    width = head_count * HEAD_DIM
    tiles = kv_ref.shape[0]

    @pl.when(place == 0)
    def _():
        kv_total[...] = jnp.zeros_like(kv_total)

    split_pairs(q_ref[...], masked_q, head_count)
    split_pairs(grad_ref[...], masked_grad, head_count)
    crossed = (grad_ref[...].astype(F32) * exact_ref[...]).T
    for head in range(head_count):
        rows = slice(head * HEAD_DIM, (head + 1) * HEAD_DIM)
        centre[head : head + 1, :] = jnp.sum(crossed[rows, :], 0, keepdims=True)
    q_total[...] = jnp.zeros_like(q_total)
    q_bits = bits_ref[tiles + place]

    def one_tile(tile, carry):
        @pl.when((bits_ref[tile] & q_bits) != 0)
        def _():
            hide = jnp.where(k_label_ref[tile] == q_label_ref[0], 0.0, NEG)
            for pair in range(head_count // 2):
                lanes = slice(pair * 128, pair * 128 + 128)
                v_lanes = slice(width + pair * 128, width + pair * 128 + 128)
                key_part = None
                value_part = None
                for head in (2 * pair, 2 * pair + 1):
                    scores = dot(kv_ref[tile, :, lanes], masked_q[head], 1, 1) + hide
                    weights = jnp.exp(scores - logsum_ref[0, head : head + 1, :])
                    weight_grad = dot(kv_ref[tile, :, v_lanes], masked_grad[head], 1, 1)
                    score_grad = (weights * (weight_grad - centre[head : head + 1, :])).astype(
                        BF16
                    )
                    value_now = dot(weights.astype(BF16), masked_grad[head])
                    key_now = dot(score_grad, masked_q[head])
                    value_part = value_now if value_part is None else value_part + value_now
                    key_part = key_now if key_part is None else key_part + key_now
                    rows = slice(head * HEAD_DIM, (head + 1) * HEAD_DIM)
                    q_total[rows, :] += dot(turned_ref[tile, rows, :], score_grad)
                kv_total[tile, :, lanes] += key_part
                kv_total[tile, :, v_lanes] += value_part

        return carry

    lax.fori_loop(0, tiles, one_tile, 0)
    q_grad_ref[...] = q_total[...].T.astype(BF16) * jnp.asarray(HEAD_DIM**-0.5, BF16)

    @pl.when(place == pl.num_programs(0) - 1)
    def _():
        own_ref[...] = kv_total[: tiles // 2]
        other_ref[...] = kv_total[tiles // 2 :].astype(BF16)


def feed_kernel(
    steps,
    unit_ref,
    share_ref,
    recv_ref,
    vec_ref,
    up_own_ref,
    up_other_ref,
    bias_ref,
    down_own_ref,
    down_other_ref,
    new_unit_ref,
    inverse_ref,
    low_ref,
    act_ref,
    slope_ref,
    part_ref,
    low_rows,
    total,
):
    step = pl.program_id(0)

    @pl.when(step == 0)
    def _():
        stream = unit_ref[...] * vec_ref[0, 6:7, :] + vec_ref[0, 7:8, :]
        attention = share_ref[...].astype(F32) + recv_ref[...].astype(F32)
        unit, inverse = norm_parts(stream + attention + vec_ref[0, 0:1, :])
        new_unit_ref[...] = unit
        inverse_ref[...] = inverse
        low = (unit * vec_ref[0, 1:2, :] + vec_ref[0, 2:3, :]).astype(BF16)
        low_ref[...] = low
        low_rows[...] = low
        total[...] = jnp.zeros_like(total)

    def half(up_ref, down_ref):
        act, slope = gelu_parts(dot(low_rows[...], up_ref[0]) + bias_ref[0])
        low_act = act.astype(BF16)
        act_ref[...] = low_act
        slope_ref[...] = slope.astype(BF16)
        total[...] += dot(low_act, down_ref[0])

    @pl.when(step < steps // 2)
    def _():
        half(up_own_ref, down_own_ref)

    @pl.when(step >= steps // 2)
    def _():
        half(up_other_ref, down_other_ref)

    @pl.when(step == steps - 1)
    def _():
        part_ref[...] = total[...].astype(BF16)


def project_kernel(
    unit_ref,
    share_ref,
    recv_ref,
    vec_ref,
    q_weight_ref,
    kv_weight_ref,
    q_bias_ref,
    kv_bias_ref,
    new_unit_ref,
    inverse_ref,
    low_ref,
    q_ref,
    kv_ref,
):
    middle = unit_ref[...] * vec_ref[0, 1:2, :] + vec_ref[0, 2:3, :]
    feed = share_ref[...].astype(F32) + recv_ref[...].astype(F32)
    unit, inverse = norm_parts(middle + feed + vec_ref[0, 3:4, :])
    new_unit_ref[...] = unit
    inverse_ref[...] = inverse
    low = (unit * vec_ref[0, 4:5, :] + vec_ref[0, 5:6, :]).astype(BF16)
    low_ref[...] = low
    kv_ref[0] = (dot(low, kv_weight_ref[0]) + kv_bias_ref[0]).astype(BF16)
    q_ref[...] = ((dot(low, q_weight_ref[0]) + q_bias_ref[0]) * HEAD_DIM**-0.5).astype(BF16)


def feed_back_kernel(
    steps,
    top_layer,
    up_ref,
    unit_ref,
    inverse_ref,
    share_ref,
    recv_ref,
    vec_ref,
    slope_ref,
    up_own_ref,
    up_other_ref,
    down_own_ref,
    down_other_ref,
    encoded_ref,
    total_ref,
    low_ref,
    grad_ref,
    bias_ref,
    sums_ref,
    part_ref,
    low_rows,
    total,
):
    step = pl.program_id(0)

    @pl.when(step == 0)
    def _():
        added = share_ref[...].astype(F32) + recv_ref[...].astype(F32)
        if top_layer:
            middle = unit_ref[...] * vec_ref[0, 1:2, :] + vec_ref[0, 2:3, :]
            unit, inverse = norm_parts(middle + added + vec_ref[0, 3:4, :])
            encoded_ref[...] = (unit * vec_ref[0, 4:5, :] + vec_ref[0, 5:6, :]).astype(BF16)
            upstream = up_ref[...].astype(F32)
        else:
            unit = unit_ref[...]
            inverse = inverse_ref[...]
            upstream = up_ref[...] + added
        second = norm_back(upstream, unit, inverse, vec_ref[0, 4:5, :])
        sums_ref[...] = jnp.zeros_like(sums_ref)
        sums_ref[0:1, :] = jnp.sum(upstream * unit, 0, keepdims=True)
        sums_ref[1:2, :] = jnp.sum(upstream, 0, keepdims=True)
        sums_ref[2:3, :] = jnp.sum(second, 0, keepdims=True)
        total_ref[...] = second
        low = second.astype(BF16)
        low_ref[...] = low
        low_rows[...] = low
        total[...] = jnp.zeros_like(total)

    def half(up_weight_ref, down_ref):
        grad = (dot(low_rows[...], down_ref[0], 1, 1) * slope_ref[...].astype(F32)).astype(BF16)
        grad_ref[...] = grad
        bias_ref[...] = jnp.sum(grad.astype(F32), 0, keepdims=True)
        total[...] += dot(grad, up_weight_ref[0], 1, 1)

    @pl.when(step < steps // 2)
    def _():
        half(up_own_ref, down_own_ref)

    @pl.when(step >= steps // 2)
    def _():
        half(up_other_ref, down_other_ref)

    @pl.when(step == steps - 1)
    def _():
        part_ref[...] = total[...].astype(BF16)


def context_back_kernel(
    second_ref,
    share_ref,
    recv_ref,
    unit_ref,
    inverse_ref,
    vec_ref,
    out_weight_ref,
    total_ref,
    low_ref,
    grad_ref,
    sums_ref,
):
    added = share_ref[...].astype(F32) + recv_ref[...].astype(F32)
    upstream = second_ref[...] + added
    unit = unit_ref[...]
    first = norm_back(upstream, unit, inverse_ref[...], vec_ref[0, 1:2, :])
    sums_ref[...] = jnp.zeros_like(sums_ref)
    sums_ref[0:1, :] = jnp.sum(upstream * unit, 0, keepdims=True)
    sums_ref[1:2, :] = jnp.sum(upstream, 0, keepdims=True)
    sums_ref[2:3, :] = jnp.sum(first, 0, keepdims=True)
    total_ref[...] = first
    low = first.astype(BF16)
    low_ref[...] = low
    grad_ref[...] = dot(low, out_weight_ref[0], 1, 1).astype(BF16)


def joint_back_kernel(
    q_grad_ref, own_ref, recv_ref, q_weight_ref, kv_weight_ref, joint_ref, bias_ref, part_ref
):
    width = q_grad_ref.shape[1]
    q_grad = q_grad_ref[...]
    kv_grad = (own_ref[0] + recv_ref[0].astype(F32)).astype(BF16)
    joint_ref[:, :width] = q_grad
    joint_ref[:, width:] = kv_grad
    bias_ref[...] = jnp.zeros_like(bias_ref)
    bias_ref[0:1, :] = jnp.sum(q_grad.astype(F32), 0, keepdims=True)
    bias_ref[1:2, :] = jnp.sum(kv_grad[:, width:].astype(F32), 0, keepdims=True)
    part_ref[...] = (dot(q_grad, q_weight_ref[0], 1, 1) + dot(kv_grad, kv_weight_ref[0], 1, 1)).astype(
        BF16
    )


def wide_pairs(wide):
    steps = []
    reach = 1
    while reach < wide:
        steps.append([(index, index ^ reach) for index in range(wide)])
        reach *= 2
    return steps


def on_device(wide, *arguments):
    (
        tokens,
        buckets,
        lengths,
        type_table,
        query_weight,
        query_bias,
        key_weight,
        value_weight,
        value_bias,
        output_weight,
        output_bias,
        attention_gain,
        attention_shift,
        up_weight,
        up_bias,
        down_weight,
        down_bias,
        feed_gain,
        feed_shift,
        cotangent,
    ) = arguments
    share, model = tokens.shape
    lane = 2 * share
    chunks = lane // CHUNK
    local = query_weight.shape[2]
    width = 2 * local
    head_count = width // HEAD_DIM
    units = up_weight.shape[2]
    place = lax.axis_index("narrow")
    chip, core = place // 2, place % 2
    first_chip, first_core = chip == 0, core == 0

    def by_core(own, other, axis):
        return jnp.where(
            first_core,
            jnp.concatenate([own, other], axis),
            jnp.concatenate([other, own], axis),
        )

    def by_chip(own, other):
        return jnp.where(
            first_chip, jnp.concatenate([own, other], 0), jnp.concatenate([other, own], 0)
        )

    def own_rows(rows):
        return jnp.where(first_chip, rows[:share], rows[share:])

    def other_rows(rows):
        return jnp.where(first_chip, rows[share:], rows[:share])

    lane_tokens = by_chip(tokens, over_chip(tokens))
    lane_buckets = by_chip(buckets, over_chip(buckets))
    lane_cotangent = by_chip(cotangent, over_chip(cotangent))

    qw = by_core(query_weight, over_core(query_weight), 2)
    kw = by_core(key_weight, over_core(key_weight), 2)
    vw = by_core(value_weight, over_core(value_weight), 2)
    ow = by_core(output_weight, over_core(output_weight), 1)
    kvw = jnp.concatenate([kw, vw], 2)
    up_other = over_core(up_weight)
    down_other = over_core(down_weight)
    small = jnp.concatenate([query_bias, value_bias, up_bias], 1)
    small_other = over_core(small)
    q_bias = by_core(query_bias, small_other[:, :local], 1).astype(F32)[:, None, :]
    v_bias = by_core(value_bias, small_other[:, local:width], 1).astype(F32)
    kv_bias = jnp.concatenate([jnp.zeros_like(v_bias), v_bias], 1)[:, None, :]
    unit_bias = jnp.concatenate([up_bias, small_other[:, width:]], 1).astype(F32)[:, None, :]
    ones = jnp.ones((1, model), F32)
    rows = [
        value.astype(F32)
        for value in (
            output_bias,
            attention_gain,
            attention_shift,
            down_bias,
            feed_gain,
            feed_shift,
        )
    ]
    rows.append(jnp.concatenate([ones, rows[4][: LAYERS - 1]], 0))
    rows.append(jnp.concatenate([0.0 * ones, rows[5][: LAYERS - 1]], 0))
    vec = jnp.stack(rows, 1)

    ends = jnp.cumsum(lengths[0], dtype=jnp.int32)
    offsets = lax.iota(jnp.int32, share)
    spots = jnp.concatenate(
        [
            offsets + (block * 2 + which) * share
            for which in (core, 1 - core)
            for block in range(2)
        ]
    )
    labels = jnp.sum((spots[:, None] >= ends[None, :]).astype(jnp.int32), 1, dtype=jnp.int32)
    tiles = 2 * chunks
    tile_labels = labels.reshape(tiles, CHUNK)
    present = jnp.any(
        tile_labels[:, :, None] == lax.iota(jnp.int32, lengths.shape[1])[None, None, :], axis=1
    )
    bits = jnp.sum(
        jnp.where(present, jnp.left_shift(1, lax.iota(jnp.int32, lengths.shape[1]))[None, :], 0),
        axis=1,
        dtype=jnp.int32,
    )
    bits = jnp.concatenate([bits, bits[:chunks]])
    k_labels = tile_labels[:, :, None]
    q_labels = tile_labels[:chunks, None, :]

    block = (CHUNK, model)
    smem = pl.BlockSpec(memory_space=pltpu.SMEM)

    def layer_spec(layer, shape):
        return pl.BlockSpec((1,) + shape, lambda *ids: (layer,) + (0,) * len(shape))

    def rows_at(index, columns):
        return pl.BlockSpec((CHUNK, columns), lambda *ids: (index, 0))

    steps = 2 * units // CHUNK
    half_steps = steps // 2

    def unit_specs(layer):
        def early(step):
            return jnp.minimum(step, half_steps - 1)

        def late(step):
            return jnp.maximum(step - half_steps, 0)

        up_specs = [
            pl.BlockSpec((1, model, CHUNK), lambda step: (layer, 0, early(step))),
            pl.BlockSpec((1, model, CHUNK), lambda step: (layer, 0, late(step))),
        ]
        down_specs = [
            pl.BlockSpec((1, CHUNK, model), lambda step: (layer, early(step), 0)),
            pl.BlockSpec((1, CHUNK, model), lambda step: (layer, late(step), 0)),
        ]
        return up_specs, down_specs

    selector = (lane_buckets[:, None] == lax.iota(jnp.int32, type_table.shape[0])[None, :]).astype(
        BF16
    )
    stream = lane_tokens.astype(F32) + dot(selector, type_table)
    low_first = stream.astype(BF16)
    state = [stream[CHUNK * i : CHUNK * (i + 1)] for i in range(chunks)]
    kept = []
    matmul = 2 * CHUNK * model
    for layer in range(LAYERS):
        keep = {}
        if layer == 0:
            low_in = low_first
            kv = (dot(low_first, kvw[0]) + kv_bias[0]).astype(BF16).reshape(chunks, CHUNK, 2 * width)
            queries = ((dot(low_first, qw[0]) + q_bias[0]) * HEAD_DIM**-0.5).astype(BF16)
        else:
            low_in = queries = kv = None
            units_now = []
            inverses = []
            for i in range(chunks):
                outs = call(
                    project_kernel,
                    (1,),
                    [
                        (state[i], whole(block)),
                        (feed_share[i], whole(block)),
                        (feed_recv[i], whole(block)),
                        (vec, layer_spec(layer - 1, (8, model))),
                        (qw, layer_spec(layer, (model, width))),
                        (kvw, layer_spec(layer, (model, 2 * width))),
                        (q_bias, layer_spec(layer, (1, width))),
                        (kv_bias, layer_spec(layer, (1, 2 * width))),
                    ],
                    [
                        (block, F32, whole(block), None),
                        ((CHUNK, 1), F32, whole((CHUNK, 1)), None),
                        ((lane, model), BF16, rows_at(i, model), low_in),
                        ((lane, width), BF16, rows_at(i, width), queries),
                        (
                            (chunks, CHUNK, 2 * width),
                            BF16,
                            pl.BlockSpec((1, CHUNK, 2 * width), lambda *ids, i=i: (i, 0, 0)),
                            kv,
                        ),
                    ],
                    flops=matmul * 3 * width,
                    moved=6 * MIB,
                )
                units_now.append(outs[0])
                inverses.append(outs[1])
                low_in, queries, kv = outs[2:]
            state = units_now
            kept[layer - 1]["second_unit"] = units_now
            kept[layer - 1]["second_inverse"] = inverses
        kv_other = over_core(kv)
        tile_shape = (1, CHUNK, 2 * width)
        kv_all, turned = call(
            gather_kernel,
            (tiles,),
            [
                (kv, pl.BlockSpec(tile_shape, lambda t: (jnp.minimum(t, chunks - 1), 0, 0))),
                (kv_other, pl.BlockSpec(tile_shape, lambda t: (jnp.maximum(t - chunks, 0), 0, 0))),
            ],
            [
                ((tiles, CHUNK, 2 * width), BF16, pl.BlockSpec(tile_shape, lambda t: (t, 0, 0)), None),
                (
                    (tiles, 2 * width, CHUNK),
                    BF16,
                    pl.BlockSpec((1, 2 * width, CHUNK), lambda t: (t, 0, 0)),
                    None,
                ),
            ],
            moved=7 * MIB,
        )
        context = exact = logsum = None
        shares = []
        for i in range(chunks):
            context, exact, logsum, part = call(
                functools.partial(attend_kernel, head_count, i),
                (1,),
                [
                    (bits, smem),
                    (queries, rows_at(i, width)),
                    (kv_all, whole(kv_all.shape)),
                    (turned, whole(turned.shape)),
                    (q_labels[i], whole((1, CHUNK))),
                    (k_labels, whole(k_labels.shape)),
                    (ow, layer_spec(layer, (width, model))),
                ],
                [
                    ((lane, width), BF16, rows_at(i, width), context),
                    ((lane, width), F32, rows_at(i, width), exact),
                    (
                        (chunks, 8, CHUNK),
                        F32,
                        pl.BlockSpec((1, 8, CHUNK), lambda *ids, i=i: (i, 0, 0)),
                        logsum,
                    ),
                    (block, BF16, whole(block), None),
                ],
                scratch=[
                    pltpu.VMEM((head_count, CHUNK, 128), BF16),
                    pltpu.VMEM((width, CHUNK), F32),
                    pltpu.VMEM((8, CHUNK), F32),
                    pltpu.VMEM((8, CHUNK), F32),
                ],
                flops=4 * CHUNK * tiles * CHUNK * width * 4,
                moved=5 * MIB,
            )
            shares.append(part)
        received = [over_chip(part) for part in shares]
        up_specs, down_specs = unit_specs(layer)
        low_middle = act = slope = None
        first_unit, first_inverse, feed_share = [], [], []
        for i in range(chunks):
            outs = call(
                functools.partial(feed_kernel, steps),
                (steps,),
                [
                    (state[i], whole(block)),
                    (shares[i], whole(block)),
                    (received[i], whole(block)),
                    (vec, layer_spec(layer, (8, model))),
                    (up_weight, up_specs[0]),
                    (up_other, up_specs[1]),
                    (
                        unit_bias,
                        pl.BlockSpec((1, 1, CHUNK), lambda step, layer=layer: (layer, 0, step)),
                    ),
                    (down_weight, down_specs[0]),
                    (down_other, down_specs[1]),
                ],
                [
                    (block, F32, whole(block), None),
                    ((CHUNK, 1), F32, whole((CHUNK, 1)), None),
                    ((lane, model), BF16, rows_at(i, model), low_middle),
                    (
                        (lane, 2 * units),
                        BF16,
                        pl.BlockSpec((CHUNK, CHUNK), lambda step, i=i: (i, step)),
                        act,
                    ),
                    (
                        (lane, 2 * units),
                        BF16,
                        pl.BlockSpec((CHUNK, CHUNK), lambda step, i=i: (i, step)),
                        slope,
                    ),
                    (block, BF16, whole(block), None),
                ],
                scratch=[pltpu.VMEM(block, BF16), pltpu.VMEM(block, F32)],
                flops=matmul * 4 * units,
                moved=8 * MIB,
            )
            first_unit.append(outs[0])
            first_inverse.append(outs[1])
            low_middle, act, slope = outs[2:5]
            feed_share.append(outs[5])
        feed_recv = [over_chip(part) for part in feed_share]
        state = first_unit
        keep.update(
            low_in=low_in,
            queries=queries,
            kv_all=kv_all,
            turned=turned,
            context=context,
            exact=exact,
            logsum=logsum,
            first_unit=first_unit,
            first_inverse=first_inverse,
            low_middle=low_middle,
            act=act,
            slope=slope,
        )
        kept.append(keep)

    def over_wide(value):
        return lax.psum(value, "wide")

    def pair_total(own, other):
        return over_wide((own + over_core(other.astype(BF16)).astype(F32)).astype(BF16))

    def halves(full, axis):
        left, right = jnp.split(full, 2, axis)
        return jnp.where(first_core, left, right), jnp.where(first_core, right, left)

    weight_grads = [None] * LAYERS
    shared = [None] * LAYERS
    split_vectors = [None] * LAYERS
    encoded = None
    for layer in reversed(range(LAYERS)):
        keep = kept[layer]
        top_layer = layer == LAYERS - 1
        up_specs, down_specs = unit_specs(layer)
        low_second = up_grad = None
        second, unit_sums, second_sums, parts = [], [], [], []
        for i in range(chunks):
            if top_layer:
                upstream = (lane_cotangent, rows_at(i, model))
                unit = keep["first_unit"][i]
                inverse = keep["first_inverse"][i]
                added = (feed_share[i], feed_recv[i])
            else:
                upstream = (first_total[i], whole(block))
                unit = keep["second_unit"][i]
                inverse = keep["second_inverse"][i]
                added = (joint_share[i], joint_recv[i])
            outs = call(
                functools.partial(feed_back_kernel, steps, top_layer),
                (steps,),
                [
                    upstream,
                    (unit, whole(block)),
                    (inverse, whole((CHUNK, 1))),
                    (added[0], whole(block)),
                    (added[1], whole(block)),
                    (vec, layer_spec(layer, (8, model))),
                    (
                        keep["slope"],
                        pl.BlockSpec((CHUNK, CHUNK), lambda step, i=i: (i, step)),
                    ),
                    (up_weight, up_specs[0]),
                    (up_other, up_specs[1]),
                    (down_weight, down_specs[0]),
                    (down_other, down_specs[1]),
                ],
                [
                    ((lane, model), BF16, rows_at(i, model), encoded)
                    if top_layer
                    else ((8, 128), BF16, whole((8, 128)), None),
                    (block, F32, whole(block), None),
                    ((lane, model), BF16, rows_at(i, model), low_second),
                    (
                        (lane, 2 * units),
                        BF16,
                        pl.BlockSpec((CHUNK, CHUNK), lambda step, i=i: (i, step)),
                        up_grad,
                    ),
                    ((1, 2 * units), F32, pl.BlockSpec((1, CHUNK), lambda step: (0, step)), None),
                    ((8, model), F32, whole((8, model)), None),
                    (block, BF16, whole(block), None),
                ],
                scratch=[pltpu.VMEM(block, BF16), pltpu.VMEM(block, F32)],
                flops=matmul * 4 * units,
                moved=8 * MIB,
            )
            if top_layer:
                encoded = outs[0]
            second.append(outs[1])
            low_second, up_grad = outs[2:4]
            unit_sums.append(outs[4])
            second_sums.append(outs[5])
            parts.append(outs[6])
        received = [over_chip(part) for part in parts]
        down_grad = pair_total(
            dot(keep["act"][:, :units], low_second, 0, 0),
            dot(keep["act"][:, units:], low_second, 0, 0),
        )
        up_weight_grad = pair_total(
            dot(keep["low_middle"], up_grad[:, :units], 0, 0),
            dot(keep["low_middle"], up_grad[:, units:], 0, 0),
        )
        low_total = context_grad = None
        first_total, first_sums = [], []
        for i in range(chunks):
            outs = call(
                context_back_kernel,
                (1,),
                [
                    (second[i], whole(block)),
                    (parts[i], whole(block)),
                    (received[i], whole(block)),
                    (keep["first_unit"][i], whole(block)),
                    (keep["first_inverse"][i], whole((CHUNK, 1))),
                    (vec, layer_spec(layer, (8, model))),
                    (ow, layer_spec(layer, (width, model))),
                ],
                [
                    (block, F32, whole(block), None),
                    ((lane, model), BF16, rows_at(i, model), low_total),
                    ((lane, width), BF16, rows_at(i, width), context_grad),
                    ((8, model), F32, whole((8, model)), None),
                ],
                flops=matmul * width,
                moved=5 * MIB,
            )
            first_total.append(outs[0])
            low_total, context_grad = outs[1:3]
            first_sums.append(outs[3])
        own, other = halves(dot(keep["context"], low_total, 0, 0), 0)
        out_grad = pair_total(own, other)
        tile_rows = pl.BlockSpec((CHUNK, width), lambda t: (t, 0))
        turned_keys = (tiles, width, CHUNK)
        half_shape = (chunks, CHUNK, 2 * width)
        q_grad, kv_grad, kv_grad_other = call(
            functools.partial(attend_back_kernel, head_count),
            (chunks,),
            [
                (bits, smem),
                (keep["queries"], tile_rows),
                (keep["kv_all"], whole(keep["kv_all"].shape)),
                (keep["turned"], whole(turned_keys)),
                (q_labels, pl.BlockSpec((1, 1, CHUNK), lambda t: (t, 0, 0))),
                (k_labels, whole(k_labels.shape)),
                (context_grad, tile_rows),
                (keep["exact"], tile_rows),
                (keep["logsum"], pl.BlockSpec((1, 8, CHUNK), lambda t: (t, 0, 0))),
            ],
            [
                ((lane, width), BF16, tile_rows, None),
                (half_shape, F32, whole(half_shape), None),
                (half_shape, BF16, whole(half_shape), None),
            ],
            scratch=[
                pltpu.VMEM((head_count, CHUNK, 128), BF16),
                pltpu.VMEM((head_count, CHUNK, 128), BF16),
                pltpu.VMEM((8, CHUNK), F32),
                pltpu.VMEM((width, CHUNK), F32),
                pltpu.VMEM((tiles, CHUNK, 2 * width), F32),
            ],
            flops=10 * lane * tiles * CHUNK * width * 4,
            moved=12 * MIB,
        )
        kv_recv = over_core(kv_grad_other)
        joint_grad = None
        joint_share, bias_sums = [], []
        for i in range(chunks):
            tile_spec = pl.BlockSpec((1, CHUNK, 2 * width), lambda *ids, i=i: (i, 0, 0))
            joint_grad, sums, part = call(
                joint_back_kernel,
                (1,),
                [
                    (q_grad, rows_at(i, width)),
                    (kv_grad, tile_spec),
                    (kv_recv, tile_spec),
                    (qw, layer_spec(layer, (model, width))),
                    (kvw, layer_spec(layer, (model, 2 * width))),
                ],
                [
                    ((lane, 3 * width), BF16, rows_at(i, 3 * width), joint_grad),
                    ((8, width), F32, whole((8, width)), None),
                    (block, BF16, whole(block), None),
                ],
                flops=matmul * 3 * width,
                moved=5 * MIB,
            )
            joint_share.append(part)
            bias_sums.append(sums)
        if layer > 0:
            joint_recv = [over_chip(part) for part in joint_share]
        joint_weight_grad = dot(keep["low_in"], joint_grad, 0, 0)
        pieces = [
            halves(joint_weight_grad[:, width * k : width * (k + 1)], 1) for k in range(3)
        ]
        own = jnp.concatenate([piece[0] for piece in pieces], 1)
        other = jnp.concatenate([piece[1] for piece in pieces], 1)
        joint = pair_total(own, other)
        weight_grads[layer] = (
            joint[:, :local],
            joint[:, local : 2 * local],
            joint[:, 2 * local :],
            out_grad,
            up_weight_grad,
            down_grad,
        )
        second_sum, first_sum = sum(second_sums), sum(first_sums)
        shared[layer] = jnp.concatenate([second_sum[:3], first_sum[:3]], 0)
        unit_sum, bias_sum = sum(unit_sums), sum(bias_sums)
        q_own, q_other = halves(bias_sum[0], 0)
        v_own, v_other = halves(bias_sum[1], 0)
        split_vectors[layer] = (
            jnp.concatenate([q_own, v_own, unit_sum[0, :units]]),
            jnp.concatenate([q_other, v_other, unit_sum[0, units:]]),
        )

    joint_rows = jnp.concatenate(joint_share, 0)
    joint_mine = own_rows(joint_rows).astype(F32)
    joint_theirs = over_chip(other_rows(joint_rows)).astype(F32)
    tokens_grad = own_rows(jnp.concatenate(first_total, 0)) + (joint_mine + joint_theirs)
    own_selector = (buckets[:, None] == lax.iota(jnp.int32, type_table.shape[0])[None, :]).astype(
        BF16
    )
    high = tokens_grad.astype(BF16)
    rest = (tokens_grad - high.astype(F32)).astype(BF16)
    table = dot(own_selector, high, 0, 0) + dot(own_selector, rest, 0, 0)

    def wide_sum(value):
        if wide != 8:
            return lax.psum(value, "wide")
        for pairs in wide_pairs(wide):
            value = value + lax.ppermute(value, "wide", pairs)
        return value

    def summed_in_bf16(value, pairs, axis):
        low = value.astype(BF16)
        return low.astype(F32) + lax.ppermute(low, axis, pairs).astype(F32)

    table_own, table_other = halves(table, 0)
    table_half = table_own + over_core(table_other)
    table_half = summed_in_bf16(table_half, CHIP_SWAP, "narrow")
    if wide == 8:
        for pairs in wide_pairs(wide):
            table_half = summed_in_bf16(table_half, pairs, "wide")
    else:
        table_half = lax.psum(table_half, "wide")
    table_grad = by_core(table_half, over_core(table_half), 0)

    common = jnp.concatenate(shared, 0)
    mine = jnp.stack([value[0] for value in split_vectors])
    theirs = jnp.stack([value[1] for value in split_vectors])
    vectors = jnp.concatenate([common.reshape(-1), mine.reshape(-1)])
    sent = jnp.concatenate([common.reshape(-1), theirs.reshape(-1)])
    vectors = wide_sum((vectors + over_core(sent)).reshape(-1, 128)).reshape(-1)
    common = vectors[: common.size].reshape(LAYERS, 6, model)
    mine = vectors[common.size :].reshape(LAYERS, -1)

    def stacked(member):
        return jnp.stack([weight_grads[layer][member] for layer in range(LAYERS)]).astype(F32)

    return (
        own_rows(encoded),
        tokens_grad,
        table_grad,
        stacked(0),
        mine[:, :local],
        stacked(1),
        stacked(2),
        mine[:, local : 2 * local],
        stacked(3),
        common[:, 5],
        common[:, 3],
        common[:, 4],
        stacked(4),
        mine[:, 2 * local :],
        stacked(5),
        common[:, 2],
        common[:, 0],
        common[:, 1],
    )


def solution(mesh):
    rows = P(("wide", "narrow"), None)
    third = P(None, None, "narrow")
    second = P(None, "narrow")
    middle = P(None, "narrow", None)
    in_specs = (
        rows,
        P(("wide", "narrow")),
        P("wide", None),
        P(),
        third,
        second,
        third,
        third,
        second,
        middle,
        P(),
        P(),
        P(),
        third,
        second,
        middle,
        P(),
        P(),
        P(),
        rows,
    )
    out_specs = (
        rows,
        rows,
        P(),
        third,
        second,
        third,
        third,
        second,
        middle,
        P(),
        P(),
        P(),
        third,
        second,
        middle,
        P(),
        P(),
        P(),
    )
    return jax.shard_map(
        functools.partial(on_device, mesh.shape["wide"]),
        mesh=mesh,
        in_specs=in_specs,
        out_specs=out_specs,
        check_vma=False,
    )
```

time: 1570 us -> 700 us (0.45)
  waiting for transfers between devices: 1020 us -> 219 us
  matrix products: 282 us -> 34.7 us
  Pallas kernels: 0 us -> 228 us
  blocking collectives: 69.6 us -> 0 us
  starting transfers between devices: 2.96 us -> 61.7 us
  other arithmetic: 94.6 us -> 53.7 us
    psum x2 -> x1, waiting for transfers between devices: 496 us -> 155 us  [over_wide(): return lax.psum(value, 'wide')]
    reduce_scatter x12 -> x0, waiting for transfers between devices: 292 us -> none  [the longest x4 117 us: layer_parts(): lax.psum_scatter(jnp.dot(low_activation, down_weight, preferred_element_t...]
    all_gather x10 -> x0, waiting for transfers between devices: 231 us -> none  [the longest x4 84.2 us: layer_parts(): lax.all_gather(middle.astype(jnp.bfloat16), 'narrow', axis=0, tiled=True)]
    pallas_call x0 -> x37, Pallas kernels: none -> 228 us  [call(): pl.pallas_call(body, grid=grid, in_specs=specs, out_specs=[spec for shape...]
    dot_general x78 -> x17, matrix products: 242 us -> 34.7 us  [dot(): lax.dot_general(left, right, (((left_axis,), (right_axis,)), ((), ())), p...]
    psum x2 -> x0, blocking collectives: 69.6 us -> none  [the longest x1 40 us: on_device(): lax.psum((table_grad, common[0], common[1], common[2], common[3], common[...]
    ppermute x0 -> x54, waiting for transfers between devices: none -> 63.6 us  [the longest x4 47.9 us: summed_in_bf16(): return low.astype(F32) + lax.ppermute(low, axis, pairs).astype(F32)]
    ppermute x0 -> x54, starting transfers between devices: none -> 61.7 us  [the longest x22 32.7 us: over_core(): return lax.ppermute(value, 'narrow', CORE_SWAP)]
  transfers between devices with their start and end apart: 24 -> 55, of which waited for: 24 -> 11; matrix products, arithmetic and copies ran while one was open for 9% -> 17% of each run, Pallas kernels for 0% -> 33%
where the time goes in v1:
time: 700 us; the launch traced here: 690 us
  Pallas kernels  228 us (33%)
  waiting for transfers between devices  219 us (31%)
  local copies, waits for them, and re-layouts  76.3 us (11%)
  starting transfers between devices  61.7 us (9%)
  other arithmetic  53.7 us (8%)
  matrix products  34.7 us (5%)
  between operations  16.6 us (2%)
    pallas_call x37, Pallas kernels, call(): pl.pallas_call(body, grid=grid, in_specs=specs, out_specs=[spec for shape...  228 us
    psum x1, waiting for transfers between devices, over_wide(): return lax.psum(value, 'wide')  155 us
    ppermute x4, waiting for transfers between devices, summed_in_bf16(): return low.astype(F32) + lax.ppermute(low, axis, pairs).astype(F32)  47.9 us
    unnamed x406, local copies, waits for them, and re-layouts  45.8 us
    dot_general x17, matrix products, dot(): lax.dot_general(left, right, (((left_axis,), (right_axis,)), ((), ())), p...  34.7 us
    ppermute x22, starting transfers between devices, over_core(): return lax.ppermute(value, 'narrow', CORE_SWAP)  32.7 us
    ppermute x25, starting transfers between devices, over_chip(): return lax.ppermute(value, 'narrow', CHIP_SWAP)  21 us
  transfers between devices with their start and end apart: 55, of which 11 were waited for; matrix products, arithmetic and copies ran while one was open for 17% of the time, Pallas kernels for 33%

profile of v1, /device:TPU:1, one launch (start us, length us, event | category | flops | bytes accessed | tf_op | source)
XLA Modules:
  0.0 690.3 jit_solution(15256832570539037885)
XLA Ops:
  55.9 10.2 %shard_map.332 = (bf16[768,384]{1,0:T(8,128)(2,1)S(1)}, f32[768,384]{1,0:T(8,128)S(1)}, f32[3,8,256]{2,1,0:T(8,128)S(1)}, bf16[256,768]{1,0:T(8,128)(2,1)S(1)}) custom-call(s32[9]{0:T(128)S(1)} %pad_add_fusion.1.refs_0_, bf16[768,384]{1,0:T(8,128)(2,1)S(1)} %fusion.7.refs_1_, bf16[6,256,768]{2,1,0:T(8,128)(2,1)S(1)} %get-tuple-element.184.refs_2_, ...), custom_call_target="tpu_custom_call" | custom-call | flops 2415919104 | bytes 5242880 | tf_op jit(solution)/shard_map/pallas_call | solution.py:87
  67.9 12.0 %shard_map.333 = (bf16[768,384]{1,0:T(8,128)(2,1)S(1)}, f32[768,384]{1,0:T(8,128)S(1)}, f32[3,8,256]{2,1,0:T(8,128)S(1)}, bf16[256,768]{1,0:T(8,128)(2,1)S(1)}) custom-call(s32[9]{0:T(128)S(1)} %pad_add_fusion.1.refs_0_, bf16[768,384]{1,0:T(8,128)(2,1)S(1)} %fusion.7.refs_1_, ...), custom_call_target="tpu_custom_call", output_to_operand_aliasing={{0}: (7, {}), {1}: (8, {}), {2}: (9, {})} | custom-call | flops 2415919104 | bytes 5242880 | tf_op jit(solution)/shard_map/pallas_call | solution.py:87
  88.3 7.5 %shard_map.335 = (f32[256,768]{1,0:T(8,128)S(1)}, f32[256,1]{1,0:T(8,128)S(1)}, bf16[768,768]{1,0:T(8,128)(2,1)S(1)}, bf16[768,1536]{1,0:T(8,128)(2,1)S(1)}, bf1...) custom-call(f32[256,768]{1,0:T(8,128)S(1)} %get-tuple-element.446.refs_0_, ...), custom_call_target="tpu_custom_call" | custom-call | flops 1207959552 | bytes 8388608 | tf_op jit(solution)/shard_map/pallas_call | solution.py:87
  96.9 7.5 %shard_map.336 = (f32[256,768]{1,0:T(8,128)S(1)}, f32[256,1]{1,0:T(8,128)S(1)}, bf16[768,768]{1,0:T(8,128)(2,1)S(1)}, bf16[768,1536]{1,0:T(8,128)(2,1)S(1)}, bf1...) custom-call(f32[256,768]{1,0:T(8,128)S(1)} %get-tuple-element.447.re, ...), custom_call_target="tpu_custom_call", output_to_operand_aliasing={{2}: (9, {}), {3}: (10, {}), {4}: (11, {})} | custom-call | flops 1207959552 | bytes 8388608 | tf_op jit(solution)/shard_map/pallas_call | solution.py:87
  105.0 7.8 %shard_map.337 = (f32[256,768]{1,0:T(8,128)S(1)}, f32[256,1]{1,0:T(8,128)S(1)}, bf16[768,768]{1,0:T(8,128)(2,1)S(1)}, bf16[768,1536]{1,0:T(8,128)(2,1)S(1)}, bf1...) custom-call(f32[256,768]{1,0:T(8,128)S(1)} %get-tuple-element.448.re, ...), custom_call_target="tpu_custom_call", output_to_operand_aliasing={{2}: (9, {}), {3}: (10, {}), {4}: (11, {})} | custom-call | flops 1207959552 | bytes 8388608 | tf_op jit(solution)/shard_map/pallas_call | solution.py:87
  131.5 10.2 %shard_map.342 = (bf16[768,384]{1,0:T(8,128)(2,1)S(1)}, f32[768,384]{1,0:T(8,128)S(1)}, f32[3,8,256]{2,1,0:T(8,128)S(1)}, bf16[256,768]{1,0:T(8,128)(2,1)S(1)}) custom-call(s32[9]{0:T(128)S(1)} %pad_add_fusion.1.refs_0_, bf16[768,384]{1,0:T(8,128)(2,1)S(1)} %get-tuple-element.214.refs_1_, bf16[6,256,768]{2,1,0:T(8,128)(2,1)S(1)} %get-tuple-element.216.refs_2_, ...), custom_call_target="tpu_custom_call" | custom-call | flops 2415919104 | bytes 5242880 | tf_op jit(solution)/shard_map/pallas_call | solution.py:87
  142.5 12.0 %shard_map.343 = (bf16[768,384]{1,0:T(8,128)(2,1)S(1)}, f32[768,384]{1,0:T(8,128)S(1)}, f32[3,8,256]{2,1,0:T(8,128)S(1)}, bf16[256,768]{1,0:T(8,128)(2,1)S(1)}) custom-call(s32[9]{0:T(128)S(1)} %pad_add_fusion.1.refs_0_, bf16[768,384]{1,0:T(8,128)(2,1)S(1)} %get-tuple-element.214.refs_1_, ...), custom_call_target="tpu_custom_call", output_to_operand_aliasing={{0}: (7, {}), {1}: (8, {}), {2}: (9, {})} | custom-call | flops 2415919104 | bytes 5242880 | tf_op jit(solution)/shard_map/pallas_call | solution.py:87
  155.4 6.6 shard_map.344
  164.6 8.2 %shard_map.345 = (f32[256,768]{1,0:T(8,128)S(1)}, f32[256,1]{1,0:T(8,128)S(1)}, bf16[768,768]{1,0:T(8,128)(2,1)S(1)}, bf16[768,1536]{1,0:T(8,128)(2,1)S(1)}, bf1...) custom-call(f32[256,768]{1,0:T(8,128)S(1)} %get-tuple-element.227.refs_0_.refs_1_, ...), custom_call_target="tpu_custom_call" | custom-call | flops 1207959552 | bytes 8388608 | tf_op jit(solution)/shard_map/pallas_call | solution.py:87
  173.5 8.4 %shard_map.346 = (f32[256,768]{1,0:T(8,128)S(1)}, f32[256,1]{1,0:T(8,128)S(1)}, bf16[768,768]{1,0:T(8,128)(2,1)S(1)}, bf16[768,1536]{1,0:T(8,128)(2,1)S(1)}, bf1...) custom-call(f32[256,768]{1,0:T(8,128)S(1)} %get-tuple-element.225.re, ...), custom_call_target="tpu_custom_call", output_to_operand_aliasing={{2}: (9, {}), {3}: (10, {}), {4}: (11, {})} | custom-call | flops 1207959552 | bytes 8388608 | tf_op jit(solution)/shard_map/pallas_call | solution.py:87
  182.7 8.2 %shard_map.347 = (f32[256,768]{1,0:T(8,128)S(1)}, f32[256,1]{1,0:T(8,128)S(1)}, bf16[768,768]{1,0:T(8,128)(2,1)S(1)}, bf16[768,1536]{1,0:T(8,128)(2,1)S(1)}, bf1...) custom-call(f32[256,768]{1,0:T(8,128)S(1)} %get-tuple-element.213.re, ...), custom_call_target="tpu_custom_call", output_to_operand_aliasing={{2}: (9, {}), {3}: (10, {}), {4}: (11, {})} | custom-call | flops 1207959552 | bytes 8388608 | tf_op jit(solution)/shard_map/pallas_call | solution.py:87
  200.6 7.5 %shard_map.348 = (bf16[768,768]{1,0:T(8,128)(2,1)S(1)}, f32[256,768]{1,0:T(8,128)S(1)}, bf16[768,768]{1,0:T(8,128)(2,1)S(1)}, bf16[768,1536]{1,0:T(8,128)(2,1)S(...) custom-call(bf16[768,768]{1,0:T(8,128)(2,1)S(1)} %maximum_select_fusion.refs_0_, ...), custom_call_target="tpu_custom_call" | custom-call | flops 1207959552 | bytes 8388608 | tf_op jit(solution)/shard_map/pallas_call | solution.py:87
  208.9 7.6 %shard_map.349 = (bf16[768,768]{1,0:T(8,128)(2,1)S(1)}, f32[256,768]{1,0:T(8,128)S(1)}, bf16[768,768]{1,0:T(8,128)(2,1)S(1)}, bf16[768,1536]{1,0:T(8,128)(2,1)S(...) custom-call(bf16[768,768]{1,0:T(8,128)(2,1)S(1)} %maximum_select_fus, ...), custom_call_target="tpu_custom_call", output_to_operand_aliasing={{0}: (11, {}), {2}: (12, {}), {3}: (13, {})} | custom-call | flops 1207959552 | bytes 8388608 | tf_op jit(solution)/shard_map/pallas_call | solution.py:87
  218.2 8.1 %shard_map.350 = (bf16[768,768]{1,0:T(8,128)(2,1)S(1)}, f32[256,768]{1,0:T(8,128)S(1)}, bf16[768,768]{1,0:T(8,128)(2,1)S(1)}, bf16[768,1536]{1,0:T(8,128)(2,1)S(...) custom-call(bf16[768,768]{1,0:T(8,128)(2,1)S(1)} %maximum_select_fus, ...), custom_call_target="tpu_custom_call", output_to_operand_aliasing={{0}: (11, {}), {2}: (12, {}), {3}: (13, {})} | custom-call | flops 1207959552 | bytes 8388608 | tf_op jit(solution)/shard_map/pallas_call | solution.py:87
  246.0 26.7 %shard_map.354 = (bf16[768,384]{1,0:T(8,128)(2,1)S(1)}, f32[3,256,768]{2,1,0:T(8,128)S(1)}, bf16[3,256,768]{2,1,0:T(8,128)(2,1)S(1)}) custom-call(s32[9]{0:T(128)S(1)} %pad_add_fusion.1.refs_0_, bf16[768,384]{1,0:T(8,128)(2,1)S(1)} %copy-done.26, bf16[6,256,768]{2,1,0:T(8,128)(2,1)S(1)} %copy-done.32, bf16[6,768,256]{2,1,0:T(8,128)(2,1)S(1)} %copy-done.34, ...), custom_call_target="tpu_custom_call" | custom-call | flops 18119393280 | bytes 12582912 | tf_op jit(solution)/shard_map/pallas_call | solution.py:87
  298.7 7.8 %shard_map.356 = (bf16[8,128]{1,0:T(8,128)(2,1)}, f32[256,768]{1,0:T(8,128)S(1)}, bf16[768,768]{1,0:T(8,128)(2,1)S(1)}, bf16[768,1536]{1,0:T(8,128)(2,1)S(1)}, f...) custom-call(f32[256,768]{1,0:T(8,128)S(1)} %copy-done.104, f32[256,768]{1,0:T(8,128)S(1)} %copy-done.78, ...), custom_call_target="tpu_custom_call" | custom-call | flops 1207959552 | bytes 8388608 | tf_op jit(solution)/shard_map/pallas_call | solution.py:87
  308.0 7.9 %shard_map.359 = (bf16[8,128]{1,0:T(8,128)(2,1)}, f32[256,768]{1,0:T(8,128)S(1)}, bf16[768,768]{1,0:T(8,128)(2,1)S(1)}, bf16[768,1536]{1,0:T(8,128)(2,1)S(1)}, f...) custom-call(f32[256,768]{1,0:T(8,128)S(1)} %copy-done.88, ...), custom_call_target="tpu_custom_call", output_to_operand_aliasing={{2}: (11, {}), {3}: (12, {})} | custom-call | flops 1207959552 | bytes 8388608 | tf_op jit(solution)/shard_map/pallas_call | solution.py:87
  317.2 8.0 %shard_map.362 = (bf16[8,128]{1,0:T(8,128)(2,1)}, f32[256,768]{1,0:T(8,128)S(1)}, bf16[768,768]{1,0:T(8,128)(2,1)S(1)}, bf16[768,1536]{1,0:T(8,128)(2,1)S(1)}, f...) custom-call(f32[256,768]{1,0:T(8,128)S(1)} %get-tuple-element.288.re, ...), custom_call_target="tpu_custom_call", output_to_operand_aliasing={{2}: (11, {}), {3}: (12, {})} | custom-call | flops 1207959552 | bytes 8388608 | tf_op jit(solution)/shard_map/pallas_call | solution.py:87
  346.7 27.4 %shard_map.364 = (bf16[768,384]{1,0:T(8,128)(2,1)S(1)}, f32[3,256,768]{2,1,0:T(8,128)S(1)}, bf16[3,256,768]{2,1,0:T(8,128)(2,1)}) custom-call(s32[9]{0:T(128)S(1)} %pad_add_fusion.1.refs_0_, bf16[768,384]{1,0:T(8,128)(2,1)S(1)} %copy-done.38, bf16[6,256,768]{2,1,0:T(8,128)(2,1)S(1)} %copy-done.28, bf16[6,768,256]{2,1,0:T(8,128)(2,1)S(1)} %copy-done.30, ...), custom_call_target="tpu_custom_call" | custom-call | flops 18119393280 | bytes 12582912 | tf_op jit(solution)/shard_map/pallas_call | solution.py:87
  432.0 8.7 %collective-permute-done.35 = bf16[384,768]{1,0:T(8,128)(2,1)} collective-permute-done((bf16[384,768]{1,0:T(8,128)(2,1)}, bf16[384,768]{1,0:T(8,128)(2,1)}, u32[]{:S(2)}, u32[]{:S(2)}) %collective-permute-start.35) | collective-permute-done | bytes 589856 | tf_op jit(solution)/shard_map/ppermute | solution.py:29
  452.4 8.2 %collective-permute-done.38 = bf16[128,768]{1,0:T(8,128)(2,1)S(1)} collective-permute-done((bf16[128,768]{1,0:T(8,128)(2,1)S(1)}, bf16[128,768]{1,0:T(8,128)(2,1)S(1)}, u32[]{:S(2)}, u32[]{:S(2)}) %collective-permute-start.38) | collective-permute-done | bytes 196640 | tf_op jit(solution)/shard_map/ppermute | solution.py:998
  465.3 16.1 %collective-permute-done.39 = bf16[128,768]{1,0:T(8,128)(2,1)S(1)} collective-permute-done((bf16[128,768]{1,0:T(8,128)(2,1)S(1)}, bf16[128,768]{1,0:T(8,128)(2,1)S(1)}, u32[]{:S(2)}, u32[]{:S(2)}) %collective-permute-start.39) | collective-permute-done | bytes 196640 | tf_op jit(solution)/shard_map/ppermute | solution.py:998
  484.2 18.5 %collective-permute-done.40 = bf16[128,768]{1,0:T(8,128)(2,1)S(1)} collective-permute-done((bf16[128,768]{1,0:T(8,128)(2,1)S(1)}, bf16[128,768]{1,0:T(8,128)(2,1)S(1)}, u32[]{:S(2)}, u32[]{:S(2)}) %collective-permute-start.40) | collective-permute-done | bytes 196640 | tf_op jit(solution)/shard_map/ppermute | solution.py:998
  513.5 155.4 %all-reduce.6.cloned.1.call-done = (bf16[768,576]{1,0:T(8,128)(2,1)}, bf16[768,576]{1,0:T(8,128)(2,1)}, bf16[1,192,768]{2,1,0:T(8,128)(2,1)}, bf16[1,192,768]{2,...) async-done(((bf16[768,576]{1,0:T(8,128)(2,1)}, ...) | async-done | bytes 7077904 | tf_op jit(solution)/shard_map/psum | solution.py:780
  (673 shorter events, 267.2 us)
Async XLA Ops:
  7.2 661.7 %all-reduce.6.cloned.1.call-start = ((), (), s32[]{:S(2)}) async-start(), calls=%async_computation | async-start | bytes 14548992 | tf_op jit(solution)/shard_map/psum | solution.py:780
  9.4 24.8 %collective-permute-start.1 = (bf16[384,768]{1,0:T(8,128)(2,1)}, bf16[384,768]{1,0:T(8,128)(2,1)}, u32[]{:S(2)}, u32[]{:S(2)}) collective-permute-start(bf16[384,768]{1,0:T(8,128)(2,1)} %param.20), channel_id=1, source_target_pairs={{0,2},{2,0},{1,3},{3,1},{4,6},{6,4},{5,7},{7,5},{8,10},{10,8},{9,1... | collective-permute-start | bytes 1769480 | tf_op jit(solution)/shard_map/ppermute | solution.py:29
  20.7 22.3 %collective-permute-start.3 = (bf16[2,768,192]{1,2,0:T(8,128)(2,1)}, bf16[2,768,192]{1,2,0:T(8,128)(2,1)}, u32[]{:S(2)}, u32[]{:S(2)}) collective-permute-start(bf16[2,768,192]{1,2,0:T(8,128)(2,1)} %param.24), channel_id=1, source_target_pairs={{0,1},{1,0},{2,3},{3,2},{4,5},{5,4},{6,7},{7,6},{8,9},{9,8},{10,11... | collective-permute-start | bytes 1769480 | tf_op jit(solution)/shard_map/ppermute | solution.py:25
  22.2 26.0 %collective-permute-start.8 = (bf16[2,192,768]{2,1,0:T(8,128)(2,1)}, bf16[2,192,768]{2,1,0:T(8,128)(2,1)}, u32[]{:S(2)}, u32[]{:S(2)}) collective-permute-start(bf16[2,192,768]{2,1,0:T(8,128)(2,1)} %param.29), channel_id=1, source_target_pairs={{0,1},{1,0},{2,3},{3,2},{4,5},{5,4},{6,7},{7,6},{8,9},{9,8},{10,11... | collective-permute-start | bytes 1769480 | tf_op jit(solution)/shard_map/ppermute | solution.py:25
  25.5 62.8 %collective-permute-start.10 = (bf16[2,768,768]{2,1,0:T(8,128)(2,1)S(1)}, bf16[2,768,768]{2,1,0:T(8,128)(2,1)}, u32[]{:S(2)}, u32[]{:S(2)}) collective-permute-start(bf16[2,768,768]{2,1,0:T(8,128)(2,1)S(1)} %copy-done.2), channel_id=1, source_target_pairs={{0,1},{1,0},{2,3},{3,2},{4,5},{5,4},{6,7},{7,6},{8,9},{9,8},{10,11... | collective-permute-start | bytes 7077896 | tf_op jit(solution)/shard_map/ppermute | solution.py:25
  27.7 60.6 %collective-permute-start.11 = (bf16[2,768,768]{2,1,0:T(8,128)(2,1)}, bf16[2,768,768]{2,1,0:T(8,128)(2,1)}, u32[]{:S(2)}, u32[]{:S(2)}) collective-permute-start(bf16[2,768,768]{2,1,0:T(8,128)(2,1)} %refs_9_.11), channel_id=1, source_target_pairs={{0,1},{1,0},{2,3},{3,2},{4,5},{5,4},{6,7},{7,6},{8,9},{9,8},{10,11... | collective-permute-start | bytes 7077896 | tf_op jit(solution)/shard_map/ppermute | solution.py:25
  66.1 22.2 %collective-permute-start.13 = (bf16[256,768]{1,0:T(8,128)(2,1)S(1)}, bf16[256,768]{1,0:T(8,128)(2,1)S(1)}, u32[]{:S(2)}, u32[]{:S(2)}) collective-permute-start(bf16[256,768]{1,0:T(8,128)(2,1)S(1)} %get-tuple-element.194.refs_1_), channel_id=1, source_target_pairs={{0,2},{2,0},{1,3},{3,1},{4,6},{6,4},{5,7},{7,5},{8,10},{10,8},{9,1... | collective-permute-start | bytes 1179656 | tf_op jit(solution)/shard_map/ppermute | solution.py:29
  127.8 69.2 %collective-permute-start = (bf16[384,768]{1,0:T(8,128)(2,1)}, bf16[384,768]{1,0:T(8,128)(2,1)}, u32[]{:S(2)}, u32[]{:S(2)}) collective-permute-start(bf16[384,768]{1,0:T(8,128)(2,1)} %param.39), channel_id=1, source_target_pairs={{0,2},{2,0},{1,3},{3,1},{4,6},{6,4},{5,7},{7,5},{8,10},{10,8},{9,1... | collective-permute-start | bytes 1769480 | tf_op jit(solution)/shard_map/ppermute | solution.py:29
  141.8 22.8 %collective-permute-start.20 = (bf16[256,768]{1,0:T(8,128)(2,1)S(1)}, bf16[256,768]{1,0:T(8,128)(2,1)S(1)}, u32[]{:S(2)}, u32[]{:S(2)}) collective-permute-start(bf16[256,768]{1,0:T(8,128)(2,1)S(1)} %get-tuple-element.228.refs_1_), channel_id=1, source_target_pairs={{0,2},{2,0},{1,3},{3,1},{4,6},{6,4},{5,7},{7,5},{8,10},{10,8},{9,1... | collective-permute-start | bytes 1179656 | tf_op jit(solution)/shard_map/ppermute | solution.py:29
  172.8 26.3 %collective-permute-start.23 = (bf16[256,768]{1,0:T(8,128)(2,1)}, bf16[256,768]{1,0:T(8,128)(2,1)}, u32[]{:S(2)}, u32[]{:S(2)}) collective-permute-start(bf16[256,768]{1,0:T(8,128)(2,1)} %get-tuple-element.244.refs_3_), channel_id=1, source_target_pairs={{0,2},{2,0},{1,3},{3,1},{4,6},{6,4},{5,7},{7,5},{8,10},{10,8},{9,1... | collective-permute-start | bytes 1179656 | tf_op jit(solution)/shard_map/ppermute | solution.py:29
  182.0 26.9 %collective-permute-start.22 = (bf16[256,768]{1,0:T(8,128)(2,1)}, bf16[256,768]{1,0:T(8,128)(2,1)}, u32[]{:S(2)}, u32[]{:S(2)}) collective-permute-start(bf16[256,768]{1,0:T(8,128)(2,1)} %get-tuple-element.241.refs_3_), channel_id=1, source_target_pairs={{0,2},{2,0},{1,3},{3,1},{4,6},{6,4},{5,7},{7,5},{8,10},{10,8},{9,1... | collective-permute-start | bytes 1179656 | tf_op jit(solution)/shard_map/ppermute | solution.py:29
  196.3 21.9 %collective-permute-start.21 = (bf16[256,768]{1,0:T(8,128)(2,1)}, bf16[256,768]{1,0:T(8,128)(2,1)}, u32[]{:S(2)}, u32[]{:S(2)}) collective-permute-start(bf16[256,768]{1,0:T(8,128)(2,1)} %get-tuple-element.237.refs_3_), channel_id=1, source_target_pairs={{0,2},{2,0},{1,3},{3,1},{4,6},{6,4},{5,7},{7,5},{8,10},{10,8},{9,1... | collective-permute-start | bytes 1179656 | tf_op jit(solution)/shard_map/ppermute | solution.py:29
  208.1 29.8 %collective-permute-start.24 = (bf16[256,768]{1,0:T(8,128)(2,1)S(1)}, bf16[256,768]{1,0:T(8,128)(2,1)S(1)}, u32[]{:S(2)}, u32[]{:S(2)}) collective-permute-start(bf16[256,768]{1,0:T(8,128)(2,1)S(1)} %get-tuple-element.253.refs_1_), channel_id=1, source_target_pairs={{0,2},{2,0},{1,3},{3,1},{4,6},{6,4},{5,7},{7,5},{8,10},{10,8},{9,1... | collective-permute-start | bytes 1179656 | tf_op jit(solution)/shard_map/ppermute | solution.py:29
  217.4 21.4 %collective-permute-start.26 = (bf16[256,768]{1,0:T(8,128)(2,1)S(1)}, bf16[256,768]{1,0:T(8,128)(2,1)S(1)}, u32[]{:S(2)}, u32[]{:S(2)}) collective-permute-start(bf16[256,768]{1,0:T(8,128)(2,1)S(1)} %get-tuple-element.259.refs_1_), channel_id=1, source_target_pairs={{0,2},{2,0},{1,3},{3,1},{4,6},{6,4},{5,7},{7,5},{8,10},{10,8},{9,1... | collective-permute-start | bytes 1179656 | tf_op jit(solution)/shard_map/ppermute | solution.py:29
  229.3 51.1 %collective-permute-start.53 = (bf16[768,768]{1,0:T(8,128)(2,1)}, bf16[768,768]{1,0:T(8,128)(2,1)}, u32[]{:S(2)}, u32[]{:S(2)}) collective-permute-start(bf16[768,768]{1,0:T(8,128)(2,1)} %convolution_convert_fusion), channel_id=1, source_target_pairs={{0,1},{1,0},{2,3},{3,2},{4,5},{5,4},{6,7},{7,6},{8,9},{9,8},{10,11... | collective-permute-start | bytes 3538952 | tf_op jit(solution)/shard_map/ppermute | solution.py:25
  237.9 46.0 %collective-permute-start.51 = (bf16[768,768]{1,0:T(8,128)(2,1)}, bf16[768,768]{1,0:T(8,128)(2,1)}, u32[]{:S(2)}, u32[]{:S(2)}) collective-permute-start(bf16[768,768]{1,0:T(8,128)(2,1)} %convolution_convert_fusion.2), channel_id=1, source_target_pairs={{0,1},{1,0},{2,3},{3,2},{4,5},{5,4},{6,7},{7,6},{8,9},{9,8},{10,11... | collective-permute-start | bytes 3538952 | tf_op jit(solution)/shard_map/ppermute | solution.py:25
  291.4 25.8 %collective-permute-start.32 = (bf16[256,768]{1,0:T(8,128)(2,1)S(1)}, bf16[256,768]{1,0:T(8,128)(2,1)S(1)}, u32[]{:S(2)}, u32[]{:S(2)}) collective-permute-start(bf16[256,768]{1,0:T(8,128)(2,1)S(1)} %get-tuple-element.291.refs_3_), channel_id=1, source_target_pairs={{0,2},{2,0},{1,3},{3,1},{4,6},{6,4},{5,7},{7,5},{8,10},{10,8},{9,1... | collective-permute-start | bytes 1179656 | tf_op jit(solution)/shard_map/ppermute | solution.py:29
  307.2 30.8 %collective-permute-start.29 = (bf16[256,768]{1,0:T(8,128)(2,1)}, bf16[256,768]{1,0:T(8,128)(2,1)}, u32[]{:S(2)}, u32[]{:S(2)}) collective-permute-start(bf16[256,768]{1,0:T(8,128)(2,1)} %get-tuple-element.273.refs_1_), channel_id=1, source_target_pairs={{0,2},{2,0},{1,3},{3,1},{4,6},{6,4},{5,7},{7,5},{8,10},{10,8},{9,1... | collective-permute-start | bytes 1179656 | tf_op jit(solution)/shard_map/ppermute | solution.py:29
  316.5 23.7 %collective-permute-start.31 = (bf16[256,768]{1,0:T(8,128)(2,1)}, bf16[256,768]{1,0:T(8,128)(2,1)}, u32[]{:S(2)}, u32[]{:S(2)}) collective-permute-start(bf16[256,768]{1,0:T(8,128)(2,1)} %get-tuple-element.283.refs_1_), channel_id=1, source_target_pairs={{0,2},{2,0},{1,3},{3,1},{4,6},{6,4},{5,7},{7,5},{8,10},{10,8},{9,1... | collective-permute-start | bytes 1179656 | tf_op jit(solution)/shard_map/ppermute | solution.py:29
  331.5 51.4 %collective-permute-start.43 = (bf16[768,576]{0,1:T(8,128)(2,1)}, bf16[768,576]{0,1:T(8,128)(2,1)}, u32[]{:S(2)}, u32[]{:S(2)}) collective-permute-start(bf16[768,576]{0,1:T(8,128)(2,1)} %copy.200), channel_id=1, source_target_pairs={{0,1},{1,0},{2,3},{3,2},{4,5},{5,4},{6,7},{7,6},{8,9},{9,8},{10,11... | collective-permute-start | bytes 2654216 | tf_op jit(solution)/shard_map/ppermute | solution.py:25
  337.9 65.1 %collective-permute-start.52 = (bf16[768,768]{1,0:T(8,128)(2,1)}, bf16[768,768]{1,0:T(8,128)(2,1)}, u32[]{:S(2)}, u32[]{:S(2)}) collective-permute-start(bf16[768,768]{1,0:T(8,128)(2,1)} %convolution_convert_fusion.1), channel_id=1, source_target_pairs={{0,1},{1,0},{2,3},{3,2},{4,5},{5,4},{6,7},{7,6},{8,9},{9,8},{10,11... | collective-permute-start | bytes 3538952 | tf_op jit(solution)/shard_map/ppermute | solution.py:25
  382.6 24.0 %collective-permute-start.50 = (bf16[768,768]{1,0:T(8,128)(2,1)}, bf16[768,768]{1,0:T(8,128)(2,1)}, u32[]{:S(2)}, u32[]{:S(2)}) collective-permute-start(bf16[768,768]{1,0:T(8,128)(2,1)} %convolution_convert_fusion.3), channel_id=1, source_target_pairs={{0,1},{1,0},{2,3},{3,2},{4,5},{5,4},{6,7},{7,6},{8,9},{9,8},{10,11... | collective-permute-start | bytes 3538952 | tf_op jit(solution)/shard_map/ppermute | solution.py:25
  462.9 21.2 %collective-permute-start.47 = (f32[90,128]{1,0:T(8,128)S(1)}, f32[90,128]{1,0:T(8,128)S(1)}, u32[]{:S(2)}, u32[]{:S(2)}) collective-permute-start(f32[90,128]{1,0:T(8,128)S(1)} %fusion.65), channel_id=1, source_target_pairs={{0,16},{4,20},{8,24},{12,28},{16,0},{20,4},{24,8},{28,12},{1,17},{... | collective-permute-start | bytes 138248 | tf_op jit(solution)/shard_map/ppermute | solution.py:993
  481.5 21.1 %collective-permute-start.40 = (bf16[128,768]{1,0:T(8,128)(2,1)S(1)}, bf16[128,768]{1,0:T(8,128)(2,1)S(1)}, u32[]{:S(2)}, u32[]{:S(2)}) collective-permute-start(bf16[128,768]{1,0:T(8,128)(2,1)S(1)} %add_convert_fusion.7), channel_id=1, source_target_pairs={{0,16},{4,20},{8,24},{12,28},{16,0},{20,4},{24,8},{28,12},{1,17},{... | collective-permute-start | bytes 589832 | tf_op jit(solution)/shard_map/ppermute | solution.py:998
  (229 other events, 1834.9 us)
Sparse Core Ops, SparseCore 0:
  414.2 254.6 all-reduce.5

commit v2 on v1

v2 whole, which is shorter than its diff:
```python
import functools

import jax
import jax.numpy as jnp
from jax import lax
from jax.experimental import pallas as pl
from jax.experimental.pallas import tpu as pltpu
from jax.sharding import PartitionSpec as P

HEAD_DIM = 64
LAYERS = 2
CHUNK = 256
EPS = 1e-12
ROOT_HALF = 0.7071067811865476
DENSITY = 0.3989422804014327
NEG = -1e30
F32 = jnp.float32
BF16 = jnp.bfloat16
MIB = 1 << 20
CORE_SWAP = [(0, 1), (1, 0), (2, 3), (3, 2)]
CHIP_SWAP = [(0, 2), (2, 0), (1, 3), (3, 1)]


def over_core(value):
    return lax.ppermute(value, "narrow", CORE_SWAP)


def over_chip(value):
    return lax.ppermute(value, "narrow", CHIP_SWAP)


def dot(left, right, left_axis=1, right_axis=0):
    return lax.dot_general(
        left, right, (((left_axis,), (right_axis,)), ((), ())), preferred_element_type=F32
    )


def norm_parts(summed):
    row_mean = jnp.mean(summed, -1, keepdims=True)
    centred = summed - row_mean
    spread = jnp.mean(centred * centred, -1, keepdims=True)
    inverse = lax.rsqrt(spread + EPS)
    return centred * inverse, inverse


def norm_back(upstream, unit_rows, inverse, gain_row):
    scaled = upstream * gain_row
    return inverse * (
        scaled
        - jnp.mean(scaled, -1, keepdims=True)
        - unit_rows * jnp.mean(scaled * unit_rows, -1, keepdims=True)
    )


def gelu_parts(preact):
    size = jnp.abs(preact) * ROOT_HALF
    bell = jnp.exp(-(size * size))
    step = 1.0 / (1.0 + 0.3275911 * size)
    series = step * (
        0.254829592
        + step * (-0.284496736 + step * (1.421413741 + step * (-1.453152027 + step * 1.061405429)))
    )
    tail = 0.5 * series * bell
    cdf = jnp.where(preact >= 0.0, 1.0 - tail, tail)
    return preact * cdf, cdf + preact * DENSITY * bell


ON_CHIP = pl.BlockSpec(memory_space=pltpu.VMEM)


def whole(shape):
    zeros = (0,) * len(shape)
    return pl.BlockSpec(shape, lambda *ids: zeros)


def call(kernel, grid, inputs, outputs, scratch=(), cost=1, limit=16, after=()):
    arrays = [array for array, spec in inputs]
    specs = [spec for array, spec in inputs]
    aliases = {}
    for place, (shape, dtype, spec, buffer) in enumerate(outputs):
        if buffer is not None:
            aliases[len(arrays)] = place
            arrays.append(buffer)
            specs.append(pl.BlockSpec(memory_space=pl.ANY))
    for array in after:
        arrays.append(array)
        specs.append(pl.BlockSpec(memory_space=pl.ANY))
    given, extra = len(inputs), len(aliases) + len(after)

    def body(*refs):
        kernel(*refs[:given], *refs[given + extra :])

    return pl.pallas_call(
        body,
        **({} if grid is None else {"grid": grid}),
        in_specs=specs,
        out_specs=[spec for shape, dtype, spec, buffer in outputs],
        out_shape=[
            jax.ShapeDtypeStruct(shape, dtype) for shape, dtype, spec, buffer in outputs
        ],
        scratch_shapes=list(scratch),
        input_output_aliases=aliases,
        compiler_params=pltpu.CompilerParams(vmem_limit_bytes=limit * MIB),
        cost_estimate=pl.CostEstimate(flops=cost * 4000000000, bytes_accessed=1, transcendentals=0),
    )(*arrays)


def gather_kernel(*refs):
    sources, (rows_ref, turned_ref) = refs[:-2], refs[-2:]
    for place, source in enumerate(sources):
        tile = source[...]
        rows_ref[place] = tile
        turned_ref[place] = tile.astype(F32).T.astype(BF16)


def split_pairs(pair_block, target, head_count):
    lanes = lax.broadcasted_iota(jnp.int32, (CHUNK, 2 * HEAD_DIM), 1)
    low_half = lanes < HEAD_DIM
    for head in range(head_count):
        pair = pair_block[:, (head // 2) * 128 : (head // 2) * 128 + 128]
        keep = low_half if head % 2 == 0 else jnp.logical_not(low_half)
        target[head] = jnp.where(keep, pair, jnp.zeros_like(pair))


def attend_kernel(
    head_count,
    layer,
    place,
    bits_ref,
    q_ref,
    kv_ref,
    turned_ref,
    q_label_ref,
    k_label_ref,
    out_weight_ref,
    context_ref,
    exact_ref,
    logsum_ref,
    share_ref,
    masked_q,
    total,
    top,
    mass,
    score_tiles,
):
    width = head_count * HEAD_DIM
    split_pairs(q_ref[...], masked_q, head_count)
    top[...] = jnp.full_like(top, NEG)
    mass[...] = jnp.zeros_like(mass)
    total[...] = jnp.zeros_like(total)
    tiles = kv_ref.shape[0]
    q_bits = bits_ref[tiles + place]

    def score_tile(tile, carry):
        @pl.when((bits_ref[tile] & q_bits) != 0)
        def _():
            hide = jnp.where(k_label_ref[tile] == q_label_ref[place], 0.0, NEG)
            for head in range(head_count):
                pair = (head // 2) * 128
                scores = dot(kv_ref[tile, :, pair : pair + 128], masked_q[head], 1, 1) + hide
                score_tiles[head, tile] = scores
                highest = jnp.max(scores.reshape(-1, 8, CHUNK), 0)
                top[head] = jnp.maximum(top[head], highest)

        return carry

    lax.fori_loop(0, tiles, score_tile, 0)
    for head in range(head_count):
        top[head] = jnp.broadcast_to(jnp.max(top[head], 0, keepdims=True), (8, CHUNK))

    def weigh_tile(tile, carry):
        @pl.when((bits_ref[tile] & q_bits) != 0)
        def _():
            for head in range(head_count):
                weights = jnp.exp(score_tiles[head, tile] - top[head, 0:1, :])
                mass[head] += jnp.sum(weights.reshape(-1, 8, CHUNK), 0)
                rows = slice(head * HEAD_DIM, (head + 1) * HEAD_DIM)
                total[rows, :] += dot(
                    turned_ref[tile, width + head * HEAD_DIM : width + (head + 1) * HEAD_DIM, :],
                    weights.astype(BF16),
                )

        return carry

    lax.fori_loop(0, tiles, weigh_tile, 0)
    logsum_ref[...] = jnp.zeros_like(logsum_ref)
    for head in range(head_count):
        rows = slice(head * HEAD_DIM, (head + 1) * HEAD_DIM)
        amount = jnp.sum(mass[head], 0, keepdims=True)
        total[rows, :] = total[rows, :] / amount
        logsum_ref[head : head + 1, :] = top[head, 0:1, :] + jnp.log(amount)
    exact = total[...].T
    exact_ref[...] = exact
    context = exact.astype(BF16)
    context_ref[...] = context
    share_ref[...] = dot(context, out_weight_ref[layer]).astype(BF16)


def attend_back_kernel(pair, head_count, chunks, *refs):
    bits_ref, kv_ref, turned_ref, q_label_ref, k_label_ref = refs[:5]
    q_refs, grad_refs, exact_refs, logsum_refs = (
        refs[5 + chunks * k : 5 + chunks * (k + 1)] for k in range(4)
    )
    q_grad_ref, own_ref, other_ref, masked_q, masked_grad, centre, q_total, kv_total = refs[
        5 + 4 * chunks :
    ]
    tiles = kv_ref.shape[0]
    lanes = slice(pair * 128, pair * 128 + 128)
    v_lanes = slice(head_count * HEAD_DIM + pair * 128, head_count * HEAD_DIM + pair * 128 + 128)
    kv_total[...] = jnp.zeros_like(kv_total)
    for place in range(chunks):
        split_pairs(q_refs[place][:, lanes], masked_q, 2)
        split_pairs(grad_refs[place][:, lanes], masked_grad, 2)
        crossed = (grad_refs[place][:, lanes].astype(F32) * exact_refs[place][:, lanes]).T
        for head in range(2):
            rows = slice(head * HEAD_DIM, (head + 1) * HEAD_DIM)
            centre[head : head + 1, :] = jnp.sum(crossed[rows, :], 0, keepdims=True)
        q_total[...] = jnp.zeros_like(q_total)
        q_bits = bits_ref[tiles + place]
        logsum_ref = logsum_refs[place]

        def one_tile(tile, carry):
            @pl.when((bits_ref[tile] & q_bits) != 0)
            def _():
                hide = jnp.where(k_label_ref[tile] == q_label_ref[place], 0.0, NEG)
                key_part = None
                value_part = None
                for head in range(2):
                    number = 2 * pair + head
                    scores = dot(kv_ref[tile, :, lanes], masked_q[head], 1, 1) + hide
                    weights = jnp.exp(scores - logsum_ref[number : number + 1, :])
                    weight_grad = dot(kv_ref[tile, :, v_lanes], masked_grad[head], 1, 1)
                    score_grad = (weights * (weight_grad - centre[head : head + 1, :])).astype(BF16)
                    value_now = dot(weights.astype(BF16), masked_grad[head])
                    key_now = dot(score_grad, masked_q[head])
                    value_part = value_now if value_part is None else value_part + value_now
                    key_part = key_now if key_part is None else key_part + key_now
                    rows = slice(head * HEAD_DIM, (head + 1) * HEAD_DIM)
                    turned = slice(number * HEAD_DIM, (number + 1) * HEAD_DIM)
                    q_total[rows, :] += dot(turned_ref[tile, turned, :], score_grad)
                kv_total[tile, :, :128] += key_part
                kv_total[tile, :, 128:] += value_part

            return carry

        lax.fori_loop(0, tiles, one_tile, 0)
        q_grad_ref[place * CHUNK : (place + 1) * CHUNK, :] = q_total[...].T.astype(
            BF16
        ) * jnp.asarray(HEAD_DIM**-0.5, BF16)
    own_ref[...] = kv_total[: tiles // 2]
    other_ref[...] = kv_total[tiles // 2 :].astype(BF16)


def weight_grad_kernel(chunks, left_start, right_start, *refs):
    lefts, rights, recv_refs = refs[:chunks], refs[chunks : 2 * chunks], refs[2 * chunks : -1]
    out_ref = refs[-1]
    rows, columns = out_ref.shape
    step = CHUNK if rows % CHUNK == 0 else rows
    for start in range(0, rows, step):
        left_lanes = slice(left_start + start, left_start + start + step)
        right_lanes = slice(right_start, right_start + columns)
        total = None
        for left, right in zip(lefts, rights):
            part = dot(left[:, left_lanes], right[:, right_lanes], 0, 0)
            total = part if total is None else total + part
        for recv_ref in recv_refs:
            total = total + recv_ref[start : start + step, :].astype(F32)
        out_ref[start : start + step, :] = total.astype(out_ref.dtype)


def out_grad_kernel(chunks, core_ref, *refs):
    lefts, rights, (own_ref, other_ref, full) = refs[:chunks], refs[chunks:-3], refs[-3:]
    total = None
    for left, right in zip(lefts, rights):
        part = dot(left[...], right[...], 0, 0)
        total = part if total is None else total + part
    full[...] = total
    local = own_ref.shape[0]
    own_ref[...] = full[pl.ds(pl.multiple_of(core_ref[0] * local, local), local), :]
    other_ref[...] = full[pl.ds(pl.multiple_of((1 - core_ref[0]) * local, local), local), :].astype(
        BF16
    )


def feed_kernel(
    layer,
    place,
    unit_ref,
    share_ref,
    recv_ref,
    vec_ref,
    up_own_ref,
    up_other_ref,
    bias_ref,
    down_own_ref,
    down_other_ref,
    new_unit_ref,
    inverse_ref,
    low_ref,
    act_ref,
    slope_ref,
    part_ref,
):
    stream = unit_ref[...] * vec_ref[layer, 6:7, :] + vec_ref[layer, 7:8, :]
    attention = share_ref[...].astype(F32) + recv_ref[...].astype(F32)
    unit, inverse = norm_parts(stream + attention + vec_ref[layer, 0:1, :])
    new_unit_ref[...] = unit
    inverse_ref[...] = inverse
    low_ref[...] = (unit * vec_ref[layer, 1:2, :] + vec_ref[layer, 2:3, :]).astype(BF16)
    units = up_own_ref.shape[2]
    total = None
    for half, (up_ref, down_ref) in enumerate(
        ((up_own_ref, down_own_ref), (up_other_ref, down_other_ref))
    ):
        lanes = slice(half * units, (half + 1) * units)
        act, slope = gelu_parts(dot(low_ref[...], up_ref[layer]) + bias_ref[layer, :, lanes])
        low_act = act.astype(BF16)
        act_ref[:, lanes] = low_act
        slope_ref[:, lanes] = slope.astype(BF16)
        part = dot(low_act, down_ref[layer])
        total = part if total is None else total + part
    part_ref[...] = total.astype(BF16)


def project_kernel(
    layer,
    place,
    unit_ref,
    share_ref,
    recv_ref,
    vec_ref,
    q_weight_ref,
    kv_weight_ref,
    q_bias_ref,
    kv_bias_ref,
    new_unit_ref,
    inverse_ref,
    low_ref,
    q_ref,
    kv_ref,
):
    old = layer - 1
    middle = unit_ref[...] * vec_ref[old, 1:2, :] + vec_ref[old, 2:3, :]
    feed = share_ref[...].astype(F32) + recv_ref[...].astype(F32)
    unit, inverse = norm_parts(middle + feed + vec_ref[old, 3:4, :])
    new_unit_ref[...] = unit
    inverse_ref[...] = inverse
    low = (unit * vec_ref[old, 4:5, :] + vec_ref[old, 5:6, :]).astype(BF16)
    low_ref[...] = low
    kv_ref[...] = (dot(low, kv_weight_ref[layer], 1, 1) + kv_bias_ref[layer]).astype(BF16)
    q_ref[...] = (
        (dot(low, q_weight_ref[layer], 1, 1) + q_bias_ref[layer]) * HEAD_DIM**-0.5
    ).astype(BF16)


def feed_back_kernel(
    layer,
    place,
    top_layer,
    up_ref,
    unit_ref,
    inverse_ref,
    share_ref,
    recv_ref,
    vec_ref,
    slope_ref,
    up_own_ref,
    up_other_ref,
    down_own_ref,
    down_other_ref,
    encoded_ref,
    total_ref,
    low_ref,
    grad_ref,
    bias_ref,
    sums_ref,
    part_ref,
):
    keep_span = slice(place * CHUNK, (place + 1) * CHUNK)
    added = share_ref[...].astype(F32) + recv_ref[...].astype(F32)
    if top_layer:
        middle = unit_ref[...] * vec_ref[layer, 1:2, :] + vec_ref[layer, 2:3, :]
        unit, inverse = norm_parts(middle + added + vec_ref[layer, 3:4, :])
        encoded_ref[...] = (unit * vec_ref[layer, 4:5, :] + vec_ref[layer, 5:6, :]).astype(BF16)
        upstream = up_ref[keep_span, :].astype(F32)
    else:
        unit = unit_ref[...]
        inverse = inverse_ref[...]
        upstream = up_ref[...] + added
        encoded_ref[...] = jnp.zeros_like(encoded_ref)
    second = norm_back(upstream, unit, inverse, vec_ref[layer, 4:5, :])
    sums_ref[...] = jnp.zeros_like(sums_ref)
    sums_ref[0:1, :] = jnp.sum(upstream * unit, 0, keepdims=True)
    sums_ref[1:2, :] = jnp.sum(upstream, 0, keepdims=True)
    sums_ref[2:3, :] = jnp.sum(second, 0, keepdims=True)
    total_ref[...] = second
    low_ref[...] = second.astype(BF16)
    units = up_own_ref.shape[2]
    total = None
    for half, (up_weight_ref, down_ref) in enumerate(
        ((up_own_ref, down_own_ref), (up_other_ref, down_other_ref))
    ):
        lanes = slice(half * units, (half + 1) * units)
        grad = (
            dot(low_ref[...], down_ref[layer], 1, 1) * slope_ref[:, lanes].astype(F32)
        ).astype(BF16)
        grad_ref[:, lanes] = grad
        bias_ref[:, lanes] = jnp.sum(grad.astype(F32), 0, keepdims=True)
        part = dot(grad, up_weight_ref[layer], 1, 1)
        total = part if total is None else total + part
    part_ref[...] = total.astype(BF16)


def context_back_kernel(
    layer,
    place,
    second_ref,
    share_ref,
    recv_ref,
    unit_ref,
    inverse_ref,
    vec_ref,
    out_weight_ref,
    total_ref,
    low_ref,
    grad_ref,
    sums_ref,
):
    added = share_ref[...].astype(F32) + recv_ref[...].astype(F32)
    upstream = second_ref[...] + added
    unit = unit_ref[...]
    first = norm_back(upstream, unit, inverse_ref[...], vec_ref[layer, 1:2, :])
    sums_ref[...] = jnp.zeros_like(sums_ref)
    sums_ref[0:1, :] = jnp.sum(upstream * unit, 0, keepdims=True)
    sums_ref[1:2, :] = jnp.sum(upstream, 0, keepdims=True)
    sums_ref[2:3, :] = jnp.sum(first, 0, keepdims=True)
    total_ref[...] = first
    low = first.astype(BF16)
    low_ref[...] = low
    grad_ref[...] = dot(low, out_weight_ref[layer], 1, 1).astype(BF16)


def joint_back_kernel(layer, place, core_ref, *refs):
    pairs = (len(refs) - 6) // 3
    q_refs, own_refs, recv_refs = (refs[k * pairs : (k + 1) * pairs] for k in range(3))
    q_weight_ref, kv_weight_ref, mine_ref, theirs_ref, bias_ref, part_ref = refs[3 * pairs :]
    width = 128 * pairs
    local = width // 2
    keep_span = slice(place * CHUNK, (place + 1) * CHUNK)
    q_grad = jnp.concatenate([ref[keep_span, :] for ref in q_refs], 1)
    both = [
        (own[place] + recv[place].astype(F32)).astype(BF16) for own, recv in zip(own_refs, recv_refs)
    ]
    kv_grad = jnp.concatenate(
        [part[:, :128] for part in both] + [part[:, 128:] for part in both], 1
    )
    first = core_ref[0] == 0
    for member, value in enumerate((q_grad, kv_grad[:, :width], kv_grad[:, width:])):
        left, right = value[:, :local].astype(F32), value[:, local:].astype(F32)
        lanes = slice(member * local, (member + 1) * local)
        mine_ref[:, lanes] = jnp.where(first, left, right).astype(BF16)
        theirs_ref[:, lanes] = jnp.where(first, right, left).astype(BF16)
    bias_ref[...] = jnp.zeros_like(bias_ref)
    bias_ref[0:1, :] = jnp.sum(q_grad.astype(F32), 0, keepdims=True)
    bias_ref[1:2, :] = jnp.sum(kv_grad[:, width:].astype(F32), 0, keepdims=True)
    part_ref[...] = (
        dot(q_grad, q_weight_ref[layer]) + dot(kv_grad, kv_weight_ref[layer])
    ).astype(BF16)


def weights_kernel(core_ref, *refs):
    sources, vectors, small_ref, other_ref = refs[:8], refs[8:14], refs[14], refs[15]
    q_ref, kv_ref, out_ref, vec_ref, q_bias_ref, kv_bias_ref, unit_bias_ref = refs[16:]
    local = sources[0].shape[1]
    width = 2 * local
    own_row = pl.multiple_of(core_ref[0] * local, local)
    other_row = pl.multiple_of((1 - core_ref[0]) * local, local)
    for layer in range(LAYERS):
        for member, (target, start) in enumerate(
            ((q_ref, 0), (kv_ref, 0), (kv_ref, width), (out_ref, 0))
        ):
            target[layer, pl.ds(start + own_row, local), :] = sources[2 * member][layer]
            target[layer, pl.ds(start + other_row, local), :] = sources[2 * member + 1][layer]

    first = core_ref[0] == 0
    for layer in range(LAYERS):
        row = slice(layer, layer + 1)
        for member, vector in enumerate(vectors):
            vec_ref[layer, member : member + 1, :] = vector[...].astype(F32)[row]
        if layer == 0:
            vec_ref[layer, 6:7, :] = jnp.ones_like(vec_ref[layer, 6:7, :])
            vec_ref[layer, 7:8, :] = jnp.zeros_like(vec_ref[layer, 7:8, :])
        else:
            vec_ref[layer, 6:8, :] = vec_ref[layer - 1, 4:6, :]
        own = small_ref[...].astype(F32)[row]
        other = other_ref[...].astype(F32)[row]
        kv_bias_ref[layer] = jnp.zeros_like(kv_bias_ref[layer])
        for target, start, lanes in (
            (q_bias_ref, 0, slice(0, local)),
            (kv_bias_ref, width, slice(local, width)),
        ):
            left, right = own[:, lanes], other[:, lanes]
            target[layer, :, start : start + local] = jnp.where(first, left, right)
            target[layer, :, start + local : start + width] = jnp.where(first, right, left)
        units = own.shape[1] - width
        unit_bias_ref[layer, :, :units] = own[:, width:]
        unit_bias_ref[layer, :, units:] = other[:, width:]


def widen_kernel(source_ref, target_ref):
    target_ref[0] = source_ref[...].astype(F32)


def unpack_rows_kernel(place_ref, *refs):
    count = 1 if len(refs) == 2 else 4
    sources, targets = refs[:-count], refs[-count:]
    rows = targets[0].shape[1]
    start = 0
    for number, source in enumerate(sources):
        pieces, size = source.shape[0], source.shape[1]
        for piece in range(pieces):
            target, row = targets[start // rows], start % rows
            target[0, row : row + size, :] = source[piece ^ place_ref[number]].astype(F32)
            start += size


class Wide:
    def __init__(self, size):
        self.small = size == 8
        index = lax.axis_index("wide")
        self.bits = {}
        if self.small:
            for name, reach in (("y", 1), ("near", 2), ("far", 4)):
                self.bits[name] = (
                    (index // reach) % 2,
                    [(number, number ^ reach) for number in range(size)],
                )

    def place(self, order):
        if not self.small:
            return jnp.int32(0)
        first, second, third = (self.bits[name][0] for name in order)
        return (first * 4 + second * 2 + third).astype(jnp.int32)

    def chain(self, value, order):
        return Chain(self, value, order)

    def exchanged(self, value):
        if not self.small:
            return lax.psum(value, "wide")
        for name in ("y", "near", "far"):
            low = value.astype(BF16)
            value = low.astype(F32) + lax.ppermute(low, "wide", self.bits[name][1]).astype(F32)
        return value


def gate(value, *later):
    return lax.optimization_barrier((value,) + later)[0] if later else value


class Chain:
    def __init__(self, wide, value, order):
        self.wide, self.order, self.step = wide, order, 0
        self.addends, self.pieces = [value], None

    def advance(self, *later):
        if not self.wide.small:
            if self.pieces is None:
                value = self.addends[0]
                self.pieces = lax.psum(value, "wide").reshape(8, -1, value.shape[1])
            return self.pieces
        self.step += 1
        if self.step <= 3:
            bit, pairs = self.wide.bits[self.order[self.step - 1]]
            parts = self.addends[:-1] + [gate(self.addends[-1], *later)]
            split = [part.reshape(2, part.shape[0] // 2, part.shape[1]) for part in parts]
            sent = sum(
                lax.dynamic_index_in_dim(part, 1 - bit, 0, False).astype(F32) for part in split
            ).astype(BF16)
            mine = [lax.dynamic_index_in_dim(part, bit, 0, False) for part in split]
            self.addends = mine + [lax.ppermute(sent, "wide", pairs)]
            return sent
        if self.step == 4:
            parts = self.addends[:-1] + [gate(self.addends[-1], *later)]
            sent = sum(part.astype(F32) for part in parts).astype(BF16)[None]
        else:
            sent = jnp.concatenate([self.pieces, gate(self.received, *later)], 0)
        self.pieces = sent
        self.received = lax.ppermute(sent, "wide", self.wide.bits[self.order[6 - self.step]][1])
        return sent

    def finish(self, *later):
        while self.step < 6 and self.wide.small:
            self.advance()
        if not self.wide.small:
            return self.advance()
        return jnp.concatenate([self.pieces, gate(self.received, *later)], 0)


def on_device(wide, *arguments):
    (
        tokens,
        buckets,
        lengths,
        type_table,
        query_weight,
        query_bias,
        key_weight,
        value_weight,
        value_bias,
        output_weight,
        output_bias,
        attention_gain,
        attention_shift,
        up_weight,
        up_bias,
        down_weight,
        down_bias,
        feed_gain,
        feed_shift,
        cotangent,
    ) = arguments
    share, model = tokens.shape
    lane = 2 * share
    chunks = lane // CHUNK
    local = query_weight.shape[2]
    width = 2 * local
    head_count = width // HEAD_DIM
    units = up_weight.shape[2]
    place = lax.axis_index("narrow")
    chip, core = place // 2, place % 2
    first_chip, first_core = chip == 0, core == 0

    def by_core(own, other, axis):
        return jnp.where(
            first_core,
            jnp.concatenate([own, other], axis),
            jnp.concatenate([other, own], axis),
        )

    def by_chip(own, other):
        return jnp.where(
            first_chip, jnp.concatenate([own, other], 0), jnp.concatenate([other, own], 0)
        )

    def own_rows(rows):
        return jnp.where(first_chip, rows[:share], rows[share:])

    def other_rows(rows):
        return jnp.where(first_chip, rows[share:], rows[:share])

    lane_tokens = by_chip(tokens, over_chip(tokens))
    lane_buckets = by_chip(buckets, over_chip(buckets))
    lane_cotangent = by_chip(cotangent, over_chip(cotangent))

    smem = pl.BlockSpec(memory_space=pltpu.SMEM)
    core_number = core.astype(jnp.int32).reshape(1)
    shards = []
    turned_weights = [
        jnp.swapaxes(weight, 1, 2) for weight in (query_weight, key_weight, value_weight)
    ]
    for weight in turned_weights + [output_weight]:
        shards += [(weight, ON_CHIP), (over_core(weight), ON_CHIP)]

    small = jnp.concatenate([query_bias, value_bias, up_bias], 1)
    vectors = [
        output_bias,
        attention_gain,
        attention_shift,
        down_bias,
        feed_gain,
        feed_shift,
        small,
        over_core(small),
    ]
    qw, kvw, ow, vec, q_bias, kv_bias, unit_bias = call(
        weights_kernel,
        None,
        [(core_number, smem)] + shards + [(vector, ON_CHIP) for vector in vectors],
        [
            (shape, dtype, ON_CHIP, None)
            for shape, dtype in (
                ((LAYERS, width, model), BF16),
                ((LAYERS, 2 * width, model), BF16),
                ((LAYERS, width, model), BF16),
                ((LAYERS, 8, model), F32),
                ((LAYERS, 1, width), F32),
                ((LAYERS, 1, 2 * width), F32),
                ((LAYERS, 1, 2 * units), F32),
            )
        ],
    )
    up_other = over_core(up_weight)
    down_other = over_core(down_weight)

    ends = jnp.cumsum(lengths[0], dtype=jnp.int32)
    offsets = lax.iota(jnp.int32, share)
    spots = jnp.concatenate(
        [
            offsets + (block * 2 + which) * share
            for which in (core, 1 - core)
            for block in range(2)
        ]
    )
    labels = jnp.sum((spots[:, None] >= ends[None, :]).astype(jnp.int32), 1, dtype=jnp.int32)
    tiles = 2 * chunks
    tile_labels = labels.reshape(tiles, CHUNK)
    present = jnp.any(
        tile_labels[:, :, None] == lax.iota(jnp.int32, lengths.shape[1])[None, None, :], axis=1
    )
    bits = jnp.sum(
        jnp.where(present, jnp.left_shift(1, lax.iota(jnp.int32, lengths.shape[1]))[None, :], 0),
        axis=1,
        dtype=jnp.int32,
    )
    bits = jnp.concatenate([bits, bits[:chunks]])
    k_labels = tile_labels[:, :, None]
    q_labels = tile_labels[:chunks, None, :]

    block = (CHUNK, model)

    def layer_spec(layer, shape):
        return pl.BlockSpec((1,) + shape, lambda *ids: (layer,) + (0,) * len(shape))

    selector = (lane_buckets[:, None] == lax.iota(jnp.int32, type_table.shape[0])[None, :]).astype(
        BF16
    )
    stream = lane_tokens.astype(F32) + dot(selector, type_table)
    low_first = stream.astype(BF16)
    state = [stream[CHUNK * i : CHUNK * (i + 1)] for i in range(chunks)]
    kept = []
    for layer in range(LAYERS):
        keep = {}
        if layer == 0:
            kv = (dot(low_first, kvw[0], 1, 1) + kv_bias[0]).astype(BF16)
            queries = ((dot(low_first, qw[0], 1, 1) + q_bias[0]) * HEAD_DIM**-0.5).astype(BF16)
            low_in, kv, queries = (
                [value[CHUNK * i : CHUNK * (i + 1)] for i in range(chunks)]
                for value in (low_first, kv, queries)
            )
            kv_other = [over_core(part) for part in kv]
        else:
            low_in, queries, kv, kv_other = [], [], [], []
            units_now, inverses = [], []
            for i in range(chunks):
                outs = call(
                    functools.partial(project_kernel, layer, i),
                    None,
                    [
                        (value, ON_CHIP)
                        for value in (
                            state[i],
                            feed_share[i],
                            feed_recv[i],
                            vec,
                            qw,
                            kvw,
                            q_bias,
                            kv_bias,
                        )
                    ],
                    [
                        (block, F32, ON_CHIP, None),
                        ((CHUNK, 1), F32, ON_CHIP, None),
                        (block, BF16, ON_CHIP, None),
                        ((CHUNK, width), BF16, ON_CHIP, None),
                        ((CHUNK, 2 * width), BF16, ON_CHIP, None),
                    ],
                    cost=2,
                )
                units_now.append(outs[0])
                inverses.append(outs[1])
                low_in.append(outs[2])
                queries.append(outs[3])
                kv.append(outs[4])
                kv_other.append(over_core(outs[4]))
            state = units_now
            kept[layer - 1]["second_unit"] = units_now
            kept[layer - 1]["second_inverse"] = inverses
        kv_all, turned = call(
            gather_kernel,
            None,
            [(part, ON_CHIP) for part in kv + kv_other],
            [
                ((tiles, CHUNK, 2 * width), BF16, ON_CHIP, None),
                ((tiles, 2 * width, CHUNK), BF16, ON_CHIP, None),
            ],
            cost=2,
        )
        context, exact, logsum, shares = [], [], [], []
        for i in range(chunks):
            outs = call(
                functools.partial(attend_kernel, head_count, layer, i),
                None,
                [(bits, smem)]
                + [
                    (value, ON_CHIP)
                    for value in (queries[i], kv_all, turned, q_labels, k_labels, ow)
                ],
                [
                    ((CHUNK, width), BF16, ON_CHIP, None),
                    ((CHUNK, width), F32, ON_CHIP, None),
                    ((8, CHUNK), F32, ON_CHIP, None),
                    (block, BF16, ON_CHIP, None),
                ],
                scratch=[
                    pltpu.VMEM((head_count, CHUNK, 128), BF16),
                    pltpu.VMEM((width, CHUNK), F32),
                    pltpu.VMEM((head_count, 8, CHUNK), F32),
                    pltpu.VMEM((head_count, 8, CHUNK), F32),
                    pltpu.VMEM((head_count, tiles, CHUNK, CHUNK), F32),
                ],
                cost=6,
                limit=20,
            )
            for target, value in zip((context, exact, logsum, shares), outs):
                target.append(value)
        received = [over_chip(part) for part in shares]
        low_middle, act, slope, first_unit, first_inverse, feed_share = [], [], [], [], [], []
        for i in range(chunks):
            outs = call(
                functools.partial(feed_kernel, layer, i),
                None,
                [
                    (value, ON_CHIP)
                    for value in (
                        state[i],
                        shares[i],
                        received[i],
                        vec,
                        up_weight,
                        up_other,
                        unit_bias,
                        down_weight,
                        down_other,
                    )
                ],
                [
                    (block, F32, ON_CHIP, None),
                    ((CHUNK, 1), F32, ON_CHIP, None),
                    (block, BF16, ON_CHIP, None),
                    ((CHUNK, 2 * units), BF16, ON_CHIP, None),
                    ((CHUNK, 2 * units), BF16, ON_CHIP, None),
                    (block, BF16, ON_CHIP, None),
                ],
                cost=8,
            )
            for target, value in zip(
                (first_unit, first_inverse, low_middle, act, slope, feed_share), outs
            ):
                target.append(value)
        feed_recv = [over_chip(part) for part in feed_share]
        state = first_unit
        keep.update(
            low_in=low_in,
            queries=queries,
            kv_all=kv_all,
            turned=turned,
            context=context,
            exact=exact,
            logsum=logsum,
            first_unit=first_unit,
            first_inverse=first_inverse,
            low_middle=low_middle,
            act=act,
            slope=slope,
        )
        kept.append(keep)

    sums = Wide(wide)
    pair_order, other_order = ("y", "near", "far"), ("near", "y", "far")

    def halves(full, axis):
        left, right = jnp.split(full, 2, axis)
        return jnp.where(first_core, left, right), jnp.where(first_core, right, left)

    def unpacked(kernel, layer, places, sources, shapes, buffers, scratch=()):
        return call(
            kernel,
            (1,),
            ([] if places is None else [(jnp.stack(places), smem)])
            + [(source, whole(source.shape)) for source in sources],
            [
                ((LAYERS,) + shape, F32, layer_spec(layer, shape), buffer)
                for shape, buffer in zip(shapes, buffers)
            ],
            scratch,
        )

    turned_out = [None] * 4
    shared = [None] * LAYERS
    split_vectors = [None] * LAYERS
    encoded = []
    for layer in reversed(range(LAYERS)):
        keep = kept[layer]
        top_layer = layer == LAYERS - 1
        second, low_second, up_grad, unit_sums, second_sums, parts = [], [], [], [], [], []
        for i in range(chunks):
            if top_layer:
                upstream = lane_cotangent
                unit = keep["first_unit"][i]
                inverse = keep["first_inverse"][i]
                added = (feed_share[i], feed_recv[i])
            else:
                upstream = first_total[i]
                unit = keep["second_unit"][i]
                inverse = keep["second_inverse"][i]
                added = (joint_share[i], joint_recv[i])
            outs = call(
                functools.partial(feed_back_kernel, layer, i, top_layer),
                None,
                [
                    (value, ON_CHIP)
                    for value in (
                        upstream,
                        unit,
                        inverse,
                        added[0],
                        added[1],
                        vec,
                        keep["slope"][i],
                        up_weight,
                        up_other,
                        down_weight,
                        down_other,
                    )
                ],
                [
                    (block if top_layer else (8, 128), BF16, ON_CHIP, None),
                    (block, F32, ON_CHIP, None),
                    (block, BF16, ON_CHIP, None),
                    ((CHUNK, 2 * units), BF16, ON_CHIP, None),
                    ((1, 2 * units), F32, ON_CHIP, None),
                    ((8, model), F32, ON_CHIP, None),
                    (block, BF16, ON_CHIP, None),
                ],
                cost=8,
                after=[upper.advance(*second_sums[1:2])] if i != 1 and not top_layer else [],
            )
            if top_layer:
                encoded.append(outs[0])
            for target, value in zip(
                (second, low_second, up_grad, unit_sums, second_sums, parts), outs[1:]
            ):
                target.append(value)
        received = [over_chip(part) for part in parts]

        def weight_grad(lefts, rights, shape, left_start=0, right_start=0, received=()):
            return call(
                functools.partial(weight_grad_kernel, chunks, left_start, right_start),
                None,
                [(value, ON_CHIP) for value in [*lefts, *rights, *received]],
                [(shape, BF16, ON_CHIP, None)],
                cost=2,
            )[0]

        square = (model, units)
        down_other_grad = over_core(
            weight_grad(keep["act"], low_second, square[::-1], left_start=units)
        )
        up_other_grad = over_core(
            weight_grad(keep["low_middle"], up_grad, square, right_start=units)
        )
        down_grad = weight_grad(
            keep["act"], low_second, square[::-1], received=[down_other_grad]
        )
        up_weight_grad = weight_grad(
            keep["low_middle"], up_grad, square, received=[up_other_grad]
        )
        first_total, low_total, context_grad, first_sums = [], [], [], []
        for i in range(chunks):
            outs = call(
                functools.partial(context_back_kernel, layer, i),
                None,
                [
                    (value, ON_CHIP)
                    for value in (
                        second[i],
                        parts[i],
                        received[i],
                        keep["first_unit"][i],
                        keep["first_inverse"][i],
                        vec,
                        ow,
                    )
                ],
                [
                    (block, F32, ON_CHIP, None),
                    (block, BF16, ON_CHIP, None),
                    ((CHUNK, width), BF16, ON_CHIP, None),
                    ((8, model), F32, ON_CHIP, None),
                ],
                after=[upper.advance(second_sums[2])] if i == 1 and not top_layer else [],
            )
            for target, value in zip((first_total, low_total, context_grad, first_sums), outs):
                target.append(value)
        own, other = call(
            functools.partial(out_grad_kernel, chunks),
            None,
            [(core_number, smem)]
            + [(value, ON_CHIP) for value in keep["context"] + low_total],
            [((local, model), F32, ON_CHIP, None), ((local, model), BF16, ON_CHIP, None)],
            scratch=[pltpu.VMEM((width, model), F32)],
        )
        out_grad = (own + over_core(other).astype(F32)).astype(BF16)
        pending = [out_grad, up_weight_grad, down_grad]
        if top_layer:
            feed_sums = lax.psum((up_weight_grad, down_grad), "wide")
        else:
            strands = [
                sums.chain(up_weight_grad, pair_order),
                sums.chain(down_grad, other_order),
            ]
            pending = [out_grad, upper.advance(first_sums[2])] + [
                strand.advance() for strand in strands
            ]
        half_shape = (chunks, CHUNK, 256)
        q_grads, kv_owns, kv_recvs = [], [], []
        for pair in range(head_count // 2):
            q_grad, kv_grad, kv_grad_other = call(
                functools.partial(attend_back_kernel, pair, head_count, chunks),
                None,
                [(bits, smem)]
                + [
                    (value, ON_CHIP)
                    for value in [keep["kv_all"], keep["turned"], q_labels, k_labels]
                    + keep["queries"]
                    + context_grad
                    + keep["exact"]
                    + keep["logsum"]
                ],
                [
                    ((lane, 128), BF16, ON_CHIP, None),
                    (half_shape, F32, ON_CHIP, None),
                    (half_shape, BF16, ON_CHIP, None),
                ],
                scratch=[
                    pltpu.VMEM((2, CHUNK, 128), BF16),
                    pltpu.VMEM((2, CHUNK, 128), BF16),
                    pltpu.VMEM((8, CHUNK), F32),
                    pltpu.VMEM((128, CHUNK), F32),
                    pltpu.VMEM((tiles, CHUNK, 256), F32),
                ],
                cost=10,
                limit=16,
                after=pending + q_grads[-1:],
            )
            pending = []
            if not top_layer:
                if pair < 2:
                    pending = [upper.advance(q_grad)]
                pending += [strand.advance(q_grad) for strand in strands]
            q_grads.append(q_grad)
            kv_owns.append(kv_grad)
            kv_recvs.append(over_core(kv_grad_other))
        joint_own, joint_other, bias_sums, joint_share = [], [], [], []
        for i in range(chunks):
            outs = call(
                functools.partial(joint_back_kernel, layer, i),
                None,
                [(core_number, smem)]
                + [(value, ON_CHIP) for value in q_grads + kv_owns + kv_recvs + [qw, kvw]],
                [
                    ((CHUNK, 3 * local), BF16, ON_CHIP, None),
                    ((CHUNK, 3 * local), BF16, ON_CHIP, None),
                    ((8, width), F32, ON_CHIP, None),
                    (block, BF16, ON_CHIP, None),
                ],
                cost=2,
            )
            for target, value in zip((joint_own, joint_other, bias_sums, joint_share), outs):
                target.append(value)
        if layer > 0:
            joint_recv = [over_chip(part) for part in joint_share]
        joint_recv_grad = over_core(weight_grad(joint_other, keep["low_in"], (3 * local, model)))
        joint_grad = weight_grad(
            joint_own, keep["low_in"], (3 * local, model), received=[joint_recv_grad]
        )
        flat = [(local, model)] * 4
        if layer > 0:
            upper = sums.chain(jnp.concatenate([joint_grad, out_grad], 0), other_order)
        else:
            (up_out,) = unpacked(
                widen_kernel, 1, None, [gate(feed_sums[0], joint_share[-1])], [square], [None]
            )
            (down_out,) = unpacked(
                widen_kernel, 1, None, [gate(feed_sums[1], joint_share[-1])], [square[::-1]], [None]
            )
            turned_out = unpacked(
                unpack_rows_kernel, 1, [sums.place(other_order)], [upper.finish()], flat, turned_out
            )
            first_chain = sums.chain(joint_grad[: 2 * local], pair_order)
            second_chain = sums.chain(
                jnp.concatenate([joint_grad[2 * local :], out_grad], 0), other_order
            )
            turned_out = unpacked(
                unpack_rows_kernel,
                layer,
                [sums.place(pair_order), sums.place(other_order)],
                [first_chain.finish(), second_chain.finish()],
                flat,
                turned_out,
            )
            (up_out,) = unpacked(
                unpack_rows_kernel,
                layer,
                [sums.place(pair_order)],
                [strands[0].finish()],
                [square],
                [up_out],
            )
            (down_out,) = unpacked(
                unpack_rows_kernel,
                layer,
                [sums.place(other_order)],
                [strands[1].finish()],
                [square[::-1]],
                [down_out],
            )
        second_sum, first_sum = sum(second_sums), sum(first_sums)
        shared[layer] = jnp.concatenate([second_sum[:3], first_sum[:3]], 0)
        unit_sum, bias_sum = sum(unit_sums), sum(bias_sums)
        q_own, q_other = halves(bias_sum[0], 0)
        v_own, v_other = halves(bias_sum[1], 0)
        split_vectors[layer] = (
            jnp.concatenate([q_own, v_own, unit_sum[0, :units]]),
            jnp.concatenate([q_other, v_other, unit_sum[0, units:]]),
        )

    joint_rows = jnp.concatenate(joint_share, 0)
    first_rows = own_rows(jnp.concatenate(first_total, 0))
    joint_theirs = over_chip(other_rows(joint_rows)).astype(F32)
    tokens_grad = first_rows + (own_rows(joint_rows).astype(F32) + joint_theirs)
    own_selector = (buckets[:, None] == lax.iota(jnp.int32, type_table.shape[0])[None, :]).astype(
        BF16
    )
    high = first_rows.astype(BF16)
    rest = (first_rows - high.astype(F32)).astype(BF16)
    table = (
        dot(own_selector, high, 0, 0) + dot(own_selector, rest, 0, 0)
    ) + dot(selector, joint_rows, 0, 0)

    common = jnp.concatenate(shared, 0)
    mine = jnp.stack([value[0] for value in split_vectors])
    theirs = jnp.stack([value[1] for value in split_vectors])
    vectors = jnp.concatenate([common.reshape(-1), mine.reshape(-1)])
    sent = jnp.concatenate([common.reshape(-1), theirs.reshape(-1)])
    vectors = (vectors + over_core(sent)).reshape(-1, model)

    table_own, table_other = halves(table, 0)
    table_half = table_own + over_core(table_other.astype(BF16)).astype(F32)
    low_half = table_half.astype(BF16)
    table_half = low_half.astype(F32) + over_chip(low_half).astype(F32)
    packed = sums.exchanged(jnp.concatenate([table_half, vectors], 0))
    table_half = packed[: table_half.shape[0]]
    vectors = packed[table_half.shape[0] :].reshape(-1)
    low_half = table_half.astype(BF16)
    table_grad = by_core(low_half, over_core(low_half), 0).astype(F32)
    common = vectors[: common.size].reshape(LAYERS, 6, model)
    mine = vectors[common.size :].reshape(LAYERS, -1)

    return (
        own_rows(jnp.concatenate(encoded, 0)),
        tokens_grad,
        table_grad,
        jnp.swapaxes(turned_out[0], 1, 2),
        mine[:, :local],
        jnp.swapaxes(turned_out[1], 1, 2),
        jnp.swapaxes(turned_out[2], 1, 2),
        mine[:, local : 2 * local],
        turned_out[3],
        common[:, 5],
        common[:, 3],
        common[:, 4],
        up_out,
        mine[:, 2 * local :],
        down_out,
        common[:, 2],
        common[:, 0],
        common[:, 1],
    )


def solution(mesh):
    rows = P(("wide", "narrow"), None)
    third = P(None, None, "narrow")
    second = P(None, "narrow")
    middle = P(None, "narrow", None)
    in_specs = (
        rows,
        P(("wide", "narrow")),
        P("wide", None),
        P(),
        third,
        second,
        third,
        third,
        second,
        middle,
        P(),
        P(),
        P(),
        third,
        second,
        middle,
        P(),
        P(),
        P(),
        rows,
    )
    out_specs = (
        rows,
        rows,
        P(),
        third,
        second,
        third,
        third,
        second,
        middle,
        P(),
        P(),
        P(),
        third,
        second,
        middle,
        P(),
        P(),
        P(),
    )
    return jax.shard_map(
        functools.partial(on_device, mesh.shape["wide"]),
        mesh=mesh,
        in_specs=in_specs,
        out_specs=out_specs,
        check_vma=False,
    )
```

time: 700 us -> 580 us (0.83)
  waiting for transfers between devices: 219 us -> 146 us
  Pallas kernels: 228 us -> 173 us
  starting transfers between devices: 61.7 us -> 102 us
  matrix products: 34.7 us -> 4.1 us
  other arithmetic: 53.7 us -> 29.4 us
  local copies, waits for them, and re-layouts: 76.3 us -> 100 us
    psum x1, waiting for transfers between devices: 155 us -> 0.01 us  [on_device(): feed_sums = lax.psum((up_weight_grad, down_grad), 'wide')]
    pallas_call x37 -> x62, Pallas kernels: 228 us -> 173 us  [call(): pl.pallas_call(body, **{} if grid is None else {'grid': grid}, in_specs=s...]
    ppermute x25 -> x26, waiting for transfers between devices: 11.8 us -> 61.9 us  [over_chip(): return lax.ppermute(value, 'narrow', CHIP_SWAP)]
    unnamed x406 -> x528, local copies, waits for them, and re-layouts: 45.8 us -> 84.9 us
    ppermute x7 -> x33, waiting for transfers between devices: 47.9 us -> 82.7 us  [the longest x15 50.3 us: advance(): self.addends = mine + [lax.ppermute(sent, 'wide', pairs)]]
    dot_general x17 -> x6, matrix products: 34.7 us -> 4.1 us  [dot(): lax.dot_general(left, right, (((left_axis,), (right_axis,)), ((), ())), p...]
    ppermute x7 -> x33, starting transfers between devices: 7.92 us -> 34 us  [the longest x15 16 us: advance(): lax.ppermute(sent, 'wide', self.wide.bits[self.order[6 - self.step]][1])]
    ppermute x22 -> x30, starting transfers between devices: 32.7 us -> 48.3 us  [over_core(): return lax.ppermute(value, 'narrow', CORE_SWAP)]
  transfers between devices with their start and end apart: 55 -> 90, of which waited for: 11 -> 33; matrix products, arithmetic and copies ran while one was open for 17% -> 9% of each run, Pallas kernels for 33% -> 26%
where the time goes in v2:
time: 580 us; the launch traced here: 571 us
  Pallas kernels  173 us (30%)
  waiting for transfers between devices  146 us (25%)
  starting transfers between devices  102 us (18%)
  local copies, waits for them, and re-layouts  100 us (17%)
  other arithmetic  29.4 us (5%)
  between operations  17.1 us (3%)
    pallas_call x62, Pallas kernels, call(): pl.pallas_call(body, **{} if grid is None else {'grid': grid}, in_specs=s...  173 us
    unnamed x528, local copies, waits for them, and re-layouts  84.9 us
    ppermute x26, waiting for transfers between devices, over_chip(): return lax.ppermute(value, 'narrow', CHIP_SWAP)  61.9 us
    ppermute x15, waiting for transfers between devices, advance(): self.addends = mine + [lax.ppermute(sent, 'wide', pairs)]  50.3 us
    ppermute x30, starting transfers between devices, over_core(): return lax.ppermute(value, 'narrow', CORE_SWAP)  48.3 us
    ppermute x15, waiting for transfers between devices, advance(): lax.ppermute(sent, 'wide', self.wide.bits[self.order[6 - self.step]][1])  23 us
    ppermute x26, starting transfers between devices, over_chip(): return lax.ppermute(value, 'narrow', CHIP_SWAP)  19.4 us
    ppermute x15, starting transfers between devices, advance(): lax.ppermute(sent, 'wide', self.wide.bits[self.order[6 - self.step]][1])  16 us
  transfers between devices with their start and end apart: 90, of which 33 were waited for; matrix products, arithmetic and copies ran while one was open for 9% of the time, Pallas kernels for 26%

profile of v2, /device:TPU:1, one launch (start us, length us, event | category | flops | bytes accessed | tf_op | source)
XLA Modules:
  0.0 570.6 jit_solution(6495965044920037814)
XLA Ops:
  42.6 5.0 shard_map.333
  49.9 6.3 %shard_map.336 = (bf16[256,384]{1,0:T(8,128)(2,1)S(1)}, f32[256,384]{1,0:T(8,128)S(1)}, f32[8,256]{1,0:T(8,128)S(1)}, bf16[256,768]{1,0:T(8,128)(2,1)S(1)}) custom-call(s32[9]{0:T(128)S(1)} %pad_add_fusion.1.refs_0_, bf16[256,384]{1,0:T(8,128)(2,1)S(1)} %get-tuple-element.477.refs_1_.refs_6_, bf16[6,256,768]{2,1,0:T(8,128)(2,1)S(1)} %get-tuple-element.238.refs_2_.refs_1_, ...), custom_call_target="tpu_custom_call" | custom-call | flops 24000000000 | bytes 1 | tf_op jit(solution)/shard_map/pallas_call | solution.py:93
  80.6 7.2 %collective-permute-start.19 = (bf16[256,768]{1,0:T(8,128)(2,1)S(1)}, bf16[256,768]{1,0:T(8,128)(2,1)}, u32[]{:S(2)}, u32[]{:S(2)}) collective-permute-start(bf16[256,768]{1,0:T(8,128)(2,1)S(1)} %get-tuple-element.248.refs_0_), channel_id=1, source_target_pairs={{0,1},{1,0},{2,3},{3,2},{4,5},{5,4},{6,7},{7,6},{8,9},{9,8},{10,11... | collective-permute-start | bytes 1179656 | tf_op jit(solution)/shard_map/ppermute | solution.py:25
  109.5 5.0 shard_map.343
  116.7 5.8 %shard_map.346 = (bf16[256,384]{1,0:T(8,128)(2,1)S(1)}, f32[256,384]{1,0:T(8,128)S(1)}, f32[8,256]{1,0:T(8,128)S(1)}, bf16[256,768]{1,0:T(8,128)(2,1)S(1)}) custom-call(s32[9]{0:T(128)S(1)} %copy-done.65, bf16[256,384]{1,0:T(8,128)(2,1)S(1)} %copy-done.199, bf16[6,256,768]{2,1,0:T(8,128)(2,1)S(1)} %get-tuple-element.257.refs_2_.refs_1_, ...), custom_call_target="tpu_custom_call" | custom-call | flops 24000000000 | bytes 1 | tf_op jit(solution)/shard_map/pallas_call | solution.py:93
  146.4 5.3 collective-permute-done.25.refs_4_
  170.9 6.1 %collective-permute-done.29.refs_2_ = bf16[256,768]{1,0:T(8,128)(2,1)S(1)} collective-permute-done((bf16[256,768]{1,0:T(8,128)(2,1)S(1)}, bf16[256,768]{1,0:T(8,128)(2,1)S(1)}, u32[]{:S(2)}, u32[]{:S(2)}) %collective-permute-start.29) | collective-permute-done | bytes 393248 | tf_op jit(solution)/shard_map/ppermute | solution.py:29
  178.7 6.8 %collective-permute-done.30.refs_2_ = bf16[256,768]{1,0:T(8,128)(2,1)S(1)} collective-permute-done((bf16[256,768]{1,0:T(8,128)(2,1)S(1)}, bf16[256,768]{1,0:T(8,128)(2,1)S(1)}, u32[]{:S(2)}, u32[]{:S(2)}) %collective-permute-start.30) | collective-permute-done | bytes 393248 | tf_op jit(solution)/shard_map/ppermute | solution.py:29
  205.9 10.7 %shard_map.360 = (bf16[768,128]{1,0:T(8,128)(2,1)S(1)}, f32[3,256,256]{2,1,0:T(8,128)S(1)}, bf16[3,256,256]{2,1,0:T(8,128)(2,1)S(1)}) custom-call(s32[9]{0:T(128)S(1)} %copy-done.66, bf16[6,256,768]{2,1,0:T(8,128)(2,1)S(1)} %copy-done.99, bf16[6,768,256]{2,1,0:T(8,128)(2,1)S(1)} %copy-done.102, s32[3,1,256]{2,1,0:T(1,128)S(1)} %copy-done.18, ...), custom_call_target="tpu_custom_call" | custom-call | flops 40000000000 | bytes 1 | tf_op jit(solution)/shard_map/pallas_call | solution.py:93
  230.0 10.7 %shard_map.361 = (bf16[768,128]{1,0:T(8,128)(2,1)S(1)}, f32[3,256,256]{2,1,0:T(8,128)S(1)}, bf16[3,256,256]{2,1,0:T(8,128)(2,1)S(1)}) custom-call(s32[9]{0:T(128)S(1)} %copy-done.66, bf16[6,256,768]{2,1,0:T(8,128)(2,1)S(1)} %copy-done.100, bf16[6,768,256]{2,1,0:T(8,128)(2,1)S(1)} %copy-done.103, s32[3,1,256]{2,1,0:T(1,128)S(1)} %copy-done.18, ...), custom_call_target="tpu_custom_call" | custom-call | flops 40000000000 | bytes 1 | tf_op jit(solution)/shard_map/pallas_call | solution.py:93
  240.7 10.9 %shard_map.362 = (bf16[768,128]{1,0:T(8,128)(2,1)S(1)}, f32[3,256,256]{2,1,0:T(8,128)S(1)}, bf16[3,256,256]{2,1,0:T(8,128)(2,1)S(1)}) custom-call(s32[9]{0:T(128)S(1)} %copy-done.66, bf16[6,256,768]{2,1,0:T(8,128)(2,1)S(1)} %copy-done.100, bf16[6,768,256]{2,1,0:T(8,128)(2,1)S(1)} %copy-done.103, s32[3,1,256]{2,1,0:T(1,128)S(1)} %copy-done.18, ...), custom_call_target="tpu_custom_call" | custom-call | flops 40000000000 | bytes 1 | tf_op jit(solution)/shard_map/pallas_call | solution.py:93
  277.8 13.4 %collective-permute-done.37.refs_4_ = bf16[256,768]{1,0:T(8,128)(2,1)S(1)} collective-permute-done((bf16[256,768]{1,0:T(8,128)(2,1)}, bf16[256,768]{1,0:T(8,128)(2,1)S(1)}, u32[]{:S(2)}, u32[]{:S(2)}) %collective-permute-start.37) | collective-permute-done | bytes 393248 | tf_op jit(solution)/shard_map/ppermute | solution.py:29
  298.2 5.7 collective-permute-done.39.refs_2_
  304.7 7.5 %collective-permute-done.42 = bf16[384,768]{1,0:T(8,128)(2,1)S(1)} collective-permute-done((bf16[384,768]{1,0:T(8,128)(2,1)S(1)}, bf16[384,768]{1,0:T(8,128)(2,1)S(1)}, u32[]{:S(2)}, u32[]{:S(2)}) %collective-permute-start.42) | collective-permute-done | bytes 589856 | tf_op jit(solution)/shard_map/ppermute | solution.py:581
  331.6 5.7 collective-permute-done.47
  343.2 10.6 %shard_map.379 = (bf16[768,128]{1,0:T(8,128)(2,1)S(1)}, f32[3,256,256]{2,1,0:T(8,128)S(1)}, bf16[3,256,256]{2,1,0:T(8,128)(2,1)S(1)}) custom-call(s32[9]{0:T(128)S(1)} %copy-done.67, bf16[6,256,768]{2,1,0:T(8,128)(2,1)S(1)} %copy-done.95, bf16[6,768,256]{2,1,0:T(8,128)(2,1)S(1)} %copy-done.97, s32[3,1,256]{2,1,0:T(1,128)S(1)} %copy-done.18, ...), custom_call_target="tpu_custom_call" | custom-call | flops 40000000000 | bytes 1 | tf_op jit(solution)/shard_map/pallas_call | solution.py:93
  355.5 7.2 %collective-permute-done.52 = bf16[384,768]{1,0:T(8,128)(2,1)S(1)} collective-permute-done((bf16[384,768]{1,0:T(8,128)(2,1)S(1)}, bf16[384,768]{1,0:T(8,128)(2,1)S(1)}, u32[]{:S(2)}, u32[]{:S(2)}) %collective-permute-start.52) | collective-permute-done | bytes 589856 | tf_op jit(solution)/shard_map/ppermute | solution.py:581
  363.6 10.6 %shard_map.380 = (bf16[768,128]{1,0:T(8,128)(2,1)S(1)}, f32[3,256,256]{2,1,0:T(8,128)S(1)}, bf16[3,256,256]{2,1,0:T(8,128)(2,1)S(1)}) custom-call(s32[9]{0:T(128)S(1)} %copy-done.67, bf16[6,256,768]{2,1,0:T(8,128)(2,1)S(1)} %copy-done.95, bf16[6,768,256]{2,1,0:T(8,128)(2,1)S(1)} %copy-done.97, s32[3,1,256]{2,1,0:T(1,128)S(1)} %copy-done.18, ...), custom_call_target="tpu_custom_call" | custom-call | flops 40000000000 | bytes 1 | tf_op jit(solution)/shard_map/pallas_call | solution.py:93
  381.0 10.8 %shard_map.381 = (bf16[768,128]{1,0:T(8,128)(2,1)S(1)}, f32[3,256,256]{2,1,0:T(8,128)S(1)}, bf16[3,256,256]{2,1,0:T(8,128)(2,1)S(1)}) custom-call(s32[9]{0:T(128)S(1)} %copy-done.67, bf16[6,256,768]{2,1,0:T(8,128)(2,1)S(1)} %copy-done.95, bf16[6,768,256]{2,1,0:T(8,128)(2,1)S(1)} %copy-done.97, s32[3,1,256]{2,1,0:T(1,128)S(1)} %copy-done.18, ...), custom_call_target="tpu_custom_call" | custom-call | flops 40000000000 | bytes 1 | tf_op jit(solution)/shard_map/pallas_call | solution.py:93
  392.7 21.3 %collective-permute-done.81 = bf16[96,768]{1,0:T(8,128)(2,1)S(1)} collective-permute-done((bf16[96,768]{1,0:T(8,128)(2,1)S(1)}, bf16[96,768]{1,0:T(8,128)(2,1)S(1)}, u32[]{:S(2)}, u32[]{:S(2)}) %collective-permute-start.81) | collective-permute-done | bytes 147488 | tf_op jit(solution)/shard_map/ppermute | solution.py:581
  419.8 7.4 %collective-permute-done.82 = bf16[1,96,768]{2,1,0:T(8,128)(2,1)} collective-permute-done((bf16[1,96,768]{2,1,0:T(8,128)(2,1)S(1)}, bf16[1,96,768]{2,1,0:T(8,128)(2,1)}, u32[]{:S(2)}, u32[]{:S(2)}) %collective-permute-start.82) | collective-permute-done | bytes 147488 | tf_op jit(solution)/shard_map/ppermute | solution.py:589
  488.0 5.1 collective-permute-done.84
  539.1 6.2 %collective-permute-done.65 = bf16[143,768]{1,0:T(8,128)(2,1)S(1)} collective-permute-done((bf16[143,768]{1,0:T(8,128)(2,1)S(1)}, bf16[143,768]{1,0:T(8,128)(2,1)S(1)}, u32[]{:S(2)}, u32[]{:S(2)}) %collective-permute-start.65) | collective-permute-done | bytes 219680 | tf_op jit(solution)/shard_map/ppermute | solution.py:553
  545.5 10.1 %collective-permute-start.66 = (bf16[128,768]{1,0:T(8,128)(2,1)S(1)}, bf16[128,768]{1,0:T(8,128)(2,1)S(1)}, u32[]{:S(2)}, u32[]{:S(2)}) collective-permute-start(bf16[128,768]{1,0:T(8,128)(2,1)S(1)} %slice.308), channel_id=1, source_target_pairs={{0,1},{1,0},{2,3},{3,2},{4,5},{5,4},{6,7},{7,6},{8,9},{9,8},{10,11... | collective-permute-start | bytes 589832 | tf_op jit(solution)/shard_map/ppermute | solution.py:25
  (876 shorter events, 352.0 us)
Async XLA Ops:
  16.2 85.0 %collective-permute-start = (bf16[384,768]{1,0:T(8,128)(2,1)}, bf16[384,768]{1,0:T(8,128)(2,1)}, u32[]{:S(2)}, u32[]{:S(2)}) collective-permute-start(bf16[384,768]{1,0:T(8,128)(2,1)} %param.39), channel_id=1, source_target_pairs={{0,2},{2,0},{1,3},{3,1},{4,6},{6,4},{5,7},{7,5},{8,10},{10,8},{9,1... | collective-permute-start | bytes 1769480 | tf_op jit(solution)/shard_map/ppermute | solution.py:29
  17.7 42.1 %collective-permute-start.12 = (bf16[2,768,768]{2,1,0:T(8,128)(2,1)}, bf16[2,768,768]{2,1,0:T(8,128)(2,1)S(1)}, u32[]{:S(2)}, u32[]{:S(2)}) collective-permute-start(bf16[2,768,768]{2,1,0:T(8,128)(2,1)} %refs_7_.25), channel_id=1, source_target_pairs={{0,1},{1,0},{2,3},{3,2},{4,5},{5,4},{6,7},{7,6},{8,9},{9,8},{10,11... | collective-permute-start | bytes 7077896 | tf_op jit(solution)/shard_map/ppermute | solution.py:25
  42.5 31.1 %collective-permute-start.17 = (bf16[256,768]{1,0:T(8,128)(2,1)S(1)}, bf16[256,768]{1,0:T(8,128)(2,1)S(1)}, u32[]{:S(2)}, u32[]{:S(2)}) collective-permute-start(bf16[256,768]{1,0:T(8,128)(2,1)S(1)} %get-tuple-element.253.refs_1_), channel_id=1, source_target_pairs={{0,2},{2,0},{1,3},{3,1},{4,6},{6,4},{5,7},{7,5},{8,10},{10,8},{9,1... | collective-permute-start | bytes 1179656 | tf_op jit(solution)/shard_map/ppermute | solution.py:29
  80.6 22.8 %collective-permute-start.19 = (bf16[256,768]{1,0:T(8,128)(2,1)S(1)}, bf16[256,768]{1,0:T(8,128)(2,1)}, u32[]{:S(2)}, u32[]{:S(2)}) collective-permute-start(bf16[256,768]{1,0:T(8,128)(2,1)S(1)} %get-tuple-element.248.refs_0_), channel_id=1, source_target_pairs={{0,1},{1,0},{2,3},{3,2},{4,5},{5,4},{6,7},{7,6},{8,9},{9,8},{10,11... | collective-permute-start | bytes 1179656 | tf_op jit(solution)/shard_map/ppermute | solution.py:25
  109.3 29.1 %collective-permute-start.26 = (bf16[256,768]{1,0:T(8,128)(2,1)S(1)}, bf16[256,768]{1,0:T(8,128)(2,1)S(1)}, u32[]{:S(2)}, u32[]{:S(2)}) collective-permute-start(bf16[256,768]{1,0:T(8,128)(2,1)S(1)} %get-tuple-element.275.refs_1_), channel_id=1, source_target_pairs={{0,2},{2,0},{1,3},{3,1},{4,6},{6,4},{5,7},{7,5},{8,10},{10,8},{9,1... | collective-permute-start | bytes 1179656 | tf_op jit(solution)/shard_map/ppermute | solution.py:29
  145.8 23.4 %collective-permute-start.28 = (bf16[256,768]{1,0:T(8,128)(2,1)S(1)}, bf16[256,768]{1,0:T(8,128)(2,1)S(1)}, u32[]{:S(2)}, u32[]{:S(2)}) collective-permute-start(bf16[256,768]{1,0:T(8,128)(2,1)S(1)} %get-tuple-element.282.refs_1_), channel_id=1, source_target_pairs={{0,2},{2,0},{1,3},{3,1},{4,6},{6,4},{5,7},{7,5},{8,10},{10,8},{9,1... | collective-permute-start | bytes 1179656 | tf_op jit(solution)/shard_map/ppermute | solution.py:29
  162.6 22.8 %collective-permute-start.30 = (bf16[256,768]{1,0:T(8,128)(2,1)S(1)}, bf16[256,768]{1,0:T(8,128)(2,1)S(1)}, u32[]{:S(2)}, u32[]{:S(2)}) collective-permute-start(bf16[256,768]{1,0:T(8,128)(2,1)S(1)} %get-tuple-element.290.refs_1_), channel_id=1, source_target_pairs={{0,2},{2,0},{1,3},{3,1},{4,6},{6,4},{5,7},{7,5},{8,10},{10,8},{9,1... | collective-permute-start | bytes 1179656 | tf_op jit(solution)/shard_map/ppermute | solution.py:29
  164.4 28.0 %collective-permute-start.33 = (bf16[768,768]{1,0:T(8,128)(2,1)S(1)}, bf16[768,768]{1,0:T(8,128)(2,1)S(1)}, u32[]{:S(2)}, u32[]{:S(2)}) collective-permute-start(bf16[768,768]{1,0:T(8,128)(2,1)S(1)} %shard_map.358), channel_id=1, source_target_pairs={{0,1},{1,0},{2,3},{3,2},{4,5},{5,4},{6,7},{7,6},{8,9},{9,8},{10,11... | collective-permute-start | bytes 3538952 | tf_op jit(solution)/shard_map/ppermute | solution.py:25
  218.2 224.2 %all-reduce.3.cloned.1.call-start = ((), (), s32[]{:S(2)}) async-start(), calls=%async_computation | async-start | bytes 4718592 | tf_op jit(solution)/shard_map/psum | solution.py:1008
  218.2 37.2 %collective-permute-start.34 = (bf16[3,256,256]{2,1,0:T(8,128)(2,1)S(1)}, bf16[3,256,256]{2,1,0:T(8,128)(2,1)S(1)}, u32[]{:S(2)}, u32[]{:S(2)}) collective-permute-start(bf16[3,256,256]{2,1,0:T(8,128)(2,1)S(1)} %get-tuple-element.324), channel_id=1, source_target_pairs={{0,1},{1,0},{2,3},{3,2},{4,5},{5,4},{6,7},{7,6},{8,9},{9,8},{10,11... | collective-permute-start | bytes 1179656 | tf_op jit(solution)/shard_map/ppermute | solution.py:25
  263.7 49.9 %collective-permute-start.44 = (bf16[256,768]{1,0:T(8,128)(2,1)S(1)}, bf16[256,768]{1,0:T(8,128)(2,1)}, u32[]{:S(2)}, u32[]{:S(2)}) collective-permute-start(bf16[256,768]{1,0:T(8,128)(2,1)S(1)} %copy-done.42), channel_id=1, source_target_pairs={{0,2},{2,0},{1,3},{3,1},{4,6},{6,4},{5,7},{7,5},{8,10},{10,8},{9,1... | collective-permute-start | bytes 1179656 | tf_op jit(solution)/shard_map/ppermute | solution.py:29
  265.3 28.8 %collective-permute-start.40 = (bf16[256,768]{1,0:T(8,128)(2,1)}, bf16[256,768]{1,0:T(8,128)(2,1)S(1)}, u32[]{:S(2)}, u32[]{:S(2)}) collective-permute-start(bf16[256,768]{1,0:T(8,128)(2,1)} %copy-done.45), channel_id=1, source_target_pairs={{0,2},{2,0},{1,3},{3,1},{4,6},{6,4},{5,7},{7,5},{8,10},{10,8},{9,1... | collective-permute-start | bytes 1179656 | tf_op jit(solution)/shard_map/ppermute | solution.py:29
  266.6 24.6 %collective-permute-start.37 = (bf16[256,768]{1,0:T(8,128)(2,1)}, bf16[256,768]{1,0:T(8,128)(2,1)S(1)}, u32[]{:S(2)}, u32[]{:S(2)}) collective-permute-start(bf16[256,768]{1,0:T(8,128)(2,1)} %copy-done.49), channel_id=1, source_target_pairs={{0,2},{2,0},{1,3},{3,1},{4,6},{6,4},{5,7},{7,5},{8,10},{10,8},{9,1... | collective-permute-start | bytes 1179656 | tf_op jit(solution)/shard_map/ppermute | solution.py:29
  273.9 38.4 %collective-permute-start.42 = (bf16[384,768]{1,0:T(8,128)(2,1)S(1)}, bf16[384,768]{1,0:T(8,128)(2,1)S(1)}, u32[]{:S(2)}, u32[]{:S(2)}) collective-permute-start(bf16[384,768]{1,0:T(8,128)(2,1)S(1)} %get-tuple-element.469.refs_11_), channel_id=1, source_target_pairs={{0,8},{4,12},{8,0},{12,4},{16,24},{20,28},{24,16},{28,20},{1,9},{5... | collective-permute-start | bytes 1769480 | tf_op jit(solution)/shard_map/ppermute | solution.py:581
  296.8 27.4 %collective-permute-start.41 = (bf16[256,768]{1,0:T(8,128)(2,1)S(1)}, bf16[256,768]{1,0:T(8,128)(2,1)S(1)}, u32[]{:S(2)}, u32[]{:S(2)}) collective-permute-start(bf16[256,768]{1,0:T(8,128)(2,1)S(1)} %get-tuple-element.347.refs_1_), channel_id=1, source_target_pairs={{0,2},{2,0},{1,3},{3,1},{4,6},{6,4},{5,7},{7,5},{8,10},{10,8},{9,1... | collective-permute-start | bytes 1179656 | tf_op jit(solution)/shard_map/ppermute | solution.py:29
  338.8 24.0 %collective-permute-start.52 = (bf16[384,768]{1,0:T(8,128)(2,1)S(1)}, bf16[384,768]{1,0:T(8,128)(2,1)S(1)}, u32[]{:S(2)}, u32[]{:S(2)}) collective-permute-start(bf16[384,768]{1,0:T(8,128)(2,1)S(1)} %get-tuple-element.465.refs_20_), channel_id=1, source_target_pairs={{0,8},{4,12},{8,0},{12,4},{16,24},{20,28},{24,16},{28,20},{1,9},{5... | collective-permute-start | bytes 1769480 | tf_op jit(solution)/shard_map/ppermute | solution.py:581
  375.3 57.5 %collective-permute-start.80 = (bf16[4,96,768]{2,1,0:T(8,128)(2,1)}, bf16[4,96,768]{2,1,0:T(8,128)(2,1)}, u32[]{:S(2)}, u32[]{:S(2)}) collective-permute-start(bf16[4,96,768]{2,1,0:T(8,128)(2,1)} %pad_maximum_fusion.10.refs_17_), channel_id=1, source_target_pairs={{0,8},{4,12},{8,0},{12,4},{16,24},{20,28},{24,16},{28,20},{1,9},{5... | collective-permute-start | bytes 1769480 | tf_op jit(solution)/shard_map/ppermute | solution.py:589
  378.4 35.7 %collective-permute-start.85 = (bf16[96,768]{1,0:T(8,128)(2,1)S(1)}, bf16[96,768]{1,0:T(8,128)(2,1)S(1)}, u32[]{:S(2)}, u32[]{:S(2)}) collective-permute-start(bf16[96,768]{1,0:T(8,128)(2,1)S(1)} %fusion.30.refs_19_), channel_id=1, source_target_pairs={{0,16},{4,20},{8,24},{12,28},{16,0},{20,4},{24,8},{28,12},{1,17},{... | collective-permute-start | bytes 442376 | tf_op jit(solution)/shard_map/ppermute | solution.py:581
  378.7 35.3 %collective-permute-start.81 = (bf16[96,768]{1,0:T(8,128)(2,1)S(1)}, bf16[96,768]{1,0:T(8,128)(2,1)S(1)}, u32[]{:S(2)}, u32[]{:S(2)}) collective-permute-start(bf16[96,768]{1,0:T(8,128)(2,1)S(1)} %fusion.29.refs_18_), channel_id=1, source_target_pairs={{0,16},{4,20},{8,24},{12,28},{16,0},{20,4},{24,8},{28,12},{1,17},{... | collective-permute-start | bytes 442376 | tf_op jit(solution)/shard_map/ppermute | solution.py:581
  431.1 46.4 %collective-permute-start.83 = (bf16[2,96,768]{2,1,0:T(8,128)(2,1)}, bf16[2,96,768]{2,1,0:T(8,128)(2,1)}, u32[]{:S(2)}, u32[]{:S(2)}) collective-permute-start(bf16[2,96,768]{2,1,0:T(8,128)(2,1)} %pad_maximum_fusion.19), channel_id=1, source_target_pairs={{0,8},{4,12},{8,0},{12,4},{16,24},{20,28},{24,16},{28,20},{1,9},{5... | collective-permute-start | bytes 884744 | tf_op jit(solution)/shard_map/ppermute | solution.py:589
  432.8 47.2 %collective-permute-start.87 = (bf16[2,96,768]{2,1,0:T(8,128)(2,1)}, bf16[2,96,768]{2,1,0:T(8,128)(2,1)}, u32[]{:S(2)}, u32[]{:S(2)}) collective-permute-start(bf16[2,96,768]{2,1,0:T(8,128)(2,1)} %pad_maximum_fusion.20), channel_id=1, source_target_pairs={{0,4},{4,0},{8,12},{12,8},{16,20},{20,16},{24,28},{28,24},{1,5},{5... | collective-permute-start | bytes 884744 | tf_op jit(solution)/shard_map/ppermute | solution.py:589
  470.1 31.7 %collective-permute-start.67 = (bf16[576,768]{1,0:T(8,128)(2,1)}, bf16[576,768]{1,0:T(8,128)(2,1)}, u32[]{:S(2)}, u32[]{:S(2)}) collective-permute-start(bf16[576,768]{1,0:T(8,128)(2,1)} %shard_map.385), channel_id=1, source_target_pairs={{0,1},{1,0},{2,3},{3,2},{4,5},{5,4},{6,7},{7,6},{8,9},{9,8},{10,11... | collective-permute-start | bytes 2654216 | tf_op jit(solution)/shard_map/ppermute | solution.py:25
  537.2 24.2 %collective-permute-start.73 = (bf16[4,48,768]{2,1,0:T(8,128)(2,1)S(1)}, bf16[4,48,768]{2,1,0:T(8,128)(2,1)S(1)}, u32[]{:S(2)}, u32[]{:S(2)}) collective-permute-start(bf16[4,48,768]{2,1,0:T(8,128)(2,1)S(1)} %pad_maximum_fusion.17), channel_id=1, source_target_pairs={{0,4},{4,0},{8,12},{12,8},{16,20},{20,16},{24,28},{28,24},{1,5},{5... | collective-permute-start | bytes 884744 | tf_op jit(solution)/shard_map/ppermute | solution.py:589
  539.0 22.4 %collective-permute-start.79 = (bf16[4,48,768]{2,1,0:T(8,128)(2,1)S(1)}, bf16[4,48,768]{2,1,0:T(8,128)(2,1)S(1)}, u32[]{:S(2)}, u32[]{:S(2)}) collective-permute-start(bf16[4,48,768]{2,1,0:T(8,128)(2,1)S(1)} %pad_maximum_fusion.18), channel_id=1, source_target_pairs={{0,8},{4,12},{8,0},{12,4},{16,24},{20,28},{24,16},{28,20},{1,9},{5... | collective-permute-start | bytes 884744 | tf_op jit(solution)/shard_map/ppermute | solution.py:589
  (328 other events, 2274.9 us)
Sparse Core Ops, SparseCore 0:
  262.9 149.5 all-reduce.2

commit v3 on v2

--- a/solution.py
+++ b/solution.py
@@ -73,7 +73,7 @@
     return pl.BlockSpec(shape, lambda *ids: zeros)
 
 
-def call(kernel, grid, inputs, outputs, scratch=(), cost=1, limit=16, after=()):
+def call(kernel, grid, inputs, outputs, scratch=(), cost=0, limit=16, after=()):
     arrays = [array for array, spec in inputs]
     specs = [spec for array, spec in inputs]
     aliases = {}
@@ -368,14 +368,10 @@
     up_other_ref,
     down_own_ref,
     down_other_ref,
-    encoded_ref,
-    total_ref,
-    low_ref,
-    grad_ref,
-    bias_ref,
-    sums_ref,
-    part_ref,
+    *rest,
 ):
+    before = rest[:-7]
+    encoded_ref, total_ref, low_ref, grad_ref, bias_ref, sums_ref, part_ref = rest[-7:]
     keep_span = slice(place * CHUNK, (place + 1) * CHUNK)
     added = share_ref[...].astype(F32) + recv_ref[...].astype(F32)
     if top_layer:
@@ -389,10 +385,10 @@
         upstream = up_ref[...] + added
         encoded_ref[...] = jnp.zeros_like(encoded_ref)
     second = norm_back(upstream, unit, inverse, vec_ref[layer, 4:5, :])
-    sums_ref[...] = jnp.zeros_like(sums_ref)
-    sums_ref[0:1, :] = jnp.sum(upstream * unit, 0, keepdims=True)
-    sums_ref[1:2, :] = jnp.sum(upstream, 0, keepdims=True)
-    sums_ref[2:3, :] = jnp.sum(second, 0, keepdims=True)
+    sums_ref[...] = before[0][...] if before else jnp.zeros_like(sums_ref)
+    sums_ref[0:1, :] += jnp.sum(upstream * unit, 0, keepdims=True)
+    sums_ref[1:2, :] += jnp.sum(upstream, 0, keepdims=True)
+    sums_ref[2:3, :] += jnp.sum(second, 0, keepdims=True)
     total_ref[...] = second
     low_ref[...] = second.astype(BF16)
     units = up_own_ref.shape[2]
@@ -405,7 +401,8 @@
             dot(low_ref[...], down_ref[layer], 1, 1) * slope_ref[:, lanes].astype(F32)
         ).astype(BF16)
         grad_ref[:, lanes] = grad
-        bias_ref[:, lanes] = jnp.sum(grad.astype(F32), 0, keepdims=True)
+        bias = jnp.sum(grad.astype(F32), 0, keepdims=True)
+        bias_ref[:, lanes] = bias + before[1][:, lanes] if before else bias
         part = dot(grad, up_weight_ref[layer], 1, 1)
         total = part if total is None else total + part
     part_ref[...] = total.astype(BF16)
@@ -421,35 +418,40 @@
     inverse_ref,
     vec_ref,
     out_weight_ref,
-    total_ref,
-    low_ref,
-    grad_ref,
-    sums_ref,
+    *rest,
 ):
+    before = rest[:-4]
+    total_ref, low_ref, grad_ref, sums_ref = rest[-4:]
     added = share_ref[...].astype(F32) + recv_ref[...].astype(F32)
     upstream = second_ref[...] + added
     unit = unit_ref[...]
     first = norm_back(upstream, unit, inverse_ref[...], vec_ref[layer, 1:2, :])
-    sums_ref[...] = jnp.zeros_like(sums_ref)
-    sums_ref[0:1, :] = jnp.sum(upstream * unit, 0, keepdims=True)
-    sums_ref[1:2, :] = jnp.sum(upstream, 0, keepdims=True)
-    sums_ref[2:3, :] = jnp.sum(first, 0, keepdims=True)
+    sums_ref[...] = before[0][...] if before else jnp.zeros_like(sums_ref)
+    sums_ref[0:1, :] += jnp.sum(upstream * unit, 0, keepdims=True)
+    sums_ref[1:2, :] += jnp.sum(upstream, 0, keepdims=True)
+    sums_ref[2:3, :] += jnp.sum(first, 0, keepdims=True)
     total_ref[...] = first
     low = first.astype(BF16)
     low_ref[...] = low
     grad_ref[...] = dot(low, out_weight_ref[layer], 1, 1).astype(BF16)
 
 
-def joint_back_kernel(layer, place, core_ref, *refs):
+def joint_back_kernel(
+    layer,
+    place,
+    core_ref,
+    *refs,
+):
     pairs = (len(refs) - 6) // 3
     q_refs, own_refs, recv_refs = (refs[k * pairs : (k + 1) * pairs] for k in range(3))
     q_weight_ref, kv_weight_ref, mine_ref, theirs_ref, bias_ref, part_ref = refs[3 * pairs :]
+    span = slice(place * CHUNK, (place + 1) * CHUNK)
     width = 128 * pairs
     local = width // 2
-    keep_span = slice(place * CHUNK, (place + 1) * CHUNK)
-    q_grad = jnp.concatenate([ref[keep_span, :] for ref in q_refs], 1)
+    q_grad = jnp.concatenate([ref[span, :] for ref in q_refs], 1)
     both = [
-        (own[place] + recv[place].astype(F32)).astype(BF16) for own, recv in zip(own_refs, recv_refs)
+        (own[place] + recv[place].astype(F32)).astype(BF16)
+        for own, recv in zip(own_refs, recv_refs)
     ]
     kv_grad = jnp.concatenate(
         [part[:, :128] for part in both] + [part[:, 128:] for part in both], 1
@@ -507,94 +509,238 @@
         unit_bias_ref[layer, :, units:] = other[:, width:]
 
 
-def widen_kernel(source_ref, target_ref):
-    target_ref[0] = source_ref[...].astype(F32)
-
-
-def unpack_rows_kernel(place_ref, *refs):
-    count = 1 if len(refs) == 2 else 4
-    sources, targets = refs[:-count], refs[-count:]
-    rows = targets[0].shape[1]
+def halve_kernel(bit, numbers_ref, *refs):
+    parts, (sent_ref, kept_ref) = refs[:-2], refs[-2:]
+    half = sent_ref.shape[0]
+    for target, number in ((sent_ref, 1 - numbers_ref[bit]), (kept_ref, numbers_ref[bit])):
+        rows = pl.ds(pl.multiple_of(number * half, half), half)
+        target[...] = sum(part[rows, :].astype(F32) for part in parts).astype(target.dtype)
+
+
+def add_kernel(kept_ref, recv_ref, piece_ref):
+    piece_ref[0] = (kept_ref[...] + recv_ref[...].astype(F32)).astype(BF16)
+
+
+def join_kernel(pieces_ref, recv_ref, joined_ref):
+    count = pieces_ref.shape[0]
+    joined_ref[:count] = pieces_ref[...]
+    joined_ref[count:] = recv_ref[...]
+
+
+def arrange(place, pieces_ref, recv_ref, full):
+    count, rows = pieces_ref.shape[0], pieces_ref.shape[1]
+    for number in range(2 * count):
+        source = pieces_ref[number] if number < count else recv_ref[number - count]
+        start = pl.multiple_of((number ^ place) * rows, rows)
+        full[pl.ds(start, rows), :] = source.astype(F32)
+
+
+def unpack_kernel(place, numbers_ref, pieces_ref, recv_ref, *refs):
+    targets, full = refs[:-1], refs[-1]
+    arrange(numbers_ref[place], pieces_ref, recv_ref, full)
     start = 0
-    for number, source in enumerate(sources):
-        pieces, size = source.shape[0], source.shape[1]
-        for piece in range(pieces):
-            target, row = targets[start // rows], start % rows
-            target[0, row : row + size, :] = source[piece ^ place_ref[number]].astype(F32)
-            start += size
+    for target in targets:
+        rows = target.shape[-2]
+        value = full[start : start + rows, :]
+        if len(target.shape) == 3:
+            target[0] = value
+        else:
+            target[...] = value.astype(target.dtype)
+        start += rows
+
+
+def vectors_unpack_kernel(place, numbers_ref, pieces_ref, recv_ref, *refs):
+    q_ref, table_ref, targets, full = refs[0], refs[1], refs[2:-1], refs[-1]
+    arrange(numbers_ref[place], pieces_ref, recv_ref, full)
+    local = q_ref.shape[1]
+    half = table_ref.shape[0]
+    q_ref[0] = full[:local, :]
+    table_ref[...] = full[local : local + half, :].astype(BF16)
+    for layer in range(LAYERS):
+        start = local + half + 8 * layer
+        row = slice(layer, layer + 1)
+        for member in range(7):
+            targets[member][row, :] = full[start + member : start + member + 1, :]
+        last = full[start + 7 : start + 8, :]
+        for member in range(2):
+            targets[7 + member][row, :] = last[:, member * local : (member + 1) * local]
+
+
+def table_kernel(chunks, share, numbers_ref, bucket_ref, *refs):
+    joints, firsts = refs[:chunks], refs[chunks : 2 * chunks]
+    vectors = refs[2 * chunks : -3]
+    mine_ref, sent_ref, full = refs[-3:]
+    buckets, half = full.shape[0], full.shape[0] // 2
+    chip, core = numbers_ref[1], numbers_ref[0]
+    numbers = lax.broadcasted_iota(jnp.int32, (buckets, CHUNK), 0)
+    places = lax.broadcasted_iota(jnp.int32, (buckets, CHUNK), 1)
+    total = None
+    for place in range(chunks):
+        hit = numbers == bucket_ref[place]
+        rows = places + place * CHUNK
+        mine = jnp.logical_and(rows >= chip * share, rows < (chip + 1) * share)
+        every = jnp.where(hit, 1.0, 0.0).astype(BF16)
+        own = jnp.where(jnp.logical_and(hit, mine), 1.0, 0.0).astype(BF16)
+        first = firsts[place][...]
+        high = first.astype(BF16)
+        rest = (first - high.astype(F32)).astype(BF16)
+        part = dot(every, joints[place][...]) + (dot(own, high) + dot(own, rest))
+        total = part if total is None else total + part
+    full[...] = total
+    mine_ref[:half, :] = full[pl.ds(pl.multiple_of(core * half, half), half), :]
+    sent_ref[:half, :] = full[pl.ds(pl.multiple_of((1 - core) * half, half), half), :].astype(BF16)
+    for layer in range(LAYERS):
+        rows = slice(half + 8 * layer, half + 8 * layer + 8)
+        mine_ref[rows, :] = vectors[2 * layer][...]
+        sent_ref[rows, :] = vectors[2 * layer + 1][...].astype(BF16)
+
+
+def vectors_kernel(numbers_ref, second_ref, first_ref, unit_ref, *refs):
+    mine_ref, sent_ref = refs[-2:]
+    second, first, unit = second_ref[...], first_ref[...], unit_ref[...]
+    bias = sum(ref[...] for ref in refs[:-2])
+    units, local = unit.shape[1] // 2, bias.shape[1] // 2
+    low = numbers_ref[0] == 0
+    for target, lanes, flip in (
+        (mine_ref, slice(0, units), False),
+        (sent_ref, slice(units, 2 * units), True),
+    ):
+        target[0:3, :] = second[0:3, :]
+        target[3:6, :] = first[0:3, :]
+        target[6:7, :] = unit[:, lanes]
+        target[7:8, :] = jnp.zeros_like(target[7:8, :])
+        for member in range(2):
+            left, right = bias[member : member + 1, :local], bias[member : member + 1, local:]
+            if flip:
+                left, right = right, left
+            target[7:8, member * local : (member + 1) * local] = jnp.where(low, left, right)
+
+
+def table_add_kernel(mine_ref, recv_ref, both_ref, sent_ref):
+    total = mine_ref[...] + recv_ref[...].astype(F32)
+    both_ref[...] = total
+    sent_ref[...] = total[: sent_ref.shape[0], :].astype(BF16)
+
+
+def pack_kernel(q_ref, both_ref, sent_ref, recv_ref, packed_ref):
+    local, half, rows = q_ref.shape[0], sent_ref.shape[0], both_ref.shape[0]
+    packed_ref[...] = jnp.zeros_like(packed_ref)
+    packed_ref[:local, :] = q_ref[...]
+    table = sent_ref[...].astype(F32) + recv_ref[...].astype(F32)
+    packed_ref[local : local + half, :] = table.astype(BF16)
+    packed_ref[local + half : local + rows, :] = both_ref[half:, :].astype(BF16)
+
+
+def pile_kernel(*refs):
+    sources, target = refs[:-1], refs[-1]
+    start = 0
+    for source in sources:
+        rows = source.shape[0]
+        target[start : start + rows, :] = source[...].astype(target.dtype)
+        start += rows
+    if start < target.shape[0]:
+        target[start:, :] = jnp.zeros_like(target[start:, :])
+
+
+def pick_rows(chip, chunk_refs, share, target):
+    for number in range(2):
+
+        @pl.when(chip == number)
+        def _():
+            start, end = number * share, (number + 1) * share
+            for place, ref in enumerate(chunk_refs):
+                low, high = max(start, place * CHUNK), min(end, (place + 1) * CHUNK)
+                if low < high:
+                    target[low - start : high - start, :] = ref[
+                        low - place * CHUNK : high - place * CHUNK, :
+                    ]
+
+
+def tokens_send_kernel(numbers_ref, *refs):
+    pick_rows(1 - numbers_ref[1], refs[:-1], refs[-1].shape[0], refs[-1])
+
+
+def tokens_kernel(chunks, numbers_ref, *refs):
+    joints, firsts = refs[:chunks], refs[chunks : 2 * chunks]
+    recv_ref, target, own = refs[2 * chunks :]
+    share = target.shape[0]
+    pick_rows(numbers_ref[1], joints, share, own)
+    pick_rows(numbers_ref[1], firsts, share, target)
+    target[...] += own[...].astype(F32) + recv_ref[...].astype(F32)
 
 
 class Wide:
-    def __init__(self, size):
-        self.small = size == 8
+    BITS = {"y": (2, 1), "near": (3, 2), "far": (4, 4)}
+    PLACES = {("y", "near", "far"): 5, ("near", "y", "far"): 6}
+
+    def __init__(self, size, chip, core):
+        self.small, self.size = size == 8, size
         index = lax.axis_index("wide")
-        self.bits = {}
-        if self.small:
-            for name, reach in (("y", 1), ("near", 2), ("far", 4)):
-                self.bits[name] = (
-                    (index // reach) % 2,
-                    [(number, number ^ reach) for number in range(size)],
-                )
-
-    def place(self, order):
-        if not self.small:
-            return jnp.int32(0)
-        first, second, third = (self.bits[name][0] for name in order)
-        return (first * 4 + second * 2 + third).astype(jnp.int32)
-
-    def chain(self, value, order):
-        return Chain(self, value, order)
-
-    def exchanged(self, value):
-        if not self.small:
-            return lax.psum(value, "wide")
-        for name in ("y", "near", "far"):
-            low = value.astype(BF16)
-            value = low.astype(F32) + lax.ppermute(low, "wide", self.bits[name][1]).astype(F32)
-        return value
+        bits = {name: (index >> k) & 1 for k, name in enumerate(("y", "near", "far"))}
+        places = [
+            sum(bits[name] << (2 - k) for k, name in enumerate(order)) if self.small else 0
+            for order in self.PLACES
+        ]
+        self.numbers = jnp.stack(
+            [
+                jnp.asarray(value, jnp.int32)
+                for value in (core, chip, bits["y"], bits["near"], bits["far"], *places, 0)
+            ]
+        )
+
+    def pairs(self, name):
+        reach = self.BITS[name][1]
+        return [(number, number ^ reach) for number in range(self.size)]
 
 
 def gate(value, *later):
     return lax.optimization_barrier((value,) + later)[0] if later else value
+
+
+SMEM = pl.BlockSpec(memory_space=pltpu.SMEM)
 
 
 class Chain:
     def __init__(self, wide, value, order):
         self.wide, self.order, self.step = wide, order, 0
-        self.addends, self.pieces = [value], None
-
-    def advance(self, *later):
+        self.parts, self.rows = [value], value.shape[0]
+
+    def advance(self, *after):
         if not self.wide.small:
-            if self.pieces is None:
-                value = self.addends[0]
-                self.pieces = lax.psum(value, "wide").reshape(8, -1, value.shape[1])
-            return self.pieces
+            if self.step == 0:
+                value = self.parts[0]
+                self.parts = lax.psum(value, "wide").reshape(2, 4, -1, value.shape[1])
+            self.step = 6
+            self.sent = self.parts[0]
+            return self.parts[0]
         self.step += 1
+        parts = [(part, ON_CHIP) for part in self.parts]
+        columns = self.parts[0].shape[-1]
         if self.step <= 3:
-            bit, pairs = self.wide.bits[self.order[self.step - 1]]
-            parts = self.addends[:-1] + [gate(self.addends[-1], *later)]
-            split = [part.reshape(2, part.shape[0] // 2, part.shape[1]) for part in parts]
-            sent = sum(
-                lax.dynamic_index_in_dim(part, 1 - bit, 0, False).astype(F32) for part in split
-            ).astype(BF16)
-            mine = [lax.dynamic_index_in_dim(part, bit, 0, False) for part in split]
-            self.addends = mine + [lax.ppermute(sent, "wide", pairs)]
+            name = self.order[self.step - 1]
+            half = (self.parts[0].shape[0] // 2, columns)
+            sent, kept = call(
+                functools.partial(halve_kernel, Wide.BITS[name][0]),
+                None,
+                [(self.wide.numbers, SMEM)] + parts,
+                [(half, BF16, ON_CHIP, None), (half, F32, ON_CHIP, None)],
+                after=after,
+            )
+            self.parts = [kept, lax.ppermute(sent, "wide", self.wide.pairs(name))]
+            self.sent = sent
             return sent
-        if self.step == 4:
-            parts = self.addends[:-1] + [gate(self.addends[-1], *later)]
-            sent = sum(part.astype(F32) for part in parts).astype(BF16)[None]
-        else:
-            sent = jnp.concatenate([self.pieces, gate(self.received, *later)], 0)
-        self.pieces = sent
-        self.received = lax.ppermute(sent, "wide", self.wide.bits[self.order[6 - self.step]][1])
+        kernel = add_kernel if self.step == 4 else join_kernel
+        shape = self.parts[0].shape
+        shape = (1,) + shape if self.step == 4 else (2 * shape[0],) + shape[1:]
+        (sent,) = call(kernel, None, parts, [(shape, BF16, ON_CHIP, None)], after=after)
+        name = self.order[6 - self.step]
+        self.parts = [sent, lax.ppermute(sent, "wide", self.wide.pairs(name))]
         return sent
 
-    def finish(self, *later):
-        while self.step < 6 and self.wide.small:
+    def finish(self):
+        while self.step < 6:
             self.advance()
-        if not self.wide.small:
-            return self.advance()
-        return jnp.concatenate([self.pieces, gate(self.received, *later)], 0)
+        return [self.parts[0], self.parts[1]]
 
 
 def on_device(wide, *arguments):
@@ -654,7 +800,8 @@
     lane_cotangent = by_chip(cotangent, over_chip(cotangent))
 
     smem = pl.BlockSpec(memory_space=pltpu.SMEM)
-    core_number = core.astype(jnp.int32).reshape(1)
+    sums = Wide(wide, chip, core)
+    core_number = sums.numbers
     shards = []
     turned_weights = [
         jnp.swapaxes(weight, 1, 2) for weight in (query_weight, key_weight, value_weight)
@@ -867,29 +1014,41 @@
         )
         kept.append(keep)
 
-    sums = Wide(wide)
     pair_order, other_order = ("y", "near", "far"), ("near", "y", "far")
 
-    def halves(full, axis):
-        left, right = jnp.split(full, 2, axis)
-        return jnp.where(first_core, left, right), jnp.where(first_core, right, left)
-
-    def unpacked(kernel, layer, places, sources, shapes, buffers, scratch=()):
+    def unpacked(kernel, layer, sources, shapes, buffers, scratch=(), after=()):
         return call(
             kernel,
             (1,),
-            ([] if places is None else [(jnp.stack(places), smem)])
-            + [(source, whole(source.shape)) for source in sources],
+            [(source, smem if source is sums.numbers else whole(source.shape)) for source in sources],
             [
                 ((LAYERS,) + shape, F32, layer_spec(layer, shape), buffer)
                 for shape, buffer in zip(shapes, buffers)
             ],
             scratch,
+            after=after,
         )
 
-    turned_out = [None] * 4
-    shared = [None] * LAYERS
-    split_vectors = [None] * LAYERS
+    def unpacked_rows(layer, chain, shapes, buffers, after=()):
+        return unpacked(
+            functools.partial(unpack_kernel, Wide.PLACES[chain.order]),
+            layer,
+            [sums.numbers] + chain.finish(),
+            shapes,
+            buffers,
+            [pltpu.VMEM((chain.rows, model), F32)],
+            after,
+        )
+
+    def piled(rows, *values):
+        return call(
+            pile_kernel,
+            None,
+            [(value, ON_CHIP) for value in values],
+            [((rows, model), BF16, ON_CHIP, None)],
+        )[0]
+
+    vector_sums = [None] * LAYERS
     encoded = []
     for layer in reversed(range(LAYERS)):
         keep = kept[layer]
@@ -923,6 +1082,8 @@
                         up_other,
                         down_weight,
                         down_other,
+                        *second_sums[-1:],
+                        *unit_sums[-1:],
                     )
                 ],
                 [
@@ -934,8 +1095,14 @@
                     ((8, model), F32, ON_CHIP, None),
                     (block, BF16, ON_CHIP, None),
                 ],
-                cost=8,
-                after=[upper.advance(*second_sums[1:2])] if i != 1 and not top_layer else [],
+                cost=0,
+                after=(
+                    []
+                    if top_layer or i == 1
+                    else [upper.advance(), feed_chain.advance(joint_share[2]), vector_sums[1][0]]
+                    if i == 0
+                    else []
+                ),
             )
             if top_layer:
                 encoded.append(outs[0])
@@ -951,7 +1118,7 @@
                 None,
                 [(value, ON_CHIP) for value in [*lefts, *rights, *received]],
                 [(shape, BF16, ON_CHIP, None)],
-                cost=2,
+                cost=0,
             )[0]
 
         square = (model, units)
@@ -982,6 +1149,7 @@
                         keep["first_inverse"][i],
                         vec,
                         ow,
+                        *first_sums[-1:],
                     )
                 ],
                 [
@@ -990,7 +1158,11 @@
                     ((CHUNK, width), BF16, ON_CHIP, None),
                     ((8, model), F32, ON_CHIP, None),
                 ],
-                after=[upper.advance(second_sums[2])] if i == 1 and not top_layer else [],
+                after=(
+                    []
+                    if top_layer or i != 1
+                    else [upper.advance(second_sums[2]), feed_chain.advance(second_sums[2])]
+                ),
             )
             for target, value in zip((first_total, low_total, context_grad, first_sums), outs):
                 target.append(value)
@@ -1005,14 +1177,18 @@
         out_grad = (own + over_core(other).astype(F32)).astype(BF16)
         pending = [out_grad, up_weight_grad, down_grad]
         if top_layer:
-            feed_sums = lax.psum((up_weight_grad, down_grad), "wide")
+            feed_chain = Chain(sums, piled(2 * units, up_weight_grad, down_grad), pair_order)
+            pending = [out_grad, feed_chain.advance()]
         else:
             strands = [
-                sums.chain(up_weight_grad, pair_order),
-                sums.chain(down_grad, other_order),
+                Chain(sums, up_weight_grad, pair_order),
+                Chain(sums, down_grad, other_order),
             ]
-            pending = [out_grad, upper.advance(first_sums[2])] + [
-                strand.advance() for strand in strands
+            pending = [
+                out_grad,
+                upper.advance(first_sums[2]),
+                feed_chain.advance(first_sums[2]),
+                *[strand.advance() for strand in strands],
             ]
         half_shape = (chunks, CHUNK, 256)
         q_grads, kv_owns, kv_recvs = [], [], []
@@ -1041,18 +1217,27 @@
                     pltpu.VMEM((128, CHUNK), F32),
                     pltpu.VMEM((tiles, CHUNK, 256), F32),
                 ],
-                cost=10,
+                cost=0,
                 limit=16,
                 after=pending + q_grads[-1:],
             )
             pending = []
             if not top_layer:
-                if pair < 2:
-                    pending = [upper.advance(q_grad)]
-                pending += [strand.advance(q_grad) for strand in strands]
+                pending = [upper.advance(q_grad)]
+                if pair == 0:
+                    pending.append(feed_chain.advance(q_grad))
+                if pair == 2:
+                    up_out, down_out = unpacked_rows(
+                        1, feed_chain, [square, square[::-1]], [None] * 2, after=[q_grad]
+                    )
+                    pending.append(up_out)
+                if pair > 0:
+                    pending += [strand.advance(q_grad) for strand in strands]
+            elif pair == 2:
+                pending = [feed_chain.advance(q_grad)]
             q_grads.append(q_grad)
             kv_owns.append(kv_grad)
-            kv_recvs.append(over_core(kv_grad_other))
+            kv_recvs.append(over_core(gate(kv_grad_other, *pending)))
         joint_own, joint_other, bias_sums, joint_share = [], [], [], []
         for i in range(chunks):
             outs = call(
@@ -1066,118 +1251,142 @@
                     ((8, width), F32, ON_CHIP, None),
                     (block, BF16, ON_CHIP, None),
                 ],
-                cost=2,
+                cost=0,
             )
             for target, value in zip((joint_own, joint_other, bias_sums, joint_share), outs):
                 target.append(value)
+        vector_sums[layer] = call(
+            vectors_kernel,
+            None,
+            [(sums.numbers, smem)]
+            + [(value, ON_CHIP) for value in second_sums[-1:] + first_sums[-1:] + unit_sums[-1:] + bias_sums],
+            [((8, model), F32, ON_CHIP, None), ((8, model), F32, ON_CHIP, None)],
+        )
         if layer > 0:
             joint_recv = [over_chip(part) for part in joint_share]
-        joint_recv_grad = over_core(weight_grad(joint_other, keep["low_in"], (3 * local, model)))
+        joint_other_grad = weight_grad(joint_other, keep["low_in"], (3 * local, model))
+        if layer == 0:
+            buckets_total = type_table.shape[0]
+            half_table = buckets_total // 2
+            table_mine, table_sent = call(
+                functools.partial(table_kernel, chunks, share),
+                None,
+                [
+                    (value, smem if value is sums.numbers else ON_CHIP)
+                    for value in [sums.numbers, lane_buckets.reshape(chunks, 1, CHUNK)]
+                    + joint_share
+                    + first_total
+                    + [*vector_sums[0], *vector_sums[1]]
+                ],
+                [
+                    ((half_table + 16, model), F32, ON_CHIP, None),
+                    ((half_table + 16, model), BF16, ON_CHIP, None),
+                ],
+                scratch=[pltpu.VMEM((buckets_total, model), F32)],
+                cost=0,
+                after=[joint_other_grad],
+            )
+            table_recv = over_core(table_sent)
+        joint_recv_grad = over_core(joint_other_grad)
+        if layer == 0:
+            table_both, table_low = call(
+                table_add_kernel,
+                None,
+                [(table_mine, ON_CHIP), (table_recv, ON_CHIP)],
+                [
+                    ((half_table + 16, model), F32, ON_CHIP, None),
+                    ((half_table, model), BF16, ON_CHIP, None),
+                ],
+            )
         joint_grad = weight_grad(
             joint_own, keep["low_in"], (3 * local, model), received=[joint_recv_grad]
         )
         flat = [(local, model)] * 4
         if layer > 0:
-            upper = sums.chain(jnp.concatenate([joint_grad, out_grad], 0), other_order)
-        else:
-            (up_out,) = unpacked(
-                widen_kernel, 1, None, [gate(feed_sums[0], joint_share[-1])], [square], [None]
+            upper = Chain(sums, piled(4 * local, joint_grad, out_grad), other_order)
+
+    second_chain = Chain(
+        sums, piled(10 * half_table // 2, joint_grad[local:], out_grad), other_order
+    )
+    second_sent = second_chain.advance()
+    table_other = over_chip(table_low)
+    (tokens_sent,) = call(
+        tokens_send_kernel,
+        None,
+        [(sums.numbers, smem)] + [(part, ON_CHIP) for part in joint_share],
+        [((share, model), BF16, ON_CHIP, None)],
+        after=[table_low],
+    )
+    tokens_recv = over_chip(tokens_sent)
+    (packed,) = call(
+        pack_kernel,
+        None,
+        [(value, ON_CHIP) for value in (joint_grad[:local], table_both, table_low, table_other)],
+        [((3 * half_table, model), BF16, ON_CHIP, None)],
+    )
+    first_chain = Chain(sums, packed, pair_order)
+    token = first_chain.advance()
+    for step in range(5):
+        for strand in strands:
+            if strand.step < 6:
+                token = strand.advance(token)
+        token = second_chain.advance(token)
+        if upper.step < 6:
+            token = upper.advance(token)
+        token = first_chain.advance(token)
+        if step == 0:
+            turned_out = unpacked_rows(1, upper, flat, [None] * 4, after=[token])
+            token = strands[0].advance(turned_out[0])
+        if step == 3:
+            (tokens_grad,) = call(
+                functools.partial(tokens_kernel, chunks),
+                (1,),
+                [(sums.numbers, smem)]
+                + [
+                    (value, whole(value.shape))
+                    for value in joint_share + first_total + [tokens_recv]
+                ],
+                [((share, model), F32, whole((share, model)), None)],
+                scratch=[pltpu.VMEM((share, model), BF16)],
+                after=[token],
             )
-            (down_out,) = unpacked(
-                widen_kernel, 1, None, [gate(feed_sums[1], joint_share[-1])], [square[::-1]], [None]
-            )
-            turned_out = unpacked(
-                unpack_rows_kernel, 1, [sums.place(other_order)], [upper.finish()], flat, turned_out
-            )
-            first_chain = sums.chain(joint_grad[: 2 * local], pair_order)
-            second_chain = sums.chain(
-                jnp.concatenate([joint_grad[2 * local :], out_grad], 0), other_order
-            )
-            turned_out = unpacked(
-                unpack_rows_kernel,
-                layer,
-                [sums.place(pair_order), sums.place(other_order)],
-                [first_chain.finish(), second_chain.finish()],
-                flat,
-                turned_out,
-            )
-            (up_out,) = unpacked(
-                unpack_rows_kernel,
-                layer,
-                [sums.place(pair_order)],
-                [strands[0].finish()],
-                [square],
-                [up_out],
-            )
-            (down_out,) = unpacked(
-                unpack_rows_kernel,
-                layer,
-                [sums.place(other_order)],
-                [strands[1].finish()],
-                [square[::-1]],
-                [down_out],
-            )
-        second_sum, first_sum = sum(second_sums), sum(first_sums)
-        shared[layer] = jnp.concatenate([second_sum[:3], first_sum[:3]], 0)
-        unit_sum, bias_sum = sum(unit_sums), sum(bias_sums)
-        q_own, q_other = halves(bias_sum[0], 0)
-        v_own, v_other = halves(bias_sum[1], 0)
-        split_vectors[layer] = (
-            jnp.concatenate([q_own, v_own, unit_sum[0, :units]]),
-            jnp.concatenate([q_other, v_other, unit_sum[0, units:]]),
-        )
-
-    joint_rows = jnp.concatenate(joint_share, 0)
-    first_rows = own_rows(jnp.concatenate(first_total, 0))
-    joint_theirs = over_chip(other_rows(joint_rows)).astype(F32)
-    tokens_grad = first_rows + (own_rows(joint_rows).astype(F32) + joint_theirs)
-    own_selector = (buckets[:, None] == lax.iota(jnp.int32, type_table.shape[0])[None, :]).astype(
-        BF16
-    )
-    high = first_rows.astype(BF16)
-    rest = (first_rows - high.astype(F32)).astype(BF16)
-    table = (
-        dot(own_selector, high, 0, 0) + dot(own_selector, rest, 0, 0)
-    ) + dot(selector, joint_rows, 0, 0)
-
-    common = jnp.concatenate(shared, 0)
-    mine = jnp.stack([value[0] for value in split_vectors])
-    theirs = jnp.stack([value[1] for value in split_vectors])
-    vectors = jnp.concatenate([common.reshape(-1), mine.reshape(-1)])
-    sent = jnp.concatenate([common.reshape(-1), theirs.reshape(-1)])
-    vectors = (vectors + over_core(sent)).reshape(-1, model)
-
-    table_own, table_other = halves(table, 0)
-    table_half = table_own + over_core(table_other.astype(BF16)).astype(F32)
-    low_half = table_half.astype(BF16)
-    table_half = low_half.astype(F32) + over_chip(low_half).astype(F32)
-    packed = sums.exchanged(jnp.concatenate([table_half, vectors], 0))
-    table_half = packed[: table_half.shape[0]]
-    vectors = packed[table_half.shape[0] :].reshape(-1)
-    low_half = table_half.astype(BF16)
-    table_grad = by_core(low_half, over_core(low_half), 0).astype(F32)
-    common = vectors[: common.size].reshape(LAYERS, 6, model)
-    mine = vectors[common.size :].reshape(LAYERS, -1)
+        if step == 4:
+            (up_out,) = unpacked_rows(0, strands[0], [square], [up_out], after=[token])
+            (down_out,) = unpacked_rows(0, strands[1], [square[::-1]], [down_out])
+    k_out, v_out, o_out = unpacked_rows(0, second_chain, flat[:3], turned_out[1:])
+    shapes = [(LAYERS, model)] * 7 + [(LAYERS, local)] * 2
+    q_out, table_half, *vector_out = call(
+        functools.partial(vectors_unpack_kernel, Wide.PLACES[pair_order]),
+        (1,),
+        [(sums.numbers, smem)] + [(value, whole(value.shape)) for value in first_chain.finish()],
+        [
+            ((LAYERS, local, model), F32, layer_spec(0, (local, model)), turned_out[0]),
+            ((half_table, model), BF16, whole((half_table, model)), None),
+        ]
+        + [(shape, F32, whole(shape), None) for shape in shapes],
+        scratch=[pltpu.VMEM((first_chain.rows, model), F32)],
+    )
+    table_grad = by_core(table_half, over_core(table_half), 0).astype(F32)
 
     return (
         own_rows(jnp.concatenate(encoded, 0)),
         tokens_grad,
         table_grad,
-        jnp.swapaxes(turned_out[0], 1, 2),
-        mine[:, :local],
-        jnp.swapaxes(turned_out[1], 1, 2),
-        jnp.swapaxes(turned_out[2], 1, 2),
-        mine[:, local : 2 * local],
-        turned_out[3],
-        common[:, 5],
-        common[:, 3],
-        common[:, 4],
+        jnp.swapaxes(q_out, 1, 2),
+        vector_out[7],
+        jnp.swapaxes(k_out, 1, 2),
+        jnp.swapaxes(v_out, 1, 2),
+        vector_out[8],
+        o_out,
+        vector_out[5],
+        vector_out[3],
+        vector_out[4],
         up_out,
-        mine[:, 2 * local :],
+        vector_out[6],
         down_out,
-        common[:, 2],
-        common[:, 0],
-        common[:, 1],
+        vector_out[2],
+        vector_out[0],
+        vector_out[1],
     )
 
 

time: 580 us -> 540 us (0.931)
  local copies, waits for them, and re-layouts: 100 us -> 31 us
  Pallas kernels: 173 us -> 196 us
  waiting for transfers between devices: 146 us -> 169 us
  other arithmetic: 29.4 us -> 10.1 us
  starting transfers between devices: 102 us -> 118 us
  between operations: 17.1 us -> 2.75 us
    unnamed x528 -> x254, local copies, waits for them, and re-layouts: 84.9 us -> 27.7 us
    pallas_call x62 -> x108, Pallas kernels: 173 us -> 196 us  [call(): pl.pallas_call(body, **{} if grid is None else {'grid': grid}, in_specs=s...]
    ppermute x33 -> x36, starting transfers between devices: 34 us -> 50.7 us  [the longest x18 26.7 us: advance(): self.parts = [kept, lax.ppermute(sent, 'wide', self.wide.pairs(name))]]
    concatenate x20 -> x0, other arithmetic: 12.1 us -> none  [the longest x10 6.78 us: advance(): sent = jnp.concatenate([self.pieces, gate(self.received, *later)], 0)]
    ppermute x26, waiting for transfers between devices: 61.9 us -> 73.5 us  [over_chip(): return lax.ppermute(value, 'narrow', CHIP_SWAP)]
    ppermute x30 -> x29, waiting for transfers between devices: 0.96 us -> 8.31 us  [over_core(): return lax.ppermute(value, 'narrow', CORE_SWAP)]
    ppermute x33 -> x36, waiting for transfers between devices: 82.7 us -> 87.2 us  [the longest x18 47.7 us: advance(): self.parts = [kept, lax.ppermute(sent, 'wide', self.wide.pairs(name))]]
    ppermute x30 -> x29, starting transfers between devices: 48.3 us -> 44 us  [over_core(): return lax.ppermute(value, 'narrow', CORE_SWAP)]
  transfers between devices with their start and end apart: 90 -> 91, of which waited for: 33 -> 40; matrix products, arithmetic and copies ran while one was open for 9% -> 3% of each run, Pallas kernels for 26% -> 33%
where the time goes in v3:
time: 540 us; the launch traced here: 531 us
  Pallas kernels  196 us (36%)
  waiting for transfers between devices  169 us (31%)
  starting transfers between devices  118 us (22%)
  local copies, waits for them, and re-layouts  31 us (6%)
  other arithmetic  10.1 us (2%)
    pallas_call x108, Pallas kernels, call(): pl.pallas_call(body, **{} if grid is None else {'grid': grid}, in_specs=s...  196 us
    ppermute x26, waiting for transfers between devices, over_chip(): return lax.ppermute(value, 'narrow', CHIP_SWAP)  73.5 us
    ppermute x18, waiting for transfers between devices, advance(): self.parts = [kept, lax.ppermute(sent, 'wide', self.wide.pairs(name))]  47.7 us
    ppermute x29, starting transfers between devices, over_core(): return lax.ppermute(value, 'narrow', CORE_SWAP)  44 us
    ppermute x18, waiting for transfers between devices, advance(): self.parts = [sent, lax.ppermute(sent, 'wide', self.wide.pairs(name))]  39.5 us
    unnamed x254, local copies, waits for them, and re-layouts  27.7 us
    ppermute x18, starting transfers between devices, advance(): self.parts = [kept, lax.ppermute(sent, 'wide', self.wide.pairs(name))]  26.7 us
    ppermute x18, starting transfers between devices, advance(): self.parts = [sent, lax.ppermute(sent, 'wide', self.wide.pairs(name))]  24 us
  transfers between devices with their start and end apart: 91, of which 40 were waited for; matrix products, arithmetic and copies ran while one was open for 3% of the time, Pallas kernels for 33%

profile of v3, /device:TPU:1, one launch (start us, length us, event | category | flops | bytes accessed | tf_op | source)
XLA Modules:
  0.0 530.7 jit_solution(12838816577733985107)
XLA Ops:
  39.8 6.3 %shard_map.336 = (bf16[256,384]{1,0:T(8,128)(2,1)S(1)}, f32[256,384]{1,0:T(8,128)S(1)}, f32[8,256]{1,0:T(8,128)S(1)}, bf16[256,768]{1,0:T(8,128)(2,1)S(1)}) custom-call(s32[9]{0:T(128)S(1)} %pad_add_fusion.1.refs_0_, bf16[256,384]{1,0:T(8,128)(2,1)S(1)} %get-tuple-element.553.refs_1_.refs_6_, bf16[6,256,768]{2,1,0:T(8,128)(2,1)S(1)} %get-tuple-element.285.refs_2_.refs_1_, ...), custom_call_target="tpu_custom_call" | custom-call | flops 24000000000 | bytes 1 | tf_op jit(solution)/shard_map/pallas_call | solution.py:93
  94.1 5.1 shard_map.343
  99.7 5.8 %shard_map.346 = (bf16[256,384]{1,0:T(8,128)(2,1)S(1)}, f32[256,384]{1,0:T(8,128)S(1)}, f32[8,256]{1,0:T(8,128)S(1)}, bf16[256,768]{1,0:T(8,128)(2,1)S(1)}) custom-call(s32[9]{0:T(128)S(1)} %pad_add_fusion.1.refs_0_, bf16[256,384]{1,0:T(8,128)(2,1)S(1)} %get-tuple-element.313.refs_1_.refs_6_, bf16[6,256,768]{2,1,0:T(8,128)(2,1)S(1)} %get-tuple-element.304.refs_2_.refs_1_, ...), custom_call_target="tpu_custom_call" | custom-call | flops 24000000000 | bytes 1 | tf_op jit(solution)/shard_map/pallas_call | solution.py:93
  106.6 13.3 %collective-permute-done.22.refs_2_ = bf16[256,768]{1,0:T(8,128)(2,1)S(1)} collective-permute-done((bf16[256,768]{1,0:T(8,128)(2,1)S(1)}, bf16[256,768]{1,0:T(8,128)(2,1)S(1)}, u32[]{:S(2)}, u32[]{:S(2)}) %collective-permute-start.22) | collective-permute-done | bytes 393248 | tf_op jit(solution)/shard_map/ppermute | solution.py:29
  140.2 5.1 collective-permute-done.25.refs_4_
  170.6 7.5 %collective-permute-done.28.refs_2_ = bf16[256,768]{1,0:T(8,128)(2,1)S(1)} collective-permute-done((bf16[256,768]{1,0:T(8,128)(2,1)S(1)}, bf16[256,768]{1,0:T(8,128)(2,1)S(1)}, u32[]{:S(2)}, u32[]{:S(2)}) %collective-permute-start.28) | collective-permute-done | bytes 393248 | tf_op jit(solution)/shard_map/ppermute | solution.py:29
  179.0 7.6 %collective-permute-done.29.refs_2_ = bf16[256,768]{1,0:T(8,128)(2,1)S(1)} collective-permute-done((bf16[256,768]{1,0:T(8,128)(2,1)}, bf16[256,768]{1,0:T(8,128)(2,1)S(1)}, u32[]{:S(2)}, u32[]{:S(2)}) %collective-permute-start.29) | collective-permute-done | bytes 393248 | tf_op jit(solution)/shard_map/ppermute | solution.py:29
  188.4 6.5 %collective-permute-done.30.refs_2_ = bf16[256,768]{1,0:T(8,128)(2,1)S(1)} collective-permute-done((bf16[256,768]{1,0:T(8,128)(2,1)}, bf16[256,768]{1,0:T(8,128)(2,1)S(1)}, u32[]{:S(2)}, u32[]{:S(2)}) %collective-permute-start.30) | collective-permute-done | bytes 393248 | tf_op jit(solution)/shard_map/ppermute | solution.py:29
  201.0 10.0 %shard_map.362 = (bf16[768,128]{1,0:T(8,128)(2,1)S(1)}, f32[3,256,256]{2,1,0:T(8,128)S(1)}, bf16[3,256,256]{2,1,0:T(8,128)(2,1)S(1)}) custom-call(s32[9]{0:T(128)S(1)} %pad_add_fusion.1.refs_0_, bf16[6,256,768]{2,1,0:T(8,128)(2,1)S(1)} %get-tuple-element.304.refs_2_.refs_1_, bf16[6,768,256]{2,1,0:T(8,128)(2,1)S(1)} %get-tuple-element.305.refs_3_.refs_2_, ...), custom_call_target="tpu_custom_call" | custom-call | bytes 1 | tf_op jit(solution)/shard_map/pallas_call | solution.py:93
  212.9 10.0 %shard_map.363 = (bf16[768,128]{1,0:T(8,128)(2,1)S(1)}, f32[3,256,256]{2,1,0:T(8,128)S(1)}, bf16[3,256,256]{2,1,0:T(8,128)(2,1)S(1)}) custom-call(s32[9]{0:T(128)S(1)} %pad_add_fusion.1.refs_0_, bf16[6,256,768]{2,1,0:T(8,128)(2,1)S(1)} %get-tuple-element.304.refs_2_.refs_1_, bf16[6,768,256]{2,1,0:T(8,128)(2,1)S(1)} %get-tuple-element.305.refs_3_.refs_2_, ...), custom_call_target="tpu_custom_call" | custom-call | bytes 1 | tf_op jit(solution)/shard_map/pallas_call | solution.py:93
  222.9 10.2 %shard_map.364 = (bf16[768,128]{1,0:T(8,128)(2,1)S(1)}, f32[3,256,256]{2,1,0:T(8,128)S(1)}, bf16[3,256,256]{2,1,0:T(8,128)(2,1)S(1)}) custom-call(s32[9]{0:T(128)S(1)} %pad_add_fusion.1.refs_0_, bf16[6,256,768]{2,1,0:T(8,128)(2,1)S(1)} %get-tuple-element.304.refs_2_.refs_1_, bf16[6,768,256]{2,1,0:T(8,128)(2,1)S(1)} %get-tuple-element.305.refs_3_.refs_2_, ...), custom_call_target="tpu_custom_call" | custom-call | bytes 1 | tf_op jit(solution)/shard_map/pallas_call | solution.py:93
  252.6 8.4 %collective-permute-done.40.refs_2_ = bf16[384,768]{1,0:T(8,128)(2,1)S(1)} collective-permute-done((bf16[384,768]{1,0:T(8,128)(2,1)S(1)}, bf16[384,768]{1,0:T(8,128)(2,1)S(1)}, u32[]{:S(2)}, u32[]{:S(2)}) %collective-permute-start.40) | collective-permute-done | bytes 589856 | tf_op jit(solution)/shard_map/ppermute | solution.py:729
  294.7 6.7 %collective-permute-done.47.refs_2_ = bf16[256,768]{1,0:T(8,128)(2,1)S(1)} collective-permute-done((bf16[256,768]{1,0:T(8,128)(2,1)S(1)}, bf16[256,768]{1,0:T(8,128)(2,1)S(1)}, u32[]{:S(2)}, u32[]{:S(2)}) %collective-permute-start.47) | collective-permute-done | bytes 393248 | tf_op jit(solution)/shard_map/ppermute | solution.py:29
  315.2 9.9 %shard_map.392 = (bf16[768,128]{1,0:T(8,128)(2,1)S(1)}, f32[3,256,256]{2,1,0:T(8,128)S(1)}, bf16[3,256,256]{2,1,0:T(8,128)(2,1)S(1)}) custom-call(s32[9]{0:T(128)S(1)} %copy-done.98, bf16[6,256,768]{2,1,0:T(8,128)(2,1)S(1)} %copy-done.11, bf16[6,768,256]{2,1,0:T(8,128)(2,1)S(1)} %copy-done.13, s32[3,1,256]{2,1,0:T(1,128)S(1)} %slice.90.refs_4_.refs_3_, ...), custom_call_target="tpu_custom_call" | custom-call | bytes 1 | tf_op jit(solution)/shard_map/pallas_call | solution.py:93
  333.2 5.6 %collective-permute-done.53.refs_1_ = bf16[96,768]{1,0:T(8,128)(2,1)S(1)} collective-permute-done((bf16[96,768]{1,0:T(8,128)(2,1)S(1)}, bf16[96,768]{1,0:T(8,128)(2,1)S(1)}, u32[]{:S(2)}, u32[]{:S(2)}) %collective-permute-start.53) | collective-permute-done | bytes 147488 | tf_op jit(solution)/shard_map/ppermute | solution.py:729
  341.6 9.9 %shard_map.395 = (bf16[768,128]{1,0:T(8,128)(2,1)S(1)}, f32[3,256,256]{2,1,0:T(8,128)S(1)}, bf16[3,256,256]{2,1,0:T(8,128)(2,1)S(1)}) custom-call(s32[9]{0:T(128)S(1)} %copy-done.98, bf16[6,256,768]{2,1,0:T(8,128)(2,1)S(1)} %copy-done.11, bf16[6,768,256]{2,1,0:T(8,128)(2,1)S(1)} %copy-done.13, s32[3,1,256]{2,1,0:T(1,128)S(1)} %slice.90.refs_4_.refs_3_, ...), custom_call_target="tpu_custom_call" | custom-call | bytes 1 | tf_op jit(solution)/shard_map/pallas_call | solution.py:93
  353.9 7.4 %collective-permute-done.56.refs_2_ = bf16[384,768]{1,0:T(8,128)(2,1)S(1)} collective-permute-done((bf16[384,768]{1,0:T(8,128)(2,1)S(1)}, bf16[384,768]{1,0:T(8,128)(2,1)S(1)}, u32[]{:S(2)}, u32[]{:S(2)}) %collective-permute-start.56) | collective-permute-done | bytes 589856 | tf_op jit(solution)/shard_map/ppermute | solution.py:729
  363.8 9.3 %collective-permute-start.58 = (bf16[3,256,256]{2,1,0:T(8,128)(2,1)S(1)}, bf16[3,256,256]{2,1,0:T(8,128)(2,1)S(1)}, u32[]{:S(2)}, u32[]{:S(2)}) collective-permute-start(bf16[3,256,256]{2,1,0:T(8,128)(2,1)S(1)} %get-tuple-element.478), channel_id=1, source_target_pairs={{0,1},{1,0},{2,3},{3,2},{4,5},{5,4},{6,7},{7,6},{8,9},{9,8},{10,11... | collective-permute-start | bytes 1179656 | tf_op jit(solution)/shard_map/ppermute | solution.py:25
  373.1 10.1 %shard_map.399 = (bf16[768,128]{1,0:T(8,128)(2,1)S(1)}, f32[3,256,256]{2,1,0:T(8,128)S(1)}, bf16[3,256,256]{2,1,0:T(8,128)(2,1)S(1)}) custom-call(s32[9]{0:T(128)S(1)} %copy-done.98, bf16[6,256,768]{2,1,0:T(8,128)(2,1)S(1)} %copy-done.11, bf16[6,768,256]{2,1,0:T(8,128)(2,1)S(1)} %copy-done.13, s32[3,1,256]{2,1,0:T(1,128)S(1)} %slice.90.refs_4_.refs_3_, ...), custom_call_target="tpu_custom_call" | custom-call | bytes 1 | tf_op jit(solution)/shard_map/pallas_call | solution.py:93
  421.6 15.4 %collective-permute-done.72.refs_1_ = bf16[96,768]{1,0:T(8,128)(2,1)S(1)} collective-permute-done((bf16[96,768]{1,0:T(8,128)(2,1)S(1)}, bf16[96,768]{1,0:T(8,128)(2,1)S(1)}, u32[]{:S(2)}, u32[]{:S(2)}) %collective-permute-start.72) | collective-permute-done | bytes 147488 | tf_op jit(solution)/shard_map/ppermute | solution.py:729
  444.8 6.1 %collective-permute-done.76.refs_1_ = bf16[1,96,768]{2,1,0:T(8,128)(2,1)S(1)} collective-permute-done((bf16[1,96,768]{2,1,0:T(8,128)(2,1)S(1)}, bf16[1,96,768]{2,1,0:T(8,128)(2,1)S(1)}, u32[]{:S(2)}, u32[]{:S(2)}) %collective-permute-start.76) | collective-permute-done | bytes 147488 | tf_op jit(solution)/shard_map/ppermute | solution.py:737
  452.7 10.8 %collective-permute-done.78.refs_1_ = bf16[2,96,768]{2,1,0:T(8,128)(2,1)S(1)} collective-permute-done((bf16[2,96,768]{2,1,0:T(8,128)(2,1)S(1)}, bf16[2,96,768]{2,1,0:T(8,128)(2,1)S(1)}, u32[]{:S(2)}, u32[]{:S(2)}) %collective-permute-start.78) | collective-permute-done | bytes 294944 | tf_op jit(solution)/shard_map/ppermute | solution.py:737
  478.6 5.2 collective-permute-done.82.refs_1_
  494.1 14.9 %collective-permute-done.86.refs_2_ = bf16[4,48,768]{2,1,0:T(8,128)(2,1)S(1)} collective-permute-done((bf16[4,48,768]{2,1,0:T(8,128)(2,1)S(1)}, bf16[4,48,768]{2,1,0:T(8,128)(2,1)S(1)}, u32[]{:S(2)}, u32[]{:S(2)}) %collective-permute-start.86) | collective-permute-done | bytes 294944 | tf_op jit(solution)/shard_map/ppermute | solution.py:737
  (553 shorter events, 320.7 us)
Async XLA Ops:
  11.7 38.8 %collective-permute-start.12 = (bf16[2,768,768]{2,1,0:T(8,128)(2,1)}, bf16[2,768,768]{2,1,0:T(8,128)(2,1)S(1)}, u32[]{:S(2)}, u32[]{:S(2)}) collective-permute-start(bf16[2,768,768]{2,1,0:T(8,128)(2,1)} %refs_7_.25), channel_id=1, source_target_pairs={{0,1},{1,0},{2,3},{3,2},{4,5},{5,4},{6,7},{7,6},{8,9},{9,8},{10,11... | collective-permute-start | bytes 7077896 | tf_op jit(solution)/shard_map/ppermute | solution.py:25
  12.4 38.2 %collective-permute-start.13 = (bf16[2,768,768]{2,1,0:T(8,128)(2,1)}, bf16[2,768,768]{2,1,0:T(8,128)(2,1)S(1)}, u32[]{:S(2)}, u32[]{:S(2)}) collective-permute-start(bf16[2,768,768]{2,1,0:T(8,128)(2,1)} %refs_9_.13), channel_id=1, source_target_pairs={{0,1},{1,0},{2,3},{3,2},{4,5},{5,4},{6,7},{7,6},{8,9},{9,8},{10,11... | collective-permute-start | bytes 7077896 | tf_op jit(solution)/shard_map/ppermute | solution.py:25
  33.1 29.2 %collective-permute-start.17 = (bf16[256,768]{1,0:T(8,128)(2,1)S(1)}, bf16[256,768]{1,0:T(8,128)(2,1)S(1)}, u32[]{:S(2)}, u32[]{:S(2)}) collective-permute-start(bf16[256,768]{1,0:T(8,128)(2,1)S(1)} %get-tuple-element.300.refs_1_), channel_id=1, source_target_pairs={{0,2},{2,0},{1,3},{3,1},{4,6},{6,4},{5,7},{7,5},{8,10},{10,8},{9,1... | collective-permute-start | bytes 1179656 | tf_op jit(solution)/shard_map/ppermute | solution.py:29
  88.0 47.7 %collective-permute-start = (bf16[384,768]{1,0:T(8,128)(2,1)}, bf16[384,768]{1,0:T(8,128)(2,1)}, u32[]{:S(2)}, u32[]{:S(2)}) collective-permute-start(bf16[384,768]{1,0:T(8,128)(2,1)} %param.39), channel_id=1, source_target_pairs={{0,2},{2,0},{1,3},{3,1},{4,6},{6,4},{5,7},{7,5},{8,10},{10,8},{9,1... | collective-permute-start | bytes 1769480 | tf_op jit(solution)/shard_map/ppermute | solution.py:29
  93.0 39.3 %collective-permute-start.26 = (bf16[256,768]{1,0:T(8,128)(2,1)S(1)}, bf16[256,768]{1,0:T(8,128)(2,1)S(1)}, u32[]{:S(2)}, u32[]{:S(2)}) collective-permute-start(bf16[256,768]{1,0:T(8,128)(2,1)S(1)} %get-tuple-element.324.refs_1_), channel_id=1, source_target_pairs={{0,2},{2,0},{1,3},{3,1},{4,6},{6,4},{5,7},{7,5},{8,10},{10,8},{9,1... | collective-permute-start | bytes 1179656 | tf_op jit(solution)/shard_map/ppermute | solution.py:29
  166.8 69.1 %collective-permute-start.36 = (bf16[768,768]{1,0:T(8,128)(2,1)S(1)}, bf16[768,768]{1,0:T(8,128)(2,1)S(1)}, u32[]{:S(2)}, u32[]{:S(2)}) collective-permute-start(bf16[768,768]{1,0:T(8,128)(2,1)S(1)} %get-tuple-element.371.refs_18_), channel_id=1, source_target_pairs={{0,4},{4,0},{8,12},{12,8},{16,20},{20,16},{24,28},{28,24},{1,5},{5... | collective-permute-start | bytes 3538952 | tf_op jit(solution)/shard_map/ppermute | solution.py:729
  169.6 25.4 %collective-permute-start.30 = (bf16[256,768]{1,0:T(8,128)(2,1)}, bf16[256,768]{1,0:T(8,128)(2,1)S(1)}, u32[]{:S(2)}, u32[]{:S(2)}) collective-permute-start(bf16[256,768]{1,0:T(8,128)(2,1)} %get-tuple-element.342.refs_1_), channel_id=1, source_target_pairs={{0,2},{2,0},{1,3},{3,1},{4,6},{6,4},{5,7},{7,5},{8,10},{10,8},{9,1... | collective-permute-start | bytes 1179656 | tf_op jit(solution)/shard_map/ppermute | solution.py:29
  211.1 25.6 %collective-permute-start.34 = (bf16[3,256,256]{2,1,0:T(8,128)(2,1)S(1)}, bf16[3,256,256]{2,1,0:T(8,128)(2,1)S(1)}, u32[]{:S(2)}, u32[]{:S(2)}) collective-permute-start(bf16[3,256,256]{2,1,0:T(8,128)(2,1)S(1)} %get-tuple-element.378), channel_id=1, source_target_pairs={{0,1},{1,0},{2,3},{3,2},{4,5},{5,4},{6,7},{7,6},{8,9},{9,8},{10,11... | collective-permute-start | bytes 1179656 | tf_op jit(solution)/shard_map/ppermute | solution.py:25
  249.1 25.4 %collective-permute-start.45 = (bf16[256,768]{1,0:T(8,128)(2,1)S(1)}, bf16[256,768]{1,0:T(8,128)(2,1)S(1)}, u32[]{:S(2)}, u32[]{:S(2)}) collective-permute-start(bf16[256,768]{1,0:T(8,128)(2,1)S(1)} %get-tuple-element.397.refs_3_), channel_id=1, source_target_pairs={{0,2},{2,0},{1,3},{3,1},{4,6},{6,4},{5,7},{7,5},{8,10},{10,8},{9,1... | collective-permute-start | bytes 1179656 | tf_op jit(solution)/shard_map/ppermute | solution.py:29
  251.8 32.4 %collective-permute-start.44 = (bf16[384,768]{1,0:T(8,128)(2,1)S(1)}, bf16[384,768]{1,0:T(8,128)(2,1)S(1)}, u32[]{:S(2)}, u32[]{:S(2)}) collective-permute-start(bf16[384,768]{1,0:T(8,128)(2,1)S(1)} %get-tuple-element.395.refs_11_), channel_id=1, source_target_pairs={{0,8},{4,12},{8,0},{12,4},{16,24},{20,28},{24,16},{28,20},{1,9},{5... | collective-permute-start | bytes 1769480 | tf_op jit(solution)/shard_map/ppermute | solution.py:729
  278.2 32.5 %collective-permute-start.52 = (bf16[768,768]{1,0:T(8,128)(2,1)S(1)}, bf16[768,768]{1,0:T(8,128)(2,1)S(1)}, u32[]{:S(2)}, u32[]{:S(2)}) collective-permute-start(bf16[768,768]{1,0:T(8,128)(2,1)S(1)} %shard_map.389), channel_id=1, source_target_pairs={{0,1},{1,0},{2,3},{3,2},{4,5},{5,4},{6,7},{7,6},{8,9},{9,8},{10,11... | collective-permute-start | bytes 3538952 | tf_op jit(solution)/shard_map/ppermute | solution.py:25
  282.5 30.0 %collective-permute-start.51 = (bf16[768,768]{1,0:T(8,128)(2,1)S(1)}, bf16[768,768]{1,0:T(8,128)(2,1)S(1)}, u32[]{:S(2)}, u32[]{:S(2)}) collective-permute-start(bf16[768,768]{1,0:T(8,128)(2,1)S(1)} %shard_map.386), channel_id=1, source_target_pairs={{0,1},{1,0},{2,3},{3,2},{4,5},{5,4},{6,7},{7,6},{8,9},{9,8},{10,11... | collective-permute-start | bytes 3538952 | tf_op jit(solution)/shard_map/ppermute | solution.py:25
  325.2 60.8 %collective-permute-start.61 = (bf16[4,192,768]{2,1,0:T(8,128)(2,1)S(1)}, bf16[4,192,768]{2,1,0:T(8,128)(2,1)S(1)}, u32[]{:S(2)}, u32[]{:S(2)}) collective-permute-start(bf16[4,192,768]{2,1,0:T(8,128)(2,1)S(1)} %shard_map.394.refs_18_.refs_1_), channel_id=1, source_target_pairs={{0,4},{4,0},{8,12},{12,8},{16,20},{20,16},{24,28},{28,24},{1,5},{5... | collective-permute-start | bytes 3538952 | tf_op jit(solution)/shard_map/ppermute | solution.py:737
  325.4 27.5 %collective-permute-start.57 = (bf16[384,768]{1,0:T(8,128)(2,1)S(1)}, bf16[384,768]{1,0:T(8,128)(2,1)S(1)}, u32[]{:S(2)}, u32[]{:S(2)}) collective-permute-start(bf16[384,768]{1,0:T(8,128)(2,1)S(1)} %get-tuple-element.465.refs_21_), channel_id=1, source_target_pairs={{0,8},{4,12},{8,0},{12,4},{16,24},{20,28},{24,16},{28,20},{1,9},{5... | collective-permute-start | bytes 1769480 | tf_op jit(solution)/shard_map/ppermute | solution.py:729
  327.0 34.3 %collective-permute-start.56 = (bf16[384,768]{1,0:T(8,128)(2,1)S(1)}, bf16[384,768]{1,0:T(8,128)(2,1)S(1)}, u32[]{:S(2)}, u32[]{:S(2)}) collective-permute-start(bf16[384,768]{1,0:T(8,128)(2,1)S(1)} %get-tuple-element.458.refs_20_), channel_id=1, source_target_pairs={{0,4},{4,0},{8,12},{12,8},{16,20},{20,16},{24,28},{28,24},{1,5},{5... | collective-permute-start | bytes 1769480 | tf_op jit(solution)/shard_map/ppermute | solution.py:729
  351.6 31.6 %collective-permute-start.60 = (bf16[2,96,768]{2,1,0:T(8,128)(2,1)S(1)}, bf16[2,96,768]{2,1,0:T(8,128)(2,1)S(1)}, u32[]{:S(2)}, u32[]{:S(2)}) collective-permute-start(bf16[2,96,768]{2,1,0:T(8,128)(2,1)S(1)} %shard_map.396.refs_17_.refs_0_), channel_id=1, source_target_pairs={{0,4},{4,0},{8,12},{12,8},{16,20},{20,16},{24,28},{28,24},{1,5},{5... | collective-permute-start | bytes 884744 | tf_op jit(solution)/shard_map/ppermute | solution.py:737
  353.6 31.1 %collective-permute-start.63 = (bf16[192,768]{1,0:T(8,128)(2,1)S(1)}, bf16[192,768]{1,0:T(8,128)(2,1)S(1)}, u32[]{:S(2)}, u32[]{:S(2)}) collective-permute-start(bf16[192,768]{1,0:T(8,128)(2,1)S(1)} %get-tuple-element.472.refs_19_), channel_id=1, source_target_pairs={{0,4},{4,0},{8,12},{12,8},{16,20},{20,16},{24,28},{28,24},{1,5},{5... | collective-permute-start | bytes 884744 | tf_op jit(solution)/shard_map/ppermute | solution.py:729
  363.8 25.6 %collective-permute-start.58 = (bf16[3,256,256]{2,1,0:T(8,128)(2,1)S(1)}, bf16[3,256,256]{2,1,0:T(8,128)(2,1)S(1)}, u32[]{:S(2)}, u32[]{:S(2)}) collective-permute-start(bf16[3,256,256]{2,1,0:T(8,128)(2,1)S(1)} %get-tuple-element.478), channel_id=1, source_target_pairs={{0,1},{1,0},{2,3},{3,2},{4,5},{5,4},{6,7},{7,6},{8,9},{9,8},{10,11... | collective-permute-start | bytes 1179656 | tf_op jit(solution)/shard_map/ppermute | solution.py:25
  409.7 32.9 %collective-permute-start.77 = (bf16[4,96,768]{2,1,0:T(8,128)(2,1)S(1)}, bf16[4,96,768]{2,1,0:T(8,128)(2,1)S(1)}, u32[]{:S(2)}, u32[]{:S(2)}) collective-permute-start(bf16[4,96,768]{2,1,0:T(8,128)(2,1)S(1)} %copy-done.31), channel_id=1, source_target_pairs={{0,8},{4,12},{8,0},{12,4},{16,24},{20,28},{24,16},{28,20},{1,9},{5... | collective-permute-start | bytes 1769480 | tf_op jit(solution)/shard_map/ppermute | solution.py:737
  414.8 26.5 %collective-permute-start.70 = (bf16[320,768]{1,0:T(8,128)(2,1)S(1)}, bf16[320,768]{1,0:T(8,128)(2,1)S(1)}, u32[]{:S(2)}, u32[]{:S(2)}) collective-permute-start(bf16[320,768]{1,0:T(8,128)(2,1)S(1)} %get-tuple-element.514), channel_id=1, source_target_pairs={{0,8},{4,12},{8,0},{12,4},{16,24},{20,28},{24,16},{28,20},{1,9},{5... | collective-permute-start | bytes 1474568 | tf_op jit(solution)/shard_map/ppermute | solution.py:729
  489.7 27.3 %collective-permute-start.66 = (bf16[384,768]{1,0:T(8,128)(2,1)}, bf16[384,768]{1,0:T(8,128)(2,1)}, u32[]{:S(2)}, u32[]{:S(2)}) collective-permute-start(bf16[384,768]{1,0:T(8,128)(2,1)} %shard_map.411), channel_id=1, source_target_pairs={{0,2},{2,0},{1,3},{3,1},{4,6},{6,4},{5,7},{7,5},{8,10},{10,8},{9,1... | collective-permute-start | bytes 1769480 | tf_op jit(solution)/shard_map/ppermute | solution.py:29
  490.7 29.8 %collective-permute-start.89 = (bf16[4,96,768]{2,1,0:T(8,128)(2,1)S(1)}, bf16[4,96,768]{2,1,0:T(8,128)(2,1)}, u32[]{:S(2)}, u32[]{:S(2)}) collective-permute-start(bf16[4,96,768]{2,1,0:T(8,128)(2,1)S(1)} %shard_map.423.refs_2_.refs_1_), channel_id=1, source_target_pairs={{0,4},{4,0},{8,12},{12,8},{16,20},{20,16},{24,28},{28,24},{1,5},{5... | collective-permute-start | bytes 1769480 | tf_op jit(solution)/shard_map/ppermute | solution.py:737
  492.4 30.8 %collective-permute-start.90 = (bf16[4,96,768]{2,1,0:T(8,128)(2,1)S(1)}, bf16[4,96,768]{2,1,0:T(8,128)(2,1)}, u32[]{:S(2)}, u32[]{:S(2)}) collective-permute-start(bf16[4,96,768]{2,1,0:T(8,128)(2,1)S(1)} %shard_map.427.refs_2_.refs_1_), channel_id=1, source_target_pairs={{0,8},{4,12},{8,0},{12,4},{16,24},{20,28},{24,16},{28,20},{1,9},{5... | collective-permute-start | bytes 1769480 | tf_op jit(solution)/shard_map/ppermute | solution.py:737
  492.9 35.2 %collective-permute-start.88 = (bf16[4,80,768]{2,1,0:T(8,128)(2,1)S(1)}, bf16[4,80,768]{2,1,0:T(8,128)(2,1)}, u32[]{:S(2)}, u32[]{:S(2)}) collective-permute-start(bf16[4,80,768]{2,1,0:T(8,128)(2,1)S(1)} %shard_map.433.refs_2_.refs_1_), channel_id=1, source_target_pairs={{0,8},{4,12},{8,0},{12,4},{16,24},{20,28},{24,16},{28,20},{1,9},{5... | collective-permute-start | bytes 1474568 | tf_op jit(solution)/shard_map/ppermute | solution.py:737
  (194 other events, 1542.8 us)

commit v4 on v3

--- a/solution.py
+++ b/solution.py
@@ -119,7 +119,7 @@
     for head in range(head_count):
         pair = pair_block[:, (head // 2) * 128 : (head // 2) * 128 + 128]
         keep = low_half if head % 2 == 0 else jnp.logical_not(low_half)
-        target[head] = jnp.where(keep, pair, jnp.zeros_like(pair))
+        target[head * CHUNK : (head + 1) * CHUNK, :] = jnp.where(keep, pair, jnp.zeros_like(pair))
 
 
 def attend_kernel(
@@ -155,30 +155,34 @@
         @pl.when((bits_ref[tile] & q_bits) != 0)
         def _():
             hide = jnp.where(k_label_ref[tile] == q_label_ref[place], 0.0, NEG)
-            for head in range(head_count):
-                pair = (head // 2) * 128
-                scores = dot(kv_ref[tile, :, pair : pair + 128], masked_q[head], 1, 1) + hide
-                score_tiles[head, tile] = scores
-                highest = jnp.max(scores.reshape(-1, 8, CHUNK), 0)
-                top[head] = jnp.maximum(top[head], highest)
+            hide = jnp.concatenate([hide, hide], 1)
+            for pair in range(head_count // 2):
+                lanes = slice(pair * 128, pair * 128 + 128)
+                rows = slice(2 * pair * CHUNK, 2 * (pair + 1) * CHUNK)
+                scores = dot(kv_ref[tile, :, lanes], masked_q[rows, :], 1, 1) + hide
+                score_tiles[pair, tile] = scores
+                highest = jnp.max(scores.reshape(-1, 8, 2 * CHUNK), 0)
+                top[pair] = jnp.maximum(top[pair], highest)
 
         return carry
 
     lax.fori_loop(0, tiles, score_tile, 0)
-    for head in range(head_count):
-        top[head] = jnp.broadcast_to(jnp.max(top[head], 0, keepdims=True), (8, CHUNK))
+    for pair in range(head_count // 2):
+        top[pair] = jnp.broadcast_to(jnp.max(top[pair], 0, keepdims=True), (8, 2 * CHUNK))
 
     def weigh_tile(tile, carry):
         @pl.when((bits_ref[tile] & q_bits) != 0)
         def _():
-            for head in range(head_count):
-                weights = jnp.exp(score_tiles[head, tile] - top[head, 0:1, :])
-                mass[head] += jnp.sum(weights.reshape(-1, 8, CHUNK), 0)
-                rows = slice(head * HEAD_DIM, (head + 1) * HEAD_DIM)
-                total[rows, :] += dot(
-                    turned_ref[tile, width + head * HEAD_DIM : width + (head + 1) * HEAD_DIM, :],
-                    weights.astype(BF16),
-                )
+            for pair in range(head_count // 2):
+                weights = jnp.exp(score_tiles[pair, tile] - top[pair, 0:1, :])
+                mass[pair] += jnp.sum(weights.reshape(-1, 8, 2 * CHUNK), 0)
+                low = weights.astype(BF16)
+                for side in range(2):
+                    start = (2 * pair + side) * HEAD_DIM
+                    total[start : start + HEAD_DIM, :] += dot(
+                        turned_ref[tile, width + start : width + start + HEAD_DIM, :],
+                        low[:, side * CHUNK : (side + 1) * CHUNK],
+                    )
 
         return carry
 
@@ -186,9 +190,10 @@
     logsum_ref[...] = jnp.zeros_like(logsum_ref)
     for head in range(head_count):
         rows = slice(head * HEAD_DIM, (head + 1) * HEAD_DIM)
-        amount = jnp.sum(mass[head], 0, keepdims=True)
+        lanes = slice((head % 2) * CHUNK, (head % 2 + 1) * CHUNK)
+        amount = jnp.sum(mass[head // 2][:, lanes], 0, keepdims=True)
         total[rows, :] = total[rows, :] / amount
-        logsum_ref[head : head + 1, :] = top[head, 0:1, :] + jnp.log(amount)
+        logsum_ref[head : head + 1, :] = top[head // 2, 0:1, lanes] + jnp.log(amount)
     exact = total[...].T
     exact_ref[...] = exact
     context = exact.astype(BF16)
@@ -214,32 +219,31 @@
         crossed = (grad_refs[place][:, lanes].astype(F32) * exact_refs[place][:, lanes]).T
         for head in range(2):
             rows = slice(head * HEAD_DIM, (head + 1) * HEAD_DIM)
-            centre[head : head + 1, :] = jnp.sum(crossed[rows, :], 0, keepdims=True)
+            side = slice(head * CHUNK, (head + 1) * CHUNK)
+            number = 2 * pair + head
+            centre[0:1, side] = jnp.sum(crossed[rows, :], 0, keepdims=True)
+            centre[2:3, side] = logsum_refs[place][number : number + 1, :]
         q_total[...] = jnp.zeros_like(q_total)
         q_bits = bits_ref[tiles + place]
-        logsum_ref = logsum_refs[place]
 
         def one_tile(tile, carry):
             @pl.when((bits_ref[tile] & q_bits) != 0)
             def _():
                 hide = jnp.where(k_label_ref[tile] == q_label_ref[place], 0.0, NEG)
-                key_part = None
-                value_part = None
-                for head in range(2):
-                    number = 2 * pair + head
-                    scores = dot(kv_ref[tile, :, lanes], masked_q[head], 1, 1) + hide
-                    weights = jnp.exp(scores - logsum_ref[number : number + 1, :])
-                    weight_grad = dot(kv_ref[tile, :, v_lanes], masked_grad[head], 1, 1)
-                    score_grad = (weights * (weight_grad - centre[head : head + 1, :])).astype(BF16)
-                    value_now = dot(weights.astype(BF16), masked_grad[head])
-                    key_now = dot(score_grad, masked_q[head])
-                    value_part = value_now if value_part is None else value_part + value_now
-                    key_part = key_now if key_part is None else key_part + key_now
-                    rows = slice(head * HEAD_DIM, (head + 1) * HEAD_DIM)
-                    turned = slice(number * HEAD_DIM, (number + 1) * HEAD_DIM)
-                    q_total[rows, :] += dot(turned_ref[tile, turned, :], score_grad)
-                kv_total[tile, :, :128] += key_part
-                kv_total[tile, :, 128:] += value_part
+                hide = jnp.concatenate([hide, hide], 1)
+                scores = dot(kv_ref[tile, :, lanes], masked_q[...], 1, 1) + hide
+                weight_grad = dot(kv_ref[tile, :, v_lanes], masked_grad[...], 1, 1)
+                weights = jnp.exp(scores - centre[2:3, :])
+                score_grad = (weights * (weight_grad - centre[0:1, :])).astype(BF16)
+                kv_total[tile, :, 128:] += dot(weights.astype(BF16), masked_grad[...])
+                kv_total[tile, :, :128] += dot(score_grad, masked_q[...])
+                for side in range(2):
+                    rows = slice(side * HEAD_DIM, (side + 1) * HEAD_DIM)
+                    turned = slice((2 * pair + side) * HEAD_DIM, (2 * pair + side + 1) * HEAD_DIM)
+                    q_total[rows, :] += dot(
+                        turned_ref[tile, turned, :],
+                        score_grad[:, side * CHUNK : (side + 1) * CHUNK],
+                    )
 
             return carry
 
@@ -654,6 +658,10 @@
                     target[low - start : high - start, :] = ref[
                         low - place * CHUNK : high - place * CHUNK, :
                     ]
+
+
+def own_rows_kernel(numbers_ref, *refs):
+    pick_rows(numbers_ref[1], refs[:-1], refs[-1].shape[0], refs[-1])
 
 
 def tokens_send_kernel(numbers_ref, *refs):
@@ -951,11 +959,11 @@
                     (block, BF16, ON_CHIP, None),
                 ],
                 scratch=[
-                    pltpu.VMEM((head_count, CHUNK, 128), BF16),
+                    pltpu.VMEM((head_count * CHUNK, 128), BF16),
                     pltpu.VMEM((width, CHUNK), F32),
-                    pltpu.VMEM((head_count, 8, CHUNK), F32),
-                    pltpu.VMEM((head_count, 8, CHUNK), F32),
-                    pltpu.VMEM((head_count, tiles, CHUNK, CHUNK), F32),
+                    pltpu.VMEM((head_count // 2, 8, 2 * CHUNK), F32),
+                    pltpu.VMEM((head_count // 2, 8, 2 * CHUNK), F32),
+                    pltpu.VMEM((head_count // 2, tiles, CHUNK, 2 * CHUNK), F32),
                 ],
                 cost=6,
                 limit=20,
@@ -1135,6 +1143,13 @@
             keep["low_middle"], up_grad, square, received=[up_other_grad]
         )
         first_total, low_total, context_grad, first_sums = [], [], [], []
+        if top_layer:
+            (own_encoded,) = call(
+                own_rows_kernel,
+                (1,),
+                [(sums.numbers, smem)] + [(part, whole(block)) for part in encoded],
+                [((share, model), BF16, whole((share, model)), None)],
+            )
         for i in range(chunks):
             outs = call(
                 functools.partial(context_back_kernel, layer, i),
@@ -1159,7 +1174,7 @@
                     ((8, model), F32, ON_CHIP, None),
                 ],
                 after=(
-                    []
+                    [own_encoded] * (top_layer and i == 0)
                     if top_layer or i != 1
                     else [upper.advance(second_sums[2]), feed_chain.advance(second_sums[2])]
                 ),
@@ -1211,9 +1226,9 @@
                     (half_shape, BF16, ON_CHIP, None),
                 ],
                 scratch=[
-                    pltpu.VMEM((2, CHUNK, 128), BF16),
-                    pltpu.VMEM((2, CHUNK, 128), BF16),
-                    pltpu.VMEM((8, CHUNK), F32),
+                    pltpu.VMEM((2 * CHUNK, 128), BF16),
+                    pltpu.VMEM((2 * CHUNK, 128), BF16),
+                    pltpu.VMEM((8, 2 * CHUNK), F32),
                     pltpu.VMEM((128, CHUNK), F32),
                     pltpu.VMEM((tiles, CHUNK, 256), F32),
                 ],
@@ -1369,7 +1384,7 @@
     table_grad = by_core(table_half, over_core(table_half), 0).astype(F32)
 
     return (
-        own_rows(jnp.concatenate(encoded, 0)),
+        own_encoded,
         tokens_grad,
         table_grad,
         jnp.swapaxes(q_out, 1, 2),

time: 540 us -> 523 us (0.969)
  Pallas kernels: 196 us -> 181 us
  starting transfers between devices: 118 us -> 107 us
  waiting for transfers between devices: 169 us -> 176 us
    pallas_call x108 -> x109, Pallas kernels: 196 us -> 181 us  [call(): pl.pallas_call(body, **{} if grid is None else {'grid': grid}, in_specs=s...]
    ppermute x26, waiting for transfers between devices: 73.5 us -> 78.9 us  [over_chip(): return lax.ppermute(value, 'narrow', CHIP_SWAP)]
    unnamed x254 -> x240, local copies, waits for them, and re-layouts: 27.7 us -> 29.3 us
  transfers between devices with their start and end apart: 91 -> 91, of which waited for: 40 -> 38; matrix products, arithmetic and copies ran while one was open for 3% -> 4% of each run, Pallas kernels for 33% -> 32%
where the time goes in v4:
time: 523 us; the launch traced here: 514 us
  Pallas kernels  181 us (35%)
  waiting for transfers between devices  176 us (34%)
  starting transfers between devices  107 us (20%)
  local copies, waits for them, and re-layouts  34.6 us (7%)
  other arithmetic  8.51 us (2%)
    pallas_call x109, Pallas kernels, call(): pl.pallas_call(body, **{} if grid is None else {'grid': grid}, in_specs=s...  181 us
    ppermute x26, waiting for transfers between devices, over_chip(): return lax.ppermute(value, 'narrow', CHIP_SWAP)  78.9 us
    ppermute x18, waiting for transfers between devices, advance(): self.parts = [kept, lax.ppermute(sent, 'wide', self.wide.pairs(name))]  52.2 us
    ppermute x29, starting transfers between devices, over_core(): return lax.ppermute(value, 'narrow', CORE_SWAP)  38.9 us
    ppermute x18, waiting for transfers between devices, advance(): self.parts = [sent, lax.ppermute(sent, 'wide', self.wide.pairs(name))]  37.2 us
    unnamed x240, local copies, waits for them, and re-layouts  29.3 us
    ppermute x18, starting transfers between devices, advance(): self.parts = [kept, lax.ppermute(sent, 'wide', self.wide.pairs(name))]  24.9 us
    ppermute x18, starting transfers between devices, advance(): self.parts = [sent, lax.ppermute(sent, 'wide', self.wide.pairs(name))]  24.7 us
  transfers between devices with their start and end apart: 91, of which 38 were waited for; matrix products, arithmetic and copies ran while one was open for 4% of the time, Pallas kernels for 32%

profile of v4, /device:TPU:1, one launch (start us, length us, event | category | flops | bytes accessed | tf_op | source)
XLA Modules:
  0.0 514.2 jit_solution(11004030179339420769)
XLA Ops:
  37.7 5.8 %shard_map.336 = (bf16[256,384]{1,0:T(8,128)(2,1)S(1)}, f32[256,384]{1,0:T(8,128)S(1)}, f32[8,256]{1,0:T(8,128)S(1)}, bf16[256,768]{1,0:T(8,128)(2,1)S(1)}) custom-call(s32[9]{0:T(128)S(1)} %pad_add_fusion.1.refs_0_, bf16[256,384]{1,0:T(8,128)(2,1)S(1)} %get-tuple-element.554.refs_1_.refs_6_, bf16[6,256,768]{2,1,0:T(8,128)(2,1)S(1)} %get-tuple-element.285.refs_2_.refs_1_, ...), custom_call_target="tpu_custom_call" | custom-call | flops 24000000000 | bytes 1 | tf_op jit(solution)/shard_map/pallas_call | solution.py:93
  45.0 5.5 %shard_map.333 = (bf16[256,384]{1,0:T(8,128)(2,1)S(1)}, f32[256,384]{1,0:T(8,128)S(1)}, f32[8,256]{1,0:T(8,128)S(1)}, bf16[256,768]{1,0:T(8,128)(2,1)S(1)}) custom-call(s32[9]{0:T(128)S(1)} %pad_add_fusion.1.refs_0_, bf16[256,384]{1,0:T(8,128)(2,1)S(1)} %get-tuple-element.555.refs_1_.refs_5_, bf16[6,256,768]{2,1,0:T(8,128)(2,1)S(1)} %get-tuple-element.285.refs_2_.refs_1_, ...), custom_call_target="tpu_custom_call" | custom-call | flops 24000000000 | bytes 1 | tf_op jit(solution)/shard_map/pallas_call | solution.py:93
  98.4 5.8 %shard_map.346 = (bf16[256,384]{1,0:T(8,128)(2,1)S(1)}, f32[256,384]{1,0:T(8,128)S(1)}, f32[8,256]{1,0:T(8,128)S(1)}, bf16[256,768]{1,0:T(8,128)(2,1)S(1)}) custom-call(s32[9]{0:T(128)S(1)} %pad_add_fusion.1.refs_0_, bf16[256,384]{1,0:T(8,128)(2,1)S(1)} %get-tuple-element.313.refs_1_.refs_6_, bf16[6,256,768]{2,1,0:T(8,128)(2,1)S(1)} %get-tuple-element.304.refs_2_.refs_1_, ...), custom_call_target="tpu_custom_call" | custom-call | flops 24000000000 | bytes 1 | tf_op jit(solution)/shard_map/pallas_call | solution.py:93
  111.0 13.4 %collective-permute-done.24.refs_2_ = bf16[256,768]{1,0:T(8,128)(2,1)S(1)} collective-permute-done((bf16[256,768]{1,0:T(8,128)(2,1)S(1)}, bf16[256,768]{1,0:T(8,128)(2,1)S(1)}, u32[]{:S(2)}, u32[]{:S(2)}) %collective-permute-start.24) | collective-permute-done | bytes 393248 | tf_op jit(solution)/shard_map/ppermute | solution.py:29
  127.3 5.5 %collective-permute-done.22.refs_2_ = bf16[256,768]{1,0:T(8,128)(2,1)S(1)} collective-permute-done((bf16[256,768]{1,0:T(8,128)(2,1)S(1)}, bf16[256,768]{1,0:T(8,128)(2,1)S(1)}, u32[]{:S(2)}, u32[]{:S(2)}) %collective-permute-start.22) | collective-permute-done | bytes 393248 | tf_op jit(solution)/shard_map/ppermute | solution.py:29
  141.9 7.7 %collective-permute-done.23.refs_4_ = bf16[256,768]{1,0:T(8,128)(2,1)S(1)} collective-permute-done((bf16[256,768]{1,0:T(8,128)(2,1)S(1)}, bf16[256,768]{1,0:T(8,128)(2,1)S(1)}, u32[]{:S(2)}, u32[]{:S(2)}) %collective-permute-start.23) | collective-permute-done | bytes 393248 | tf_op jit(solution)/shard_map/ppermute | solution.py:29
  173.7 6.9 %collective-permute-done.28.refs_2_ = bf16[256,768]{1,0:T(8,128)(2,1)S(1)} collective-permute-done((bf16[256,768]{1,0:T(8,128)(2,1)S(1)}, bf16[256,768]{1,0:T(8,128)(2,1)S(1)}, u32[]{:S(2)}, u32[]{:S(2)}) %collective-permute-start.28) | collective-permute-done | bytes 393248 | tf_op jit(solution)/shard_map/ppermute | solution.py:29
  182.5 6.5 %collective-permute-done.29.refs_2_ = bf16[256,768]{1,0:T(8,128)(2,1)S(1)} collective-permute-done((bf16[256,768]{1,0:T(8,128)(2,1)S(1)}, bf16[256,768]{1,0:T(8,128)(2,1)S(1)}, u32[]{:S(2)}, u32[]{:S(2)}) %collective-permute-start.29) | collective-permute-done | bytes 393248 | tf_op jit(solution)/shard_map/ppermute | solution.py:29
  189.9 7.6 %collective-permute-done.30.refs_2_ = bf16[256,768]{1,0:T(8,128)(2,1)S(1)} collective-permute-done((bf16[256,768]{1,0:T(8,128)(2,1)S(1)}, bf16[256,768]{1,0:T(8,128)(2,1)S(1)}, u32[]{:S(2)}, u32[]{:S(2)}) %collective-permute-start.30) | collective-permute-done | bytes 393248 | tf_op jit(solution)/shard_map/ppermute | solution.py:29
  202.7 7.9 %shard_map.363 = (bf16[768,128]{1,0:T(8,128)(2,1)S(1)}, f32[3,256,256]{2,1,0:T(8,128)S(1)}, bf16[3,256,256]{2,1,0:T(8,128)(2,1)S(1)}) custom-call(s32[9]{0:T(128)S(1)} %pad_add_fusion.1.refs_0_, bf16[6,256,768]{2,1,0:T(8,128)(2,1)S(1)} %get-tuple-element.304.refs_2_.refs_1_, bf16[6,768,256]{2,1,0:T(8,128)(2,1)S(1)} %get-tuple-element.305.refs_3_.refs_2_, ...), custom_call_target="tpu_custom_call" | custom-call | bytes 1 | tf_op jit(solution)/shard_map/pallas_call | solution.py:93
  210.6 7.9 %shard_map.364 = (bf16[768,128]{1,0:T(8,128)(2,1)S(1)}, f32[3,256,256]{2,1,0:T(8,128)S(1)}, bf16[3,256,256]{2,1,0:T(8,128)(2,1)S(1)}) custom-call(s32[9]{0:T(128)S(1)} %pad_add_fusion.1.refs_0_, bf16[6,256,768]{2,1,0:T(8,128)(2,1)S(1)} %get-tuple-element.304.refs_2_.refs_1_, bf16[6,768,256]{2,1,0:T(8,128)(2,1)S(1)} %get-tuple-element.305.refs_3_.refs_2_, ...), custom_call_target="tpu_custom_call" | custom-call | bytes 1 | tf_op jit(solution)/shard_map/pallas_call | solution.py:93
  218.6 8.1 %shard_map.365 = (bf16[768,128]{1,0:T(8,128)(2,1)S(1)}, f32[3,256,256]{2,1,0:T(8,128)S(1)}, bf16[3,256,256]{2,1,0:T(8,128)(2,1)S(1)}) custom-call(s32[9]{0:T(128)S(1)} %pad_add_fusion.1.refs_0_, bf16[6,256,768]{2,1,0:T(8,128)(2,1)S(1)} %get-tuple-element.304.refs_2_.refs_1_, bf16[6,768,256]{2,1,0:T(8,128)(2,1)S(1)} %get-tuple-element.305.refs_3_.refs_2_, ...), custom_call_target="tpu_custom_call" | custom-call | bytes 1 | tf_op jit(solution)/shard_map/pallas_call | solution.py:93
  244.0 8.6 %collective-permute-done.40.refs_2_ = bf16[384,768]{1,0:T(8,128)(2,1)S(1)} collective-permute-done((bf16[384,768]{1,0:T(8,128)(2,1)S(1)}, bf16[384,768]{1,0:T(8,128)(2,1)S(1)}, u32[]{:S(2)}, u32[]{:S(2)}) %collective-permute-start.40) | collective-permute-done | bytes 589856 | tf_op jit(solution)/shard_map/ppermute | solution.py:737
  286.3 6.7 %collective-permute-done.47.refs_2_ = bf16[256,768]{1,0:T(8,128)(2,1)S(1)} collective-permute-done((bf16[256,768]{1,0:T(8,128)(2,1)S(1)}, bf16[256,768]{1,0:T(8,128)(2,1)S(1)}, u32[]{:S(2)}, u32[]{:S(2)}) %collective-permute-start.47) | collective-permute-done | bytes 393248 | tf_op jit(solution)/shard_map/ppermute | solution.py:29
  306.1 7.9 %shard_map.393 = (bf16[768,128]{1,0:T(8,128)(2,1)S(1)}, f32[3,256,256]{2,1,0:T(8,128)S(1)}, bf16[3,256,256]{2,1,0:T(8,128)(2,1)S(1)}) custom-call(s32[9]{0:T(128)S(1)} %copy-done.90, bf16[6,256,768]{2,1,0:T(8,128)(2,1)S(1)} %copy-done.11, bf16[6,768,256]{2,1,0:T(8,128)(2,1)S(1)} %copy-done.13, s32[3,1,256]{2,1,0:T(1,128)S(1)} %slice.82.refs_4_.refs_3_, ...), custom_call_target="tpu_custom_call" | custom-call | bytes 1 | tf_op jit(solution)/shard_map/pallas_call | solution.py:93
  320.2 10.0 %collective-permute-done.53.refs_1_ = bf16[96,768]{1,0:T(8,128)(2,1)S(1)} collective-permute-done((bf16[96,768]{1,0:T(8,128)(2,1)S(1)}, bf16[96,768]{1,0:T(8,128)(2,1)S(1)}, u32[]{:S(2)}, u32[]{:S(2)}) %collective-permute-start.53) | collective-permute-done | bytes 147488 | tf_op jit(solution)/shard_map/ppermute | solution.py:737
  333.2 7.8 %shard_map.396 = (bf16[768,128]{1,0:T(8,128)(2,1)S(1)}, f32[3,256,256]{2,1,0:T(8,128)S(1)}, bf16[3,256,256]{2,1,0:T(8,128)(2,1)S(1)}) custom-call(s32[9]{0:T(128)S(1)} %copy-done.90, bf16[6,256,768]{2,1,0:T(8,128)(2,1)S(1)} %copy-done.11, bf16[6,768,256]{2,1,0:T(8,128)(2,1)S(1)} %copy-done.13, s32[3,1,256]{2,1,0:T(1,128)S(1)} %slice.82.refs_4_.refs_3_, ...), custom_call_target="tpu_custom_call" | custom-call | bytes 1 | tf_op jit(solution)/shard_map/pallas_call | solution.py:93
  343.6 6.6 %collective-permute-done.56.refs_2_ = bf16[384,768]{1,0:T(8,128)(2,1)S(1)} collective-permute-done((bf16[384,768]{1,0:T(8,128)(2,1)S(1)}, bf16[384,768]{1,0:T(8,128)(2,1)S(1)}, u32[]{:S(2)}, u32[]{:S(2)}) %collective-permute-start.56) | collective-permute-done | bytes 589856 | tf_op jit(solution)/shard_map/ppermute | solution.py:737
  360.7 8.0 %shard_map.400 = (bf16[768,128]{1,0:T(8,128)(2,1)S(1)}, f32[3,256,256]{2,1,0:T(8,128)S(1)}, bf16[3,256,256]{2,1,0:T(8,128)(2,1)S(1)}) custom-call(s32[9]{0:T(128)S(1)} %copy-done.90, bf16[6,256,768]{2,1,0:T(8,128)(2,1)S(1)} %copy-done.11, bf16[6,768,256]{2,1,0:T(8,128)(2,1)S(1)} %copy-done.13, s32[3,1,256]{2,1,0:T(1,128)S(1)} %slice.82.refs_4_.refs_3_, ...), custom_call_target="tpu_custom_call" | custom-call | bytes 1 | tf_op jit(solution)/shard_map/pallas_call | solution.py:93
  406.0 16.1 %collective-permute-done.72.refs_1_ = bf16[96,768]{1,0:T(8,128)(2,1)S(1)} collective-permute-done((bf16[96,768]{1,0:T(8,128)(2,1)S(1)}, bf16[96,768]{1,0:T(8,128)(2,1)S(1)}, u32[]{:S(2)}, u32[]{:S(2)}) %collective-permute-start.72) | collective-permute-done | bytes 147488 | tf_op jit(solution)/shard_map/ppermute | solution.py:737
  429.7 5.8 %collective-permute-done.76.refs_1_ = bf16[1,96,768]{2,1,0:T(8,128)(2,1)S(1)} collective-permute-done((bf16[1,96,768]{2,1,0:T(8,128)(2,1)S(1)}, bf16[1,96,768]{2,1,0:T(8,128)(2,1)S(1)}, u32[]{:S(2)}, u32[]{:S(2)}) %collective-permute-start.76) | collective-permute-done | bytes 147488 | tf_op jit(solution)/shard_map/ppermute | solution.py:745
  437.9 10.1 %collective-permute-done.78.refs_1_ = bf16[2,96,768]{2,1,0:T(8,128)(2,1)S(1)} collective-permute-done((bf16[2,96,768]{2,1,0:T(8,128)(2,1)S(1)}, bf16[2,96,768]{2,1,0:T(8,128)(2,1)S(1)}, u32[]{:S(2)}, u32[]{:S(2)}) %collective-permute-start.78) | collective-permute-done | bytes 294944 | tf_op jit(solution)/shard_map/ppermute | solution.py:745
  463.1 5.2 %collective-permute-done.82.refs_1_ = bf16[1,48,768]{2,1,0:T(8,128)(2,1)S(1)} collective-permute-done((bf16[1,48,768]{2,1,0:T(8,128)(2,1)S(1)}, bf16[1,48,768]{2,1,0:T(8,128)(2,1)S(1)}, u32[]{:S(2)}, u32[]{:S(2)}) %collective-permute-start.82) | collective-permute-done | bytes 73760 | tf_op jit(solution)/shard_map/ppermute | solution.py:745
  478.5 14.1 %collective-permute-done.86.refs_2_ = bf16[4,48,768]{2,1,0:T(8,128)(2,1)S(1)} collective-permute-done((bf16[4,48,768]{2,1,0:T(8,128)(2,1)S(1)}, bf16[4,48,768]{2,1,0:T(8,128)(2,1)S(1)}, u32[]{:S(2)}, u32[]{:S(2)}) %collective-permute-start.86) | collective-permute-done | bytes 294944 | tf_op jit(solution)/shard_map/ppermute | solution.py:745
  (539 shorter events, 315.9 us)
Async XLA Ops:
  16.2 34.6 %collective-permute-start.12 = (bf16[2,768,768]{2,1,0:T(8,128)(2,1)}, bf16[2,768,768]{2,1,0:T(8,128)(2,1)S(1)}, u32[]{:S(2)}, u32[]{:S(2)}) collective-permute-start(bf16[2,768,768]{2,1,0:T(8,128)(2,1)} %refs_7_.25), channel_id=1, source_target_pairs={{0,1},{1,0},{2,3},{3,2},{4,5},{5,4},{6,7},{7,6},{8,9},{9,8},{10,11... | collective-permute-start | bytes 7077896 | tf_op jit(solution)/shard_map/ppermute | solution.py:25
  16.5 34.2 %collective-permute-start.13 = (bf16[2,768,768]{2,1,0:T(8,128)(2,1)}, bf16[2,768,768]{2,1,0:T(8,128)(2,1)S(1)}, u32[]{:S(2)}, u32[]{:S(2)}) collective-permute-start(bf16[2,768,768]{2,1,0:T(8,128)(2,1)} %refs_9_.13), channel_id=1, source_target_pairs={{0,1},{1,0},{2,3},{3,2},{4,5},{5,4},{6,7},{7,6},{8,9},{9,8},{10,11... | collective-permute-start | bytes 7077896 | tf_op jit(solution)/shard_map/ppermute | solution.py:25
  92.4 47.6 %collective-permute-start = (bf16[384,768]{1,0:T(8,128)(2,1)}, bf16[384,768]{1,0:T(8,128)(2,1)}, u32[]{:S(2)}, u32[]{:S(2)}) collective-permute-start(bf16[384,768]{1,0:T(8,128)(2,1)} %param.39), channel_id=1, source_target_pairs={{0,2},{2,0},{1,3},{3,1},{4,6},{6,4},{5,7},{7,5},{8,10},{10,8},{9,1... | collective-permute-start | bytes 1769480 | tf_op jit(solution)/shard_map/ppermute | solution.py:29
  98.2 37.5 %collective-permute-start.26 = (bf16[256,768]{1,0:T(8,128)(2,1)S(1)}, bf16[256,768]{1,0:T(8,128)(2,1)S(1)}, u32[]{:S(2)}, u32[]{:S(2)}) collective-permute-start(bf16[256,768]{1,0:T(8,128)(2,1)S(1)} %get-tuple-element.324.refs_1_), channel_id=1, source_target_pairs={{0,2},{2,0},{1,3},{3,1},{4,6},{6,4},{5,7},{7,5},{8,10},{10,8},{9,1... | collective-permute-start | bytes 1179656 | tf_op jit(solution)/shard_map/ppermute | solution.py:29
  110.8 22.0 %collective-permute-start.22 = (bf16[256,768]{1,0:T(8,128)(2,1)S(1)}, bf16[256,768]{1,0:T(8,128)(2,1)S(1)}, u32[]{:S(2)}, u32[]{:S(2)}) collective-permute-start(bf16[256,768]{1,0:T(8,128)(2,1)S(1)} %get-tuple-element.306.refs_1_), channel_id=1, source_target_pairs={{0,2},{2,0},{1,3},{3,1},{4,6},{6,4},{5,7},{7,5},{8,10},{10,8},{9,1... | collective-permute-start | bytes 1179656 | tf_op jit(solution)/shard_map/ppermute | solution.py:29
  127.2 25.0 %collective-permute-start.25 = (bf16[256,768]{1,0:T(8,128)(2,1)S(1)}, bf16[256,768]{1,0:T(8,128)(2,1)S(1)}, u32[]{:S(2)}, u32[]{:S(2)}) collective-permute-start(bf16[256,768]{1,0:T(8,128)(2,1)S(1)} %get-tuple-element.317.refs_3_), channel_id=1, source_target_pairs={{0,2},{2,0},{1,3},{3,1},{4,6},{6,4},{5,7},{7,5},{8,10},{10,8},{9,1... | collective-permute-start | bytes 1179656 | tf_op jit(solution)/shard_map/ppermute | solution.py:29
  169.3 60.7 %collective-permute-start.36 = (bf16[768,768]{1,0:T(8,128)(2,1)S(1)}, bf16[768,768]{1,0:T(8,128)(2,1)S(1)}, u32[]{:S(2)}, u32[]{:S(2)}) collective-permute-start(bf16[768,768]{1,0:T(8,128)(2,1)S(1)} %get-tuple-element.371.refs_18_), channel_id=1, source_target_pairs={{0,4},{4,0},{8,12},{12,8},{16,20},{20,16},{24,28},{28,24},{1,5},{5... | collective-permute-start | bytes 3538952 | tf_op jit(solution)/shard_map/ppermute | solution.py:737
  172.1 25.4 %collective-permute-start.30 = (bf16[256,768]{1,0:T(8,128)(2,1)S(1)}, bf16[256,768]{1,0:T(8,128)(2,1)S(1)}, u32[]{:S(2)}, u32[]{:S(2)}) collective-permute-start(bf16[256,768]{1,0:T(8,128)(2,1)S(1)} %get-tuple-element.342.refs_1_), channel_id=1, source_target_pairs={{0,2},{2,0},{1,3},{3,1},{4,6},{6,4},{5,7},{7,5},{8,10},{10,8},{9,1... | collective-permute-start | bytes 1179656 | tf_op jit(solution)/shard_map/ppermute | solution.py:29
  240.7 25.4 %collective-permute-start.45 = (bf16[256,768]{1,0:T(8,128)(2,1)S(1)}, bf16[256,768]{1,0:T(8,128)(2,1)S(1)}, u32[]{:S(2)}, u32[]{:S(2)}) collective-permute-start(bf16[256,768]{1,0:T(8,128)(2,1)S(1)} %get-tuple-element.397.refs_3_), channel_id=1, source_target_pairs={{0,2},{2,0},{1,3},{3,1},{4,6},{6,4},{5,7},{7,5},{8,10},{10,8},{9,1... | collective-permute-start | bytes 1179656 | tf_op jit(solution)/shard_map/ppermute | solution.py:29
  242.7 33.1 %collective-permute-start.44 = (bf16[384,768]{1,0:T(8,128)(2,1)S(1)}, bf16[384,768]{1,0:T(8,128)(2,1)S(1)}, u32[]{:S(2)}, u32[]{:S(2)}) collective-permute-start(bf16[384,768]{1,0:T(8,128)(2,1)S(1)} %get-tuple-element.395.refs_11_), channel_id=1, source_target_pairs={{0,8},{4,12},{8,0},{12,4},{16,24},{20,28},{24,16},{28,20},{1,9},{5... | collective-permute-start | bytes 1769480 | tf_op jit(solution)/shard_map/ppermute | solution.py:737
  269.8 31.8 %collective-permute-start.52 = (bf16[768,768]{1,0:T(8,128)(2,1)S(1)}, bf16[768,768]{1,0:T(8,128)(2,1)S(1)}, u32[]{:S(2)}, u32[]{:S(2)}) collective-permute-start(bf16[768,768]{1,0:T(8,128)(2,1)S(1)} %shard_map.390), channel_id=1, source_target_pairs={{0,1},{1,0},{2,3},{3,2},{4,5},{5,4},{6,7},{7,6},{8,9},{9,8},{10,11... | collective-permute-start | bytes 3538952 | tf_op jit(solution)/shard_map/ppermute | solution.py:25
  274.1 29.3 %collective-permute-start.51 = (bf16[768,768]{1,0:T(8,128)(2,1)S(1)}, bf16[768,768]{1,0:T(8,128)(2,1)S(1)}, u32[]{:S(2)}, u32[]{:S(2)}) collective-permute-start(bf16[768,768]{1,0:T(8,128)(2,1)S(1)} %shard_map.387), channel_id=1, source_target_pairs={{0,1},{1,0},{2,3},{3,2},{4,5},{5,4},{6,7},{7,6},{8,9},{9,8},{10,11... | collective-permute-start | bytes 3538952 | tf_op jit(solution)/shard_map/ppermute | solution.py:25
  314.1 57.0 %collective-permute-start.61 = (bf16[4,192,768]{2,1,0:T(8,128)(2,1)S(1)}, bf16[4,192,768]{2,1,0:T(8,128)(2,1)S(1)}, u32[]{:S(2)}, u32[]{:S(2)}) collective-permute-start(bf16[4,192,768]{2,1,0:T(8,128)(2,1)S(1)} %shard_map.395.refs_18_.refs_1_), channel_id=1, source_target_pairs={{0,4},{4,0},{8,12},{12,8},{16,20},{20,16},{24,28},{28,24},{1,5},{5... | collective-permute-start | bytes 3538952 | tf_op jit(solution)/shard_map/ppermute | solution.py:745
  314.4 28.5 %collective-permute-start.57 = (bf16[384,768]{1,0:T(8,128)(2,1)S(1)}, bf16[384,768]{1,0:T(8,128)(2,1)S(1)}, u32[]{:S(2)}, u32[]{:S(2)}) collective-permute-start(bf16[384,768]{1,0:T(8,128)(2,1)S(1)} %get-tuple-element.465.refs_21_), channel_id=1, source_target_pairs={{0,8},{4,12},{8,0},{12,4},{16,24},{20,28},{24,16},{28,20},{1,9},{5... | collective-permute-start | bytes 1769480 | tf_op jit(solution)/shard_map/ppermute | solution.py:737
  316.7 33.6 %collective-permute-start.56 = (bf16[384,768]{1,0:T(8,128)(2,1)S(1)}, bf16[384,768]{1,0:T(8,128)(2,1)S(1)}, u32[]{:S(2)}, u32[]{:S(2)}) collective-permute-start(bf16[384,768]{1,0:T(8,128)(2,1)S(1)} %get-tuple-element.458.refs_20_), channel_id=1, source_target_pairs={{0,4},{4,0},{8,12},{12,8},{16,20},{20,16},{24,28},{28,24},{1,5},{5... | collective-permute-start | bytes 1769480 | tf_op jit(solution)/shard_map/ppermute | solution.py:737
  341.1 27.6 %collective-permute-start.60 = (bf16[2,96,768]{2,1,0:T(8,128)(2,1)S(1)}, bf16[2,96,768]{2,1,0:T(8,128)(2,1)S(1)}, u32[]{:S(2)}, u32[]{:S(2)}) collective-permute-start(bf16[2,96,768]{2,1,0:T(8,128)(2,1)S(1)} %shard_map.397.refs_17_.refs_0_), channel_id=1, source_target_pairs={{0,4},{4,0},{8,12},{12,8},{16,20},{20,16},{24,28},{28,24},{1,5},{5... | collective-permute-start | bytes 884744 | tf_op jit(solution)/shard_map/ppermute | solution.py:745
  343.6 26.2 %collective-permute-start.63 = (bf16[192,768]{1,0:T(8,128)(2,1)S(1)}, bf16[192,768]{1,0:T(8,128)(2,1)S(1)}, u32[]{:S(2)}, u32[]{:S(2)}) collective-permute-start(bf16[192,768]{1,0:T(8,128)(2,1)S(1)} %get-tuple-element.472.refs_19_), channel_id=1, source_target_pairs={{0,4},{4,0},{8,12},{12,8},{16,20},{20,16},{24,28},{28,24},{1,5},{5... | collective-permute-start | bytes 884744 | tf_op jit(solution)/shard_map/ppermute | solution.py:737
  394.5 33.1 %collective-permute-start.77 = (bf16[4,96,768]{2,1,0:T(8,128)(2,1)S(1)}, bf16[4,96,768]{2,1,0:T(8,128)(2,1)S(1)}, u32[]{:S(2)}, u32[]{:S(2)}) collective-permute-start(bf16[4,96,768]{2,1,0:T(8,128)(2,1)S(1)} %copy-done.31), channel_id=1, source_target_pairs={{0,8},{4,12},{8,0},{12,4},{16,24},{20,28},{24,16},{28,20},{1,9},{5... | collective-permute-start | bytes 1769480 | tf_op jit(solution)/shard_map/ppermute | solution.py:745
  399.3 27.0 %collective-permute-start.70 = (bf16[320,768]{1,0:T(8,128)(2,1)S(1)}, bf16[320,768]{1,0:T(8,128)(2,1)S(1)}, u32[]{:S(2)}, u32[]{:S(2)}) collective-permute-start(bf16[320,768]{1,0:T(8,128)(2,1)S(1)} %get-tuple-element.514), channel_id=1, source_target_pairs={{0,8},{4,12},{8,0},{12,4},{16,24},{20,28},{24,16},{28,20},{1,9},{5... | collective-permute-start | bytes 1474568 | tf_op jit(solution)/shard_map/ppermute | solution.py:737
  402.7 24.3 %collective-permute-start.69 = (bf16[192,768]{1,0:T(8,128)(2,1)S(1)}, bf16[192,768]{1,0:T(8,128)(2,1)S(1)}, u32[]{:S(2)}, u32[]{:S(2)}) collective-permute-start(bf16[192,768]{1,0:T(8,128)(2,1)S(1)} %get-tuple-element.512.refs_2_), channel_id=1, source_target_pairs={{0,4},{4,0},{8,12},{12,8},{16,20},{20,16},{24,28},{28,24},{1,5},{5... | collective-permute-start | bytes 884744 | tf_op jit(solution)/shard_map/ppermute | solution.py:737
  474.2 24.0 %collective-permute-start.66 = (bf16[384,768]{1,0:T(8,128)(2,1)}, bf16[384,768]{1,0:T(8,128)(2,1)}, u32[]{:S(2)}, u32[]{:S(2)}) collective-permute-start(bf16[384,768]{1,0:T(8,128)(2,1)} %shard_map.412), channel_id=1, source_target_pairs={{0,2},{2,0},{1,3},{3,1},{4,6},{6,4},{5,7},{7,5},{8,10},{10,8},{9,1... | collective-permute-start | bytes 1769480 | tf_op jit(solution)/shard_map/ppermute | solution.py:29
  474.4 29.6 %collective-permute-start.89 = (bf16[4,96,768]{2,1,0:T(8,128)(2,1)S(1)}, bf16[4,96,768]{2,1,0:T(8,128)(2,1)}, u32[]{:S(2)}, u32[]{:S(2)}) collective-permute-start(bf16[4,96,768]{2,1,0:T(8,128)(2,1)S(1)} %shard_map.424.refs_2_.refs_1_), channel_id=1, source_target_pairs={{0,4},{4,0},{8,12},{12,8},{16,20},{20,16},{24,28},{28,24},{1,5},{5... | collective-permute-start | bytes 1769480 | tf_op jit(solution)/shard_map/ppermute | solution.py:745
  476.1 30.7 %collective-permute-start.90 = (bf16[4,96,768]{2,1,0:T(8,128)(2,1)S(1)}, bf16[4,96,768]{2,1,0:T(8,128)(2,1)}, u32[]{:S(2)}, u32[]{:S(2)}) collective-permute-start(bf16[4,96,768]{2,1,0:T(8,128)(2,1)S(1)} %shard_map.428.refs_2_.refs_1_), channel_id=1, source_target_pairs={{0,8},{4,12},{8,0},{12,4},{16,24},{20,28},{24,16},{28,20},{1,9},{5... | collective-permute-start | bytes 1769480 | tf_op jit(solution)/shard_map/ppermute | solution.py:745
  477.4 34.2 %collective-permute-start.88 = (bf16[4,80,768]{2,1,0:T(8,128)(2,1)S(1)}, bf16[4,80,768]{2,1,0:T(8,128)(2,1)}, u32[]{:S(2)}, u32[]{:S(2)}) collective-permute-start(bf16[4,80,768]{2,1,0:T(8,128)(2,1)S(1)} %shard_map.434.refs_2_.refs_1_), channel_id=1, source_target_pairs={{0,8},{4,12},{8,0},{12,4},{16,24},{20,28},{24,16},{28,20},{1,9},{5... | collective-permute-start | bytes 1474568 | tf_op jit(solution)/shard_map/ppermute | solution.py:745
  (187 other events, 1547.3 us)

commit v5 on v4

--- a/solution.py
+++ b/solution.py
@@ -1365,6 +1365,7 @@
                 scratch=[pltpu.VMEM((share, model), BF16)],
                 after=[token],
             )
+            token = tokens_grad
         if step == 4:
             (up_out,) = unpacked_rows(0, strands[0], [square], [up_out], after=[token])
             (down_out,) = unpacked_rows(0, strands[1], [square[::-1]], [down_out])

time: 523 us -> 507 us (0.969)
  starting transfers between devices: 107 us -> 99.2 us
  local copies, waits for them, and re-layouts: 34.6 us -> 28.3 us
    ppermute x18, waiting for transfers between devices: 37.2 us -> 29.6 us  [advance(): self.parts = [sent, lax.ppermute(sent, 'wide', self.wide.pairs(name))]]
    ppermute x18, waiting for transfers between devices: 52.2 us -> 59.5 us  [advance(): self.parts = [kept, lax.ppermute(sent, 'wide', self.wide.pairs(name))]]
    unnamed x240 -> x236, local copies, waits for them, and re-layouts: 29.3 us -> 23.6 us
    ppermute x18, starting transfers between devices: 24.9 us -> 19.4 us  [advance(): self.parts = [kept, lax.ppermute(sent, 'wide', self.wide.pairs(name))]]
  transfers between devices with their start and end apart: 91 -> 91, of which waited for: 38 -> 42; matrix products, arithmetic and copies ran while one was open for 4% -> 3% of each run, Pallas kernels for 32% -> 32%
where the time goes in v5:
time: 507 us; the launch traced here: 500 us
  waiting for transfers between devices  181 us (36%)
  Pallas kernels  177 us (35%)
  starting transfers between devices  99.2 us (20%)
  local copies, waits for them, and re-layouts  28.3 us (6%)
  other arithmetic  7.41 us (1%)
    pallas_call x109, Pallas kernels, call(): pl.pallas_call(body, **{} if grid is None else {'grid': grid}, in_specs=s...  177 us
    ppermute x26, waiting for transfers between devices, over_chip(): return lax.ppermute(value, 'narrow', CHIP_SWAP)  82.8 us
    ppermute x18, waiting for transfers between devices, advance(): self.parts = [kept, lax.ppermute(sent, 'wide', self.wide.pairs(name))]  59.5 us
    ppermute x29, starting transfers between devices, over_core(): return lax.ppermute(value, 'narrow', CORE_SWAP)  40.3 us
    ppermute x18, waiting for transfers between devices, advance(): self.parts = [sent, lax.ppermute(sent, 'wide', self.wide.pairs(name))]  29.6 us
    unnamed x236, local copies, waits for them, and re-layouts  23.6 us
    ppermute x18, starting transfers between devices, advance(): self.parts = [sent, lax.ppermute(sent, 'wide', self.wide.pairs(name))]  21.5 us
    ppermute x18, starting transfers between devices, advance(): self.parts = [kept, lax.ppermute(sent, 'wide', self.wide.pairs(name))]  19.4 us
  transfers between devices with their start and end apart: 91, of which 42 were waited for; matrix products, arithmetic and copies ran while one was open for 3% of the time, Pallas kernels for 32%

profile of v5, /device:TPU:1, one launch (start us, length us, event | category | flops | bytes accessed | tf_op | source)
XLA Modules:
  0.0 500.0 jit_solution(1162179246657692454)
XLA Ops:
  36.9 5.8 %shard_map.336 = (bf16[256,384]{1,0:T(8,128)(2,1)S(1)}, f32[256,384]{1,0:T(8,128)S(1)}, f32[8,256]{1,0:T(8,128)S(1)}, bf16[256,768]{1,0:T(8,128)(2,1)S(1)}) custom-call(s32[9]{0:T(128)S(1)} %pad_add_fusion.1.refs_0_, bf16[256,384]{1,0:T(8,128)(2,1)S(1)} %get-tuple-element.554.refs_1_.refs_6_, bf16[6,256,768]{2,1,0:T(8,128)(2,1)S(1)} %get-tuple-element.285.refs_2_.refs_1_, ...), custom_call_target="tpu_custom_call" | custom-call | flops 24000000000 | bytes 1 | tf_op jit(solution)/shard_map/pallas_call | solution.py:93
  96.9 5.8 %shard_map.346 = (bf16[256,384]{1,0:T(8,128)(2,1)S(1)}, f32[256,384]{1,0:T(8,128)S(1)}, f32[8,256]{1,0:T(8,128)S(1)}, bf16[256,768]{1,0:T(8,128)(2,1)S(1)}) custom-call(s32[9]{0:T(128)S(1)} %pad_add_fusion.1.refs_0_, bf16[256,384]{1,0:T(8,128)(2,1)S(1)} %get-tuple-element.313.refs_1_.refs_6_, bf16[6,256,768]{2,1,0:T(8,128)(2,1)S(1)} %get-tuple-element.304.refs_2_.refs_1_, ...), custom_call_target="tpu_custom_call" | custom-call | flops 24000000000 | bytes 1 | tf_op jit(solution)/shard_map/pallas_call | solution.py:93
  109.4 14.2 %collective-permute-done.24.refs_2_ = bf16[256,768]{1,0:T(8,128)(2,1)S(1)} collective-permute-done((bf16[256,768]{1,0:T(8,128)(2,1)S(1)}, bf16[256,768]{1,0:T(8,128)(2,1)S(1)}, u32[]{:S(2)}, u32[]{:S(2)}) %collective-permute-start.24) | collective-permute-done | bytes 393248 | tf_op jit(solution)/shard_map/ppermute | solution.py:29
  141.2 7.7 %collective-permute-done.23.refs_4_ = bf16[256,768]{1,0:T(8,128)(2,1)S(1)} collective-permute-done((bf16[256,768]{1,0:T(8,128)(2,1)S(1)}, bf16[256,768]{1,0:T(8,128)(2,1)S(1)}, u32[]{:S(2)}, u32[]{:S(2)}) %collective-permute-start.23) | collective-permute-done | bytes 393248 | tf_op jit(solution)/shard_map/ppermute | solution.py:29
  173.3 6.9 %collective-permute-done.28.refs_2_ = bf16[256,768]{1,0:T(8,128)(2,1)S(1)} collective-permute-done((bf16[256,768]{1,0:T(8,128)(2,1)S(1)}, bf16[256,768]{1,0:T(8,128)(2,1)S(1)}, u32[]{:S(2)}, u32[]{:S(2)}) %collective-permute-start.28) | collective-permute-done | bytes 393248 | tf_op jit(solution)/shard_map/ppermute | solution.py:29
  183.0 5.6 %collective-permute-done.29.refs_2_ = bf16[256,768]{1,0:T(8,128)(2,1)S(1)} collective-permute-done((bf16[256,768]{1,0:T(8,128)(2,1)}, bf16[256,768]{1,0:T(8,128)(2,1)S(1)}, u32[]{:S(2)}, u32[]{:S(2)}) %collective-permute-start.29) | collective-permute-done | bytes 393248 | tf_op jit(solution)/shard_map/ppermute | solution.py:29
  190.5 6.6 %collective-permute-done.30.refs_2_ = bf16[256,768]{1,0:T(8,128)(2,1)S(1)} collective-permute-done((bf16[256,768]{1,0:T(8,128)(2,1)S(1)}, bf16[256,768]{1,0:T(8,128)(2,1)S(1)}, u32[]{:S(2)}, u32[]{:S(2)}) %collective-permute-start.30) | collective-permute-done | bytes 393248 | tf_op jit(solution)/shard_map/ppermute | solution.py:29
  202.2 7.4 %shard_map.363 = (bf16[768,128]{1,0:T(8,128)(2,1)S(1)}, f32[3,256,256]{2,1,0:T(8,128)S(1)}, bf16[3,256,256]{2,1,0:T(8,128)(2,1)S(1)}) custom-call(s32[9]{0:T(128)S(1)} %pad_add_fusion.1.refs_0_, bf16[6,256,768]{2,1,0:T(8,128)(2,1)S(1)} %get-tuple-element.304.refs_2_.refs_1_, bf16[6,768,256]{2,1,0:T(8,128)(2,1)S(1)} %get-tuple-element.305.refs_3_.refs_2_, ...), custom_call_target="tpu_custom_call" | custom-call | bytes 1 | tf_op jit(solution)/shard_map/pallas_call | solution.py:93
  209.6 7.4 %shard_map.364 = (bf16[768,128]{1,0:T(8,128)(2,1)S(1)}, f32[3,256,256]{2,1,0:T(8,128)S(1)}, bf16[3,256,256]{2,1,0:T(8,128)(2,1)S(1)}) custom-call(s32[9]{0:T(128)S(1)} %pad_add_fusion.1.refs_0_, bf16[6,256,768]{2,1,0:T(8,128)(2,1)S(1)} %get-tuple-element.304.refs_2_.refs_1_, bf16[6,768,256]{2,1,0:T(8,128)(2,1)S(1)} %get-tuple-element.305.refs_3_.refs_2_, ...), custom_call_target="tpu_custom_call" | custom-call | bytes 1 | tf_op jit(solution)/shard_map/pallas_call | solution.py:93
  217.1 7.6 %shard_map.365 = (bf16[768,128]{1,0:T(8,128)(2,1)S(1)}, f32[3,256,256]{2,1,0:T(8,128)S(1)}, bf16[3,256,256]{2,1,0:T(8,128)(2,1)S(1)}) custom-call(s32[9]{0:T(128)S(1)} %pad_add_fusion.1.refs_0_, bf16[6,256,768]{2,1,0:T(8,128)(2,1)S(1)} %get-tuple-element.304.refs_2_.refs_1_, bf16[6,768,256]{2,1,0:T(8,128)(2,1)S(1)} %get-tuple-element.305.refs_3_.refs_2_, ...), custom_call_target="tpu_custom_call" | custom-call | bytes 1 | tf_op jit(solution)/shard_map/pallas_call | solution.py:93
  244.8 9.1 %collective-permute-done.40.refs_2_ = bf16[384,768]{1,0:T(8,128)(2,1)S(1)} collective-permute-done((bf16[384,768]{1,0:T(8,128)(2,1)S(1)}, bf16[384,768]{1,0:T(8,128)(2,1)S(1)}, u32[]{:S(2)}, u32[]{:S(2)}) %collective-permute-start.40) | collective-permute-done | bytes 589856 | tf_op jit(solution)/shard_map/ppermute | solution.py:737
  261.7 5.8 %collective-permute-done.45.refs_4_ = bf16[256,768]{1,0:T(8,128)(2,1)S(1)} collective-permute-done((bf16[256,768]{1,0:T(8,128)(2,1)S(1)}, bf16[256,768]{1,0:T(8,128)(2,1)S(1)}, u32[]{:S(2)}, u32[]{:S(2)}) %collective-permute-start.45) | collective-permute-done | bytes 393248 | tf_op jit(solution)/shard_map/ppermute | solution.py:29
  279.2 6.2 %collective-permute-done.43.refs_2_ = bf16[256,768]{1,0:T(8,128)(2,1)S(1)} collective-permute-done((bf16[256,768]{1,0:T(8,128)(2,1)S(1)}, bf16[256,768]{1,0:T(8,128)(2,1)S(1)}, u32[]{:S(2)}, u32[]{:S(2)}) %collective-permute-start.43) | collective-permute-done | bytes 393248 | tf_op jit(solution)/shard_map/ppermute | solution.py:29
  287.1 6.7 %collective-permute-done.47.refs_2_ = bf16[256,768]{1,0:T(8,128)(2,1)S(1)} collective-permute-done((bf16[256,768]{1,0:T(8,128)(2,1)S(1)}, bf16[256,768]{1,0:T(8,128)(2,1)S(1)}, u32[]{:S(2)}, u32[]{:S(2)}) %collective-permute-start.47) | collective-permute-done | bytes 393248 | tf_op jit(solution)/shard_map/ppermute | solution.py:29
  307.4 7.4 %shard_map.393 = (bf16[768,128]{1,0:T(8,128)(2,1)S(1)}, f32[3,256,256]{2,1,0:T(8,128)S(1)}, bf16[3,256,256]{2,1,0:T(8,128)(2,1)S(1)}) custom-call(s32[9]{0:T(128)S(1)} %copy-done.95, bf16[6,256,768]{2,1,0:T(8,128)(2,1)S(1)} %copy-done.11, bf16[6,768,256]{2,1,0:T(8,128)(2,1)S(1)} %copy-done.13, s32[3,1,256]{2,1,0:T(1,128)S(1)} %slice.82.refs_4_.refs_3_, ...), custom_call_target="tpu_custom_call" | custom-call | bytes 1 | tf_op jit(solution)/shard_map/pallas_call | solution.py:93
  318.8 12.2 %collective-permute-done.53.refs_1_ = bf16[96,768]{1,0:T(8,128)(2,1)S(1)} collective-permute-done((bf16[96,768]{1,0:T(8,128)(2,1)S(1)}, bf16[96,768]{1,0:T(8,128)(2,1)S(1)}, u32[]{:S(2)}, u32[]{:S(2)}) %collective-permute-start.53) | collective-permute-done | bytes 147488 | tf_op jit(solution)/shard_map/ppermute | solution.py:737
  333.8 7.4 %shard_map.396 = (bf16[768,128]{1,0:T(8,128)(2,1)S(1)}, f32[3,256,256]{2,1,0:T(8,128)S(1)}, bf16[3,256,256]{2,1,0:T(8,128)(2,1)S(1)}) custom-call(s32[9]{0:T(128)S(1)} %copy-done.95, bf16[6,256,768]{2,1,0:T(8,128)(2,1)S(1)} %copy-done.11, bf16[6,768,256]{2,1,0:T(8,128)(2,1)S(1)} %copy-done.13, s32[3,1,256]{2,1,0:T(1,128)S(1)} %slice.82.refs_4_.refs_3_, ...), custom_call_target="tpu_custom_call" | custom-call | bytes 1 | tf_op jit(solution)/shard_map/pallas_call | solution.py:93
  343.6 8.4 %collective-permute-done.56.refs_2_ = bf16[384,768]{1,0:T(8,128)(2,1)S(1)} collective-permute-done((bf16[384,768]{1,0:T(8,128)(2,1)S(1)}, bf16[384,768]{1,0:T(8,128)(2,1)S(1)}, u32[]{:S(2)}, u32[]{:S(2)}) %collective-permute-start.56) | collective-permute-done | bytes 589856 | tf_op jit(solution)/shard_map/ppermute | solution.py:737
  354.1 8.3 %collective-permute-start.58 = (bf16[3,256,256]{2,1,0:T(8,128)(2,1)S(1)}, bf16[3,256,256]{2,1,0:T(8,128)(2,1)S(1)}, u32[]{:S(2)}, u32[]{:S(2)}) collective-permute-start(bf16[3,256,256]{2,1,0:T(8,128)(2,1)S(1)} %get-tuple-element.478), channel_id=1, source_target_pairs={{0,1},{1,0},{2,3},{3,2},{4,5},{5,4},{6,7},{7,6},{8,9},{9,8},{10,11... | collective-permute-start | bytes 1179656 | tf_op jit(solution)/shard_map/ppermute | solution.py:25
  362.5 7.6 %shard_map.400 = (bf16[768,128]{1,0:T(8,128)(2,1)S(1)}, f32[3,256,256]{2,1,0:T(8,128)S(1)}, bf16[3,256,256]{2,1,0:T(8,128)(2,1)S(1)}) custom-call(s32[9]{0:T(128)S(1)} %copy-done.95, bf16[6,256,768]{2,1,0:T(8,128)(2,1)S(1)} %copy-done.11, bf16[6,768,256]{2,1,0:T(8,128)(2,1)S(1)} %copy-done.13, s32[3,1,256]{2,1,0:T(1,128)S(1)} %slice.82.refs_4_.refs_3_, ...), custom_call_target="tpu_custom_call" | custom-call | bytes 1 | tf_op jit(solution)/shard_map/pallas_call | solution.py:93
  401.1 15.9 %collective-permute-done.72.refs_1_ = bf16[96,768]{1,0:T(8,128)(2,1)S(1)} collective-permute-done((bf16[96,768]{1,0:T(8,128)(2,1)S(1)}, bf16[96,768]{1,0:T(8,128)(2,1)S(1)}, u32[]{:S(2)}, u32[]{:S(2)}) %collective-permute-start.72) | collective-permute-done | bytes 147488 | tf_op jit(solution)/shard_map/ppermute | solution.py:737
  433.1 8.3 %collective-permute-done.78.refs_1_ = bf16[2,96,768]{2,1,0:T(8,128)(2,1)S(1)} collective-permute-done((bf16[2,96,768]{2,1,0:T(8,128)(2,1)S(1)}, bf16[2,96,768]{2,1,0:T(8,128)(2,1)S(1)}, u32[]{:S(2)}, u32[]{:S(2)}) %collective-permute-start.78) | collective-permute-done | bytes 294944 | tf_op jit(solution)/shard_map/ppermute | solution.py:745
  452.4 5.6 %collective-permute-done.79.refs_1_ = bf16[48,768]{1,0:T(8,128)(2,1)S(1)} collective-permute-done((bf16[48,768]{1,0:T(8,128)(2,1)S(1)}, bf16[48,768]{1,0:T(8,128)(2,1)S(1)}, u32[]{:S(2)}, u32[]{:S(2)}) %collective-permute-start.79) | collective-permute-done | bytes 73760 | tf_op jit(solution)/shard_map/ppermute | solution.py:737
  474.5 13.1 %collective-permute-done.86.refs_2_ = bf16[4,48,768]{2,1,0:T(8,128)(2,1)S(1)} collective-permute-done((bf16[4,48,768]{2,1,0:T(8,128)(2,1)S(1)}, bf16[4,48,768]{2,1,0:T(8,128)(2,1)S(1)}, u32[]{:S(2)}, u32[]{:S(2)}) %collective-permute-start.86) | collective-permute-done | bytes 294944 | tf_op jit(solution)/shard_map/ppermute | solution.py:745
  (535 shorter events, 300.3 us)
Async XLA Ops:
  16.2 33.7 %collective-permute-start.12 = (bf16[2,768,768]{2,1,0:T(8,128)(2,1)}, bf16[2,768,768]{2,1,0:T(8,128)(2,1)S(1)}, u32[]{:S(2)}, u32[]{:S(2)}) collective-permute-start(bf16[2,768,768]{2,1,0:T(8,128)(2,1)} %refs_7_.25), channel_id=1, source_target_pairs={{0,1},{1,0},{2,3},{3,2},{4,5},{5,4},{6,7},{7,6},{8,9},{9,8},{10,11... | collective-permute-start | bytes 7077896 | tf_op jit(solution)/shard_map/ppermute | solution.py:25
  16.5 33.4 %collective-permute-start.13 = (bf16[2,768,768]{2,1,0:T(8,128)(2,1)}, bf16[2,768,768]{2,1,0:T(8,128)(2,1)S(1)}, u32[]{:S(2)}, u32[]{:S(2)}) collective-permute-start(bf16[2,768,768]{2,1,0:T(8,128)(2,1)} %refs_9_.13), channel_id=1, source_target_pairs={{0,1},{1,0},{2,3},{3,2},{4,5},{5,4},{6,7},{7,6},{8,9},{9,8},{10,11... | collective-permute-start | bytes 7077896 | tf_op jit(solution)/shard_map/ppermute | solution.py:25
  91.6 47.7 %collective-permute-start = (bf16[384,768]{1,0:T(8,128)(2,1)}, bf16[384,768]{1,0:T(8,128)(2,1)}, u32[]{:S(2)}, u32[]{:S(2)}) collective-permute-start(bf16[384,768]{1,0:T(8,128)(2,1)} %param.39), channel_id=1, source_target_pairs={{0,2},{2,0},{1,3},{3,1},{4,6},{6,4},{5,7},{7,5},{8,10},{10,8},{9,1... | collective-permute-start | bytes 1769480 | tf_op jit(solution)/shard_map/ppermute | solution.py:29
  96.6 38.3 %collective-permute-start.26 = (bf16[256,768]{1,0:T(8,128)(2,1)S(1)}, bf16[256,768]{1,0:T(8,128)(2,1)S(1)}, u32[]{:S(2)}, u32[]{:S(2)}) collective-permute-start(bf16[256,768]{1,0:T(8,128)(2,1)S(1)} %get-tuple-element.324.refs_1_), channel_id=1, source_target_pairs={{0,2},{2,0},{1,3},{3,1},{4,6},{6,4},{5,7},{7,5},{8,10},{10,8},{9,1... | collective-permute-start | bytes 1179656 | tf_op jit(solution)/shard_map/ppermute | solution.py:29
  109.2 22.8 %collective-permute-start.22 = (bf16[256,768]{1,0:T(8,128)(2,1)S(1)}, bf16[256,768]{1,0:T(8,128)(2,1)S(1)}, u32[]{:S(2)}, u32[]{:S(2)}) collective-permute-start(bf16[256,768]{1,0:T(8,128)(2,1)S(1)} %get-tuple-element.306.refs_1_), channel_id=1, source_target_pairs={{0,2},{2,0},{1,3},{3,1},{4,6},{6,4},{5,7},{7,5},{8,10},{10,8},{9,1... | collective-permute-start | bytes 1179656 | tf_op jit(solution)/shard_map/ppermute | solution.py:29
  126.4 24.9 %collective-permute-start.25 = (bf16[256,768]{1,0:T(8,128)(2,1)S(1)}, bf16[256,768]{1,0:T(8,128)(2,1)S(1)}, u32[]{:S(2)}, u32[]{:S(2)}) collective-permute-start(bf16[256,768]{1,0:T(8,128)(2,1)S(1)} %get-tuple-element.317.refs_3_), channel_id=1, source_target_pairs={{0,2},{2,0},{1,3},{3,1},{4,6},{6,4},{5,7},{7,5},{8,10},{10,8},{9,1... | collective-permute-start | bytes 1179656 | tf_op jit(solution)/shard_map/ppermute | solution.py:29
  168.1 60.0 %collective-permute-start.36 = (bf16[768,768]{1,0:T(8,128)(2,1)S(1)}, bf16[768,768]{1,0:T(8,128)(2,1)S(1)}, u32[]{:S(2)}, u32[]{:S(2)}) collective-permute-start(bf16[768,768]{1,0:T(8,128)(2,1)S(1)} %get-tuple-element.371.refs_18_), channel_id=1, source_target_pairs={{0,4},{4,0},{8,12},{12,8},{16,20},{20,16},{24,28},{28,24},{1,5},{5... | collective-permute-start | bytes 3538952 | tf_op jit(solution)/shard_map/ppermute | solution.py:737
  171.6 25.4 %collective-permute-start.30 = (bf16[256,768]{1,0:T(8,128)(2,1)S(1)}, bf16[256,768]{1,0:T(8,128)(2,1)S(1)}, u32[]{:S(2)}, u32[]{:S(2)}) collective-permute-start(bf16[256,768]{1,0:T(8,128)(2,1)S(1)} %get-tuple-element.342.refs_1_), channel_id=1, source_target_pairs={{0,2},{2,0},{1,3},{3,1},{4,6},{6,4},{5,7},{7,5},{8,10},{10,8},{9,1... | collective-permute-start | bytes 1179656 | tf_op jit(solution)/shard_map/ppermute | solution.py:29
  241.8 25.6 %collective-permute-start.45 = (bf16[256,768]{1,0:T(8,128)(2,1)S(1)}, bf16[256,768]{1,0:T(8,128)(2,1)S(1)}, u32[]{:S(2)}, u32[]{:S(2)}) collective-permute-start(bf16[256,768]{1,0:T(8,128)(2,1)S(1)} %get-tuple-element.397.refs_3_), channel_id=1, source_target_pairs={{0,2},{2,0},{1,3},{3,1},{4,6},{6,4},{5,7},{7,5},{8,10},{10,8},{9,1... | collective-permute-start | bytes 1179656 | tf_op jit(solution)/shard_map/ppermute | solution.py:29
  243.7 32.9 %collective-permute-start.44 = (bf16[384,768]{1,0:T(8,128)(2,1)S(1)}, bf16[384,768]{1,0:T(8,128)(2,1)S(1)}, u32[]{:S(2)}, u32[]{:S(2)}) collective-permute-start(bf16[384,768]{1,0:T(8,128)(2,1)S(1)} %get-tuple-element.395.refs_11_), channel_id=1, source_target_pairs={{0,8},{4,12},{8,0},{12,4},{16,24},{20,28},{24,16},{28,20},{1,9},{5... | collective-permute-start | bytes 1769480 | tf_op jit(solution)/shard_map/ppermute | solution.py:737
  271.2 31.7 %collective-permute-start.52 = (bf16[768,768]{1,0:T(8,128)(2,1)S(1)}, bf16[768,768]{1,0:T(8,128)(2,1)S(1)}, u32[]{:S(2)}, u32[]{:S(2)}) collective-permute-start(bf16[768,768]{1,0:T(8,128)(2,1)S(1)} %shard_map.390), channel_id=1, source_target_pairs={{0,1},{1,0},{2,3},{3,2},{4,5},{5,4},{6,7},{7,6},{8,9},{9,8},{10,11... | collective-permute-start | bytes 3538952 | tf_op jit(solution)/shard_map/ppermute | solution.py:25
  275.0 29.7 %collective-permute-start.51 = (bf16[768,768]{1,0:T(8,128)(2,1)S(1)}, bf16[768,768]{1,0:T(8,128)(2,1)S(1)}, u32[]{:S(2)}, u32[]{:S(2)}) collective-permute-start(bf16[768,768]{1,0:T(8,128)(2,1)S(1)} %shard_map.387), channel_id=1, source_target_pairs={{0,1},{1,0},{2,3},{3,2},{4,5},{5,4},{6,7},{7,6},{8,9},{9,8},{10,11... | collective-permute-start | bytes 3538952 | tf_op jit(solution)/shard_map/ppermute | solution.py:25
  314.9 57.5 %collective-permute-start.61 = (bf16[4,192,768]{2,1,0:T(8,128)(2,1)S(1)}, bf16[4,192,768]{2,1,0:T(8,128)(2,1)S(1)}, u32[]{:S(2)}, u32[]{:S(2)}) collective-permute-start(bf16[4,192,768]{2,1,0:T(8,128)(2,1)S(1)} %shard_map.395.refs_18_.refs_1_), channel_id=1, source_target_pairs={{0,4},{4,0},{8,12},{12,8},{16,20},{20,16},{24,28},{28,24},{1,5},{5... | collective-permute-start | bytes 3538952 | tf_op jit(solution)/shard_map/ppermute | solution.py:745
  315.2 26.1 %collective-permute-start.57 = (bf16[384,768]{1,0:T(8,128)(2,1)S(1)}, bf16[384,768]{1,0:T(8,128)(2,1)S(1)}, u32[]{:S(2)}, u32[]{:S(2)}) collective-permute-start(bf16[384,768]{1,0:T(8,128)(2,1)S(1)} %get-tuple-element.465.refs_21_), channel_id=1, source_target_pairs={{0,8},{4,12},{8,0},{12,4},{16,24},{20,28},{24,16},{28,20},{1,9},{5... | collective-permute-start | bytes 1769480 | tf_op jit(solution)/shard_map/ppermute | solution.py:737
  317.6 34.4 %collective-permute-start.56 = (bf16[384,768]{1,0:T(8,128)(2,1)S(1)}, bf16[384,768]{1,0:T(8,128)(2,1)S(1)}, u32[]{:S(2)}, u32[]{:S(2)}) collective-permute-start(bf16[384,768]{1,0:T(8,128)(2,1)S(1)} %get-tuple-element.458.refs_20_), channel_id=1, source_target_pairs={{0,4},{4,0},{8,12},{12,8},{16,20},{20,16},{24,28},{28,24},{1,5},{5... | collective-permute-start | bytes 1769480 | tf_op jit(solution)/shard_map/ppermute | solution.py:737
  341.3 28.8 %collective-permute-start.60 = (bf16[2,96,768]{2,1,0:T(8,128)(2,1)S(1)}, bf16[2,96,768]{2,1,0:T(8,128)(2,1)S(1)}, u32[]{:S(2)}, u32[]{:S(2)}) collective-permute-start(bf16[2,96,768]{2,1,0:T(8,128)(2,1)S(1)} %shard_map.397.refs_17_.refs_0_), channel_id=1, source_target_pairs={{0,4},{4,0},{8,12},{12,8},{16,20},{20,16},{24,28},{28,24},{1,5},{5... | collective-permute-start | bytes 884744 | tf_op jit(solution)/shard_map/ppermute | solution.py:745
  342.0 29.1 %collective-permute-start.63 = (bf16[192,768]{1,0:T(8,128)(2,1)S(1)}, bf16[192,768]{1,0:T(8,128)(2,1)S(1)}, u32[]{:S(2)}, u32[]{:S(2)}) collective-permute-start(bf16[192,768]{1,0:T(8,128)(2,1)S(1)} %get-tuple-element.472.refs_19_), channel_id=1, source_target_pairs={{0,4},{4,0},{8,12},{12,8},{16,20},{20,16},{24,28},{28,24},{1,5},{5... | collective-permute-start | bytes 884744 | tf_op jit(solution)/shard_map/ppermute | solution.py:737
  390.4 33.0 %collective-permute-start.77 = (bf16[4,96,768]{2,1,0:T(8,128)(2,1)S(1)}, bf16[4,96,768]{2,1,0:T(8,128)(2,1)S(1)}, u32[]{:S(2)}, u32[]{:S(2)}) collective-permute-start(bf16[4,96,768]{2,1,0:T(8,128)(2,1)S(1)} %copy-done.34), channel_id=1, source_target_pairs={{0,8},{4,12},{8,0},{12,4},{16,24},{20,28},{24,16},{28,20},{1,9},{5... | collective-permute-start | bytes 1769480 | tf_op jit(solution)/shard_map/ppermute | solution.py:745
  395.7 26.4 %collective-permute-start.70 = (bf16[320,768]{1,0:T(8,128)(2,1)S(1)}, bf16[320,768]{1,0:T(8,128)(2,1)S(1)}, u32[]{:S(2)}, u32[]{:S(2)}) collective-permute-start(bf16[320,768]{1,0:T(8,128)(2,1)S(1)} %get-tuple-element.514), channel_id=1, source_target_pairs={{0,8},{4,12},{8,0},{12,4},{16,24},{20,28},{24,16},{28,20},{1,9},{5... | collective-permute-start | bytes 1474568 | tf_op jit(solution)/shard_map/ppermute | solution.py:737
  398.5 24.2 %collective-permute-start.69 = (bf16[192,768]{1,0:T(8,128)(2,1)S(1)}, bf16[192,768]{1,0:T(8,128)(2,1)S(1)}, u32[]{:S(2)}, u32[]{:S(2)}) collective-permute-start(bf16[192,768]{1,0:T(8,128)(2,1)S(1)} %get-tuple-element.512.refs_2_), channel_id=1, source_target_pairs={{0,4},{4,0},{8,12},{12,8},{16,20},{20,16},{24,28},{28,24},{1,5},{5... | collective-permute-start | bytes 884744 | tf_op jit(solution)/shard_map/ppermute | solution.py:737
  443.7 26.0 %collective-permute-start.66 = (bf16[384,768]{1,0:T(8,128)(2,1)S(1)}, bf16[384,768]{1,0:T(8,128)(2,1)S(1)}, u32[]{:S(2)}, u32[]{:S(2)}) collective-permute-start(bf16[384,768]{1,0:T(8,128)(2,1)S(1)} %shard_map.412), channel_id=1, source_target_pairs={{0,2},{2,0},{1,3},{3,1},{4,6},{6,4},{5,7},{7,5},{8,10},{10,8},{9,1... | collective-permute-start | bytes 1769480 | tf_op jit(solution)/shard_map/ppermute | solution.py:29
  468.2 23.7 %collective-permute-start.89 = (bf16[4,96,768]{2,1,0:T(8,128)(2,1)S(1)}, bf16[4,96,768]{2,1,0:T(8,128)(2,1)S(1)}, u32[]{:S(2)}, u32[]{:S(2)}) collective-permute-start(bf16[4,96,768]{2,1,0:T(8,128)(2,1)S(1)} %shard_map.424.refs_2_.refs_1_), channel_id=1, source_target_pairs={{0,4},{4,0},{8,12},{12,8},{16,20},{20,16},{24,28},{28,24},{1,5},{5... | collective-permute-start | bytes 1769480 | tf_op jit(solution)/shard_map/ppermute | solution.py:745
  468.3 25.9 %collective-permute-start.90 = (bf16[4,96,768]{2,1,0:T(8,128)(2,1)S(1)}, bf16[4,96,768]{2,1,0:T(8,128)(2,1)}, u32[]{:S(2)}, u32[]{:S(2)}) collective-permute-start(bf16[4,96,768]{2,1,0:T(8,128)(2,1)S(1)} %shard_map.428.refs_2_.refs_1_), channel_id=1, source_target_pairs={{0,8},{4,12},{8,0},{12,4},{16,24},{20,28},{24,16},{28,20},{1,9},{5... | collective-permute-start | bytes 1769480 | tf_op jit(solution)/shard_map/ppermute | solution.py:745
  474.4 23.5 %collective-permute-start.88 = (bf16[4,80,768]{2,1,0:T(8,128)(2,1)S(1)}, bf16[4,80,768]{2,1,0:T(8,128)(2,1)S(1)}, u32[]{:S(2)}, u32[]{:S(2)}) collective-permute-start(bf16[4,80,768]{2,1,0:T(8,128)(2,1)S(1)} %shard_map.434.refs_2_.refs_1_), channel_id=1, source_target_pairs={{0,8},{4,12},{8,0},{12,4},{16,24},{20,28},{24,16},{28,20},{1,9},{5... | collective-permute-start | bytes 1474568 | tf_op jit(solution)/shard_map/ppermute | solution.py:745
  (185 other events, 1947.5 us)

commit v6 on v5

--- a/solution.py
+++ b/solution.py
@@ -1366,9 +1366,10 @@
                 after=[token],
             )
             token = tokens_grad
+            (down_out,) = unpacked_rows(0, strands[1], [square[::-1]], [down_out], after=[token])
+            token = down_out
         if step == 4:
             (up_out,) = unpacked_rows(0, strands[0], [square], [up_out], after=[token])
-            (down_out,) = unpacked_rows(0, strands[1], [square[::-1]], [down_out])
     k_out, v_out, o_out = unpacked_rows(0, second_chain, flat[:3], turned_out[1:])
     shapes = [(LAYERS, model)] * 7 + [(LAYERS, local)] * 2
     q_out, table_half, *vector_out = call(

time: 507 us -> 529 us (1.043)
  starting transfers between devices: 99.2 us -> 110 us
  waiting for transfers between devices: 181 us -> 188 us
  local copies, waits for them, and re-layouts: 28.3 us -> 34.1 us
    ppermute x18, waiting for transfers between devices: 59.5 us -> 70.9 us  [advance(): self.parts = [kept, lax.ppermute(sent, 'wide', self.wide.pairs(name))]]
    ppermute x18, starting transfers between devices: 19.4 us -> 26.3 us  [advance(): self.parts = [kept, lax.ppermute(sent, 'wide', self.wide.pairs(name))]]
    unnamed x236 -> x244, local copies, waits for them, and re-layouts: 23.6 us -> 28.8 us
  transfers between devices with their start and end apart: 91 -> 91, of which waited for: 42 -> 38; matrix products, arithmetic and copies ran while one was open for 3% -> 3% of each run, Pallas kernels for 32% -> 30%
where the time goes in v6:
time: 529 us; the launch traced here: 521 us
  waiting for transfers between devices  188 us (36%)
  Pallas kernels  173 us (33%)
  starting transfers between devices  110 us (21%)
  local copies, waits for them, and re-layouts  34.1 us (6%)
  other arithmetic  7.47 us (1%)
    pallas_call x109, Pallas kernels, call(): pl.pallas_call(body, **{} if grid is None else {'grid': grid}, in_specs=s...  173 us
    ppermute x26, waiting for transfers between devices, over_chip(): return lax.ppermute(value, 'narrow', CHIP_SWAP)  79.8 us
    ppermute x18, waiting for transfers between devices, advance(): self.parts = [kept, lax.ppermute(sent, 'wide', self.wide.pairs(name))]  70.9 us
    ppermute x29, starting transfers between devices, over_core(): return lax.ppermute(value, 'narrow', CORE_SWAP)  41.6 us
    ppermute x18, waiting for transfers between devices, advance(): self.parts = [sent, lax.ppermute(sent, 'wide', self.wide.pairs(name))]  29.4 us
    unnamed x244, local copies, waits for them, and re-layouts  28.8 us
    ppermute x18, starting transfers between devices, advance(): self.parts = [kept, lax.ppermute(sent, 'wide', self.wide.pairs(name))]  26.3 us
    ppermute x18, starting transfers between devices, advance(): self.parts = [sent, lax.ppermute(sent, 'wide', self.wide.pairs(name))]  24 us
  transfers between devices with their start and end apart: 91, of which 38 were waited for; matrix products, arithmetic and copies ran while one was open for 3% of the time, Pallas kernels for 30%

profile of v6, /device:TPU:1, one launch (start us, length us, event | category | flops | bytes accessed | tf_op | source)
XLA Modules:
  0.0 520.7 jit_solution(2778571858577178128)
XLA Ops:
  36.9 5.8 %shard_map.336 = (bf16[256,384]{1,0:T(8,128)(2,1)S(1)}, f32[256,384]{1,0:T(8,128)S(1)}, f32[8,256]{1,0:T(8,128)S(1)}, bf16[256,768]{1,0:T(8,128)(2,1)S(1)}) custom-call(s32[9]{0:T(128)S(1)} %pad_add_fusion.1.refs_0_, bf16[256,384]{1,0:T(8,128)(2,1)S(1)} %get-tuple-element.554.refs_1_.refs_6_, bf16[6,256,768]{2,1,0:T(8,128)(2,1)S(1)} %get-tuple-element.285.refs_2_.refs_1_, ...), custom_call_target="tpu_custom_call" | custom-call | flops 24000000000 | bytes 1 | tf_op jit(solution)/shard_map/pallas_call | solution.py:93
  109.4 14.2 %collective-permute-done.24.refs_2_ = bf16[256,768]{1,0:T(8,128)(2,1)S(1)} collective-permute-done((bf16[256,768]{1,0:T(8,128)(2,1)S(1)}, bf16[256,768]{1,0:T(8,128)(2,1)S(1)}, u32[]{:S(2)}, u32[]{:S(2)}) %collective-permute-start.24) | collective-permute-done | bytes 393248 | tf_op jit(solution)/shard_map/ppermute | solution.py:29
  141.1 7.7 %collective-permute-done.23.refs_4_ = bf16[256,768]{1,0:T(8,128)(2,1)S(1)} collective-permute-done((bf16[256,768]{1,0:T(8,128)(2,1)S(1)}, bf16[256,768]{1,0:T(8,128)(2,1)S(1)}, u32[]{:S(2)}, u32[]{:S(2)}) %collective-permute-start.23) | collective-permute-done | bytes 393248 | tf_op jit(solution)/shard_map/ppermute | solution.py:29
  173.7 6.9 %collective-permute-done.28.refs_2_ = bf16[256,768]{1,0:T(8,128)(2,1)S(1)} collective-permute-done((bf16[256,768]{1,0:T(8,128)(2,1)S(1)}, bf16[256,768]{1,0:T(8,128)(2,1)S(1)}, u32[]{:S(2)}, u32[]{:S(2)}) %collective-permute-start.28) | collective-permute-done | bytes 393248 | tf_op jit(solution)/shard_map/ppermute | solution.py:29
  182.5 6.5 %collective-permute-done.29.refs_2_ = bf16[256,768]{1,0:T(8,128)(2,1)S(1)} collective-permute-done((bf16[256,768]{1,0:T(8,128)(2,1)S(1)}, bf16[256,768]{1,0:T(8,128)(2,1)S(1)}, u32[]{:S(2)}, u32[]{:S(2)}) %collective-permute-start.29) | collective-permute-done | bytes 393248 | tf_op jit(solution)/shard_map/ppermute | solution.py:29
  189.9 7.6 %collective-permute-done.30.refs_2_ = bf16[256,768]{1,0:T(8,128)(2,1)S(1)} collective-permute-done((bf16[256,768]{1,0:T(8,128)(2,1)S(1)}, bf16[256,768]{1,0:T(8,128)(2,1)S(1)}, u32[]{:S(2)}, u32[]{:S(2)}) %collective-permute-start.30) | collective-permute-done | bytes 393248 | tf_op jit(solution)/shard_map/ppermute | solution.py:29
  202.7 7.4 %shard_map.363 = (bf16[768,128]{1,0:T(8,128)(2,1)S(1)}, f32[3,256,256]{2,1,0:T(8,128)S(1)}, bf16[3,256,256]{2,1,0:T(8,128)(2,1)S(1)}) custom-call(s32[9]{0:T(128)S(1)} %pad_add_fusion.1.refs_0_, bf16[6,256,768]{2,1,0:T(8,128)(2,1)S(1)} %get-tuple-element.304.refs_2_.refs_1_, bf16[6,768,256]{2,1,0:T(8,128)(2,1)S(1)} %get-tuple-element.305.refs_3_.refs_2_, ...), custom_call_target="tpu_custom_call" | custom-call | bytes 1 | tf_op jit(solution)/shard_map/pallas_call | solution.py:93
  210.2 7.4 %shard_map.364 = (bf16[768,128]{1,0:T(8,128)(2,1)S(1)}, f32[3,256,256]{2,1,0:T(8,128)S(1)}, bf16[3,256,256]{2,1,0:T(8,128)(2,1)S(1)}) custom-call(s32[9]{0:T(128)S(1)} %pad_add_fusion.1.refs_0_, bf16[6,256,768]{2,1,0:T(8,128)(2,1)S(1)} %get-tuple-element.304.refs_2_.refs_1_, bf16[6,768,256]{2,1,0:T(8,128)(2,1)S(1)} %get-tuple-element.305.refs_3_.refs_2_, ...), custom_call_target="tpu_custom_call" | custom-call | bytes 1 | tf_op jit(solution)/shard_map/pallas_call | solution.py:93
  217.6 7.6 %shard_map.365 = (bf16[768,128]{1,0:T(8,128)(2,1)S(1)}, f32[3,256,256]{2,1,0:T(8,128)S(1)}, bf16[3,256,256]{2,1,0:T(8,128)(2,1)S(1)}) custom-call(s32[9]{0:T(128)S(1)} %pad_add_fusion.1.refs_0_, bf16[6,256,768]{2,1,0:T(8,128)(2,1)S(1)} %get-tuple-element.304.refs_2_.refs_1_, bf16[6,768,256]{2,1,0:T(8,128)(2,1)S(1)} %get-tuple-element.305.refs_3_.refs_2_, ...), custom_call_target="tpu_custom_call" | custom-call | bytes 1 | tf_op jit(solution)/shard_map/pallas_call | solution.py:93
  242.6 8.6 %collective-permute-done.40.refs_2_ = bf16[384,768]{1,0:T(8,128)(2,1)S(1)} collective-permute-done((bf16[384,768]{1,0:T(8,128)(2,1)S(1)}, bf16[384,768]{1,0:T(8,128)(2,1)S(1)}, u32[]{:S(2)}, u32[]{:S(2)}) %collective-permute-start.40) | collective-permute-done | bytes 589856 | tf_op jit(solution)/shard_map/ppermute | solution.py:737
  284.9 6.7 %collective-permute-done.47.refs_2_ = bf16[256,768]{1,0:T(8,128)(2,1)S(1)} collective-permute-done((bf16[256,768]{1,0:T(8,128)(2,1)S(1)}, bf16[256,768]{1,0:T(8,128)(2,1)S(1)}, u32[]{:S(2)}, u32[]{:S(2)}) %collective-permute-start.47) | collective-permute-done | bytes 393248 | tf_op jit(solution)/shard_map/ppermute | solution.py:29
  305.2 7.4 %shard_map.393 = (bf16[768,128]{1,0:T(8,128)(2,1)S(1)}, f32[3,256,256]{2,1,0:T(8,128)S(1)}, bf16[3,256,256]{2,1,0:T(8,128)(2,1)S(1)}) custom-call(s32[9]{0:T(128)S(1)} %copy-done.92, bf16[6,256,768]{2,1,0:T(8,128)(2,1)S(1)} %copy-done.11, bf16[6,768,256]{2,1,0:T(8,128)(2,1)S(1)} %copy-done.13, s32[3,1,256]{2,1,0:T(1,128)S(1)} %slice.82.refs_4_.refs_3_, ...), custom_call_target="tpu_custom_call" | custom-call | bytes 1 | tf_op jit(solution)/shard_map/pallas_call | solution.py:93
  319.1 8.2 %collective-permute-done.53.refs_1_ = bf16[96,768]{1,0:T(8,128)(2,1)S(1)} collective-permute-done((bf16[96,768]{1,0:T(8,128)(2,1)S(1)}, bf16[96,768]{1,0:T(8,128)(2,1)S(1)}, u32[]{:S(2)}, u32[]{:S(2)}) %collective-permute-start.53) | collective-permute-done | bytes 147488 | tf_op jit(solution)/shard_map/ppermute | solution.py:737
  330.2 7.4 %shard_map.396 = (bf16[768,128]{1,0:T(8,128)(2,1)S(1)}, f32[3,256,256]{2,1,0:T(8,128)S(1)}, bf16[3,256,256]{2,1,0:T(8,128)(2,1)S(1)}) custom-call(s32[9]{0:T(128)S(1)} %copy-done.92, bf16[6,256,768]{2,1,0:T(8,128)(2,1)S(1)} %copy-done.11, bf16[6,768,256]{2,1,0:T(8,128)(2,1)S(1)} %copy-done.13, s32[3,1,256]{2,1,0:T(1,128)S(1)} %slice.82.refs_4_.refs_3_, ...), custom_call_target="tpu_custom_call" | custom-call | bytes 1 | tf_op jit(solution)/shard_map/pallas_call | solution.py:93
  341.1 8.2 %collective-permute-done.56.refs_2_ = bf16[384,768]{1,0:T(8,128)(2,1)S(1)} collective-permute-done((bf16[384,768]{1,0:T(8,128)(2,1)S(1)}, bf16[384,768]{1,0:T(8,128)(2,1)S(1)}, u32[]{:S(2)}, u32[]{:S(2)}) %collective-permute-start.56) | collective-permute-done | bytes 589856 | tf_op jit(solution)/shard_map/ppermute | solution.py:737
  353.4 5.9 %collective-permute-start.58 = (bf16[3,256,256]{2,1,0:T(8,128)(2,1)S(1)}, bf16[3,256,256]{2,1,0:T(8,128)(2,1)S(1)}, u32[]{:S(2)}, u32[]{:S(2)}) collective-permute-start(bf16[3,256,256]{2,1,0:T(8,128)(2,1)S(1)} %get-tuple-element.478), channel_id=1, source_target_pairs={{0,1},{1,0},{2,3},{3,2},{4,5},{5,4},{6,7},{7,6},{8,9},{9,8},{10,11... | collective-permute-start | bytes 1179656 | tf_op jit(solution)/shard_map/ppermute | solution.py:25
  359.4 7.6 %shard_map.400 = (bf16[768,128]{1,0:T(8,128)(2,1)S(1)}, f32[3,256,256]{2,1,0:T(8,128)S(1)}, bf16[3,256,256]{2,1,0:T(8,128)(2,1)S(1)}) custom-call(s32[9]{0:T(128)S(1)} %copy-done.92, bf16[6,256,768]{2,1,0:T(8,128)(2,1)S(1)} %copy-done.11, bf16[6,768,256]{2,1,0:T(8,128)(2,1)S(1)} %copy-done.13, s32[3,1,256]{2,1,0:T(1,128)S(1)} %slice.82.refs_4_.refs_3_, ...), custom_call_target="tpu_custom_call" | custom-call | bytes 1 | tf_op jit(solution)/shard_map/pallas_call | solution.py:93
  405.7 14.4 %collective-permute-done.72.refs_1_ = bf16[96,768]{1,0:T(8,128)(2,1)S(1)} collective-permute-done((bf16[96,768]{1,0:T(8,128)(2,1)S(1)}, bf16[96,768]{1,0:T(8,128)(2,1)S(1)}, u32[]{:S(2)}, u32[]{:S(2)}) %collective-permute-start.72) | collective-permute-done | bytes 147488 | tf_op jit(solution)/shard_map/ppermute | solution.py:737
  427.7 6.4 %collective-permute-done.76.refs_1_ = bf16[1,96,768]{2,1,0:T(8,128)(2,1)S(1)} collective-permute-done((bf16[1,96,768]{2,1,0:T(8,128)(2,1)S(1)}, bf16[1,96,768]{2,1,0:T(8,128)(2,1)S(1)}, u32[]{:S(2)}, u32[]{:S(2)}) %collective-permute-start.76) | collective-permute-done | bytes 147488 | tf_op jit(solution)/shard_map/ppermute | solution.py:745
  435.8 10.8 %collective-permute-done.78.refs_1_ = bf16[2,96,768]{2,1,0:T(8,128)(2,1)S(1)} collective-permute-done((bf16[2,96,768]{2,1,0:T(8,128)(2,1)S(1)}, bf16[2,96,768]{2,1,0:T(8,128)(2,1)S(1)}, u32[]{:S(2)}, u32[]{:S(2)}) %collective-permute-start.78) | collective-permute-done | bytes 294944 | tf_op jit(solution)/shard_map/ppermute | solution.py:745
  449.4 10.1 %collective-permute-done.74.refs_2_ = bf16[160,768]{1,0:T(8,128)(2,1)S(1)} collective-permute-done((bf16[160,768]{1,0:T(8,128)(2,1)S(1)}, bf16[160,768]{1,0:T(8,128)(2,1)S(1)}, u32[]{:S(2)}, u32[]{:S(2)}) %collective-permute-start.74) | collective-permute-done | bytes 245792 | tf_op jit(solution)/shard_map/ppermute | solution.py:737
  462.5 11.9 %collective-permute-done.80.refs_1_ = bf16[80,768]{1,0:T(8,128)(2,1)S(1)} collective-permute-done((bf16[80,768]{1,0:T(8,128)(2,1)S(1)}, bf16[80,768]{1,0:T(8,128)(2,1)S(1)}, u32[]{:S(2)}, u32[]{:S(2)}) %collective-permute-start.80) | collective-permute-done | bytes 122912 | tf_op jit(solution)/shard_map/ppermute | solution.py:737
  477.3 7.2 %collective-permute-done.79.refs_1_ = bf16[48,768]{1,0:T(8,128)(2,1)S(1)} collective-permute-done((bf16[48,768]{1,0:T(8,128)(2,1)S(1)}, bf16[48,768]{1,0:T(8,128)(2,1)S(1)}, u32[]{:S(2)}, u32[]{:S(2)}) %collective-permute-start.79) | collective-permute-done | bytes 73760 | tf_op jit(solution)/shard_map/ppermute | solution.py:737
  501.0 8.1 %collective-permute-done.87.refs_2_ = bf16[4,48,768]{2,1,0:T(8,128)(2,1)S(1)} collective-permute-done((bf16[4,48,768]{2,1,0:T(8,128)(2,1)S(1)}, bf16[4,48,768]{2,1,0:T(8,128)(2,1)S(1)}, u32[]{:S(2)}, u32[]{:S(2)}) %collective-permute-start.87) | collective-permute-done | bytes 294944 | tf_op jit(solution)/shard_map/ppermute | solution.py:745
  (543 shorter events, 318.0 us)
Async XLA Ops:
  16.2 33.8 %collective-permute-start.12 = (bf16[2,768,768]{2,1,0:T(8,128)(2,1)}, bf16[2,768,768]{2,1,0:T(8,128)(2,1)S(1)}, u32[]{:S(2)}, u32[]{:S(2)}) collective-permute-start(bf16[2,768,768]{2,1,0:T(8,128)(2,1)} %refs_7_.25), channel_id=1, source_target_pairs={{0,1},{1,0},{2,3},{3,2},{4,5},{5,4},{6,7},{7,6},{8,9},{9,8},{10,11... | collective-permute-start | bytes 7077896 | tf_op jit(solution)/shard_map/ppermute | solution.py:25
  16.5 33.4 %collective-permute-start.13 = (bf16[2,768,768]{2,1,0:T(8,128)(2,1)}, bf16[2,768,768]{2,1,0:T(8,128)(2,1)S(1)}, u32[]{:S(2)}, u32[]{:S(2)}) collective-permute-start(bf16[2,768,768]{2,1,0:T(8,128)(2,1)} %refs_9_.13), channel_id=1, source_target_pairs={{0,1},{1,0},{2,3},{3,2},{4,5},{5,4},{6,7},{7,6},{8,9},{9,8},{10,11... | collective-permute-start | bytes 7077896 | tf_op jit(solution)/shard_map/ppermute | solution.py:25
  65.9 21.8 %collective-permute-start.14 = (bf16[256,768]{1,0:T(8,128)(2,1)S(1)}, bf16[256,768]{1,0:T(8,128)(2,1)S(1)}, u32[]{:S(2)}, u32[]{:S(2)}) collective-permute-start(bf16[256,768]{1,0:T(8,128)(2,1)S(1)} %get-tuple-element.292.refs_1_), channel_id=1, source_target_pairs={{0,2},{2,0},{1,3},{3,1},{4,6},{6,4},{5,7},{7,5},{8,10},{10,8},{9,1... | collective-permute-start | bytes 1179656 | tf_op jit(solution)/shard_map/ppermute | solution.py:29
  91.6 47.6 %collective-permute-start = (bf16[384,768]{1,0:T(8,128)(2,1)}, bf16[384,768]{1,0:T(8,128)(2,1)}, u32[]{:S(2)}, u32[]{:S(2)}) collective-permute-start(bf16[384,768]{1,0:T(8,128)(2,1)} %param.39), channel_id=1, source_target_pairs={{0,2},{2,0},{1,3},{3,1},{4,6},{6,4},{5,7},{7,5},{8,10},{10,8},{9,1... | collective-permute-start | bytes 1769480 | tf_op jit(solution)/shard_map/ppermute | solution.py:29
  96.7 38.3 %collective-permute-start.26 = (bf16[256,768]{1,0:T(8,128)(2,1)S(1)}, bf16[256,768]{1,0:T(8,128)(2,1)S(1)}, u32[]{:S(2)}, u32[]{:S(2)}) collective-permute-start(bf16[256,768]{1,0:T(8,128)(2,1)S(1)} %get-tuple-element.324.refs_1_), channel_id=1, source_target_pairs={{0,2},{2,0},{1,3},{3,1},{4,6},{6,4},{5,7},{7,5},{8,10},{10,8},{9,1... | collective-permute-start | bytes 1179656 | tf_op jit(solution)/shard_map/ppermute | solution.py:29
  109.2 22.8 %collective-permute-start.22 = (bf16[256,768]{1,0:T(8,128)(2,1)S(1)}, bf16[256,768]{1,0:T(8,128)(2,1)S(1)}, u32[]{:S(2)}, u32[]{:S(2)}) collective-permute-start(bf16[256,768]{1,0:T(8,128)(2,1)S(1)} %get-tuple-element.306.refs_1_), channel_id=1, source_target_pairs={{0,2},{2,0},{1,3},{3,1},{4,6},{6,4},{5,7},{7,5},{8,10},{10,8},{9,1... | collective-permute-start | bytes 1179656 | tf_op jit(solution)/shard_map/ppermute | solution.py:29
  126.4 25.0 %collective-permute-start.25 = (bf16[256,768]{1,0:T(8,128)(2,1)S(1)}, bf16[256,768]{1,0:T(8,128)(2,1)S(1)}, u32[]{:S(2)}, u32[]{:S(2)}) collective-permute-start(bf16[256,768]{1,0:T(8,128)(2,1)S(1)} %get-tuple-element.317.refs_3_), channel_id=1, source_target_pairs={{0,2},{2,0},{1,3},{3,1},{4,6},{6,4},{5,7},{7,5},{8,10},{10,8},{9,1... | collective-permute-start | bytes 1179656 | tf_op jit(solution)/shard_map/ppermute | solution.py:29
  168.6 60.1 %collective-permute-start.36 = (bf16[768,768]{1,0:T(8,128)(2,1)S(1)}, bf16[768,768]{1,0:T(8,128)(2,1)S(1)}, u32[]{:S(2)}, u32[]{:S(2)}) collective-permute-start(bf16[768,768]{1,0:T(8,128)(2,1)S(1)} %get-tuple-element.371.refs_18_), channel_id=1, source_target_pairs={{0,4},{4,0},{8,12},{12,8},{16,20},{20,16},{24,28},{28,24},{1,5},{5... | collective-permute-start | bytes 3538952 | tf_op jit(solution)/shard_map/ppermute | solution.py:737
  172.1 25.4 %collective-permute-start.30 = (bf16[256,768]{1,0:T(8,128)(2,1)S(1)}, bf16[256,768]{1,0:T(8,128)(2,1)S(1)}, u32[]{:S(2)}, u32[]{:S(2)}) collective-permute-start(bf16[256,768]{1,0:T(8,128)(2,1)S(1)} %get-tuple-element.342.refs_1_), channel_id=1, source_target_pairs={{0,2},{2,0},{1,3},{3,1},{4,6},{6,4},{5,7},{7,5},{8,10},{10,8},{9,1... | collective-permute-start | bytes 1179656 | tf_op jit(solution)/shard_map/ppermute | solution.py:29
  239.4 25.4 %collective-permute-start.45 = (bf16[256,768]{1,0:T(8,128)(2,1)S(1)}, bf16[256,768]{1,0:T(8,128)(2,1)S(1)}, u32[]{:S(2)}, u32[]{:S(2)}) collective-permute-start(bf16[256,768]{1,0:T(8,128)(2,1)S(1)} %get-tuple-element.397.refs_3_), channel_id=1, source_target_pairs={{0,2},{2,0},{1,3},{3,1},{4,6},{6,4},{5,7},{7,5},{8,10},{10,8},{9,1... | collective-permute-start | bytes 1179656 | tf_op jit(solution)/shard_map/ppermute | solution.py:29
  241.3 33.1 %collective-permute-start.44 = (bf16[384,768]{1,0:T(8,128)(2,1)S(1)}, bf16[384,768]{1,0:T(8,128)(2,1)S(1)}, u32[]{:S(2)}, u32[]{:S(2)}) collective-permute-start(bf16[384,768]{1,0:T(8,128)(2,1)S(1)} %get-tuple-element.395.refs_11_), channel_id=1, source_target_pairs={{0,8},{4,12},{8,0},{12,4},{16,24},{20,28},{24,16},{28,20},{1,9},{5... | collective-permute-start | bytes 1769480 | tf_op jit(solution)/shard_map/ppermute | solution.py:737
  268.5 32.2 %collective-permute-start.52 = (bf16[768,768]{1,0:T(8,128)(2,1)S(1)}, bf16[768,768]{1,0:T(8,128)(2,1)S(1)}, u32[]{:S(2)}, u32[]{:S(2)}) collective-permute-start(bf16[768,768]{1,0:T(8,128)(2,1)S(1)} %shard_map.390), channel_id=1, source_target_pairs={{0,1},{1,0},{2,3},{3,2},{4,5},{5,4},{6,7},{7,6},{8,9},{9,8},{10,11... | collective-permute-start | bytes 3538952 | tf_op jit(solution)/shard_map/ppermute | solution.py:25
  272.7 29.7 %collective-permute-start.51 = (bf16[768,768]{1,0:T(8,128)(2,1)S(1)}, bf16[768,768]{1,0:T(8,128)(2,1)S(1)}, u32[]{:S(2)}, u32[]{:S(2)}) collective-permute-start(bf16[768,768]{1,0:T(8,128)(2,1)S(1)} %shard_map.387), channel_id=1, source_target_pairs={{0,1},{1,0},{2,3},{3,2},{4,5},{5,4},{6,7},{7,6},{8,9},{9,8},{10,11... | collective-permute-start | bytes 3538952 | tf_op jit(solution)/shard_map/ppermute | solution.py:25
  312.6 56.6 %collective-permute-start.61 = (bf16[4,192,768]{2,1,0:T(8,128)(2,1)S(1)}, bf16[4,192,768]{2,1,0:T(8,128)(2,1)S(1)}, u32[]{:S(2)}, u32[]{:S(2)}) collective-permute-start(bf16[4,192,768]{2,1,0:T(8,128)(2,1)S(1)} %shard_map.395.refs_18_.refs_1_), channel_id=1, source_target_pairs={{0,4},{4,0},{8,12},{12,8},{16,20},{20,16},{24,28},{28,24},{1,5},{5... | collective-permute-start | bytes 3538952 | tf_op jit(solution)/shard_map/ppermute | solution.py:745
  314.4 26.0 %collective-permute-start.57 = (bf16[384,768]{1,0:T(8,128)(2,1)S(1)}, bf16[384,768]{1,0:T(8,128)(2,1)S(1)}, u32[]{:S(2)}, u32[]{:S(2)}) collective-permute-start(bf16[384,768]{1,0:T(8,128)(2,1)S(1)} %get-tuple-element.465.refs_21_), channel_id=1, source_target_pairs={{0,8},{4,12},{8,0},{12,4},{16,24},{20,28},{24,16},{28,20},{1,9},{5... | collective-permute-start | bytes 1769480 | tf_op jit(solution)/shard_map/ppermute | solution.py:737
  315.2 34.1 %collective-permute-start.56 = (bf16[384,768]{1,0:T(8,128)(2,1)S(1)}, bf16[384,768]{1,0:T(8,128)(2,1)S(1)}, u32[]{:S(2)}, u32[]{:S(2)}) collective-permute-start(bf16[384,768]{1,0:T(8,128)(2,1)S(1)} %get-tuple-element.458.refs_20_), channel_id=1, source_target_pairs={{0,4},{4,0},{8,12},{12,8},{16,20},{20,16},{24,28},{28,24},{1,5},{5... | collective-permute-start | bytes 1769480 | tf_op jit(solution)/shard_map/ppermute | solution.py:737
  337.6 29.3 %collective-permute-start.60 = (bf16[2,96,768]{2,1,0:T(8,128)(2,1)S(1)}, bf16[2,96,768]{2,1,0:T(8,128)(2,1)S(1)}, u32[]{:S(2)}, u32[]{:S(2)}) collective-permute-start(bf16[2,96,768]{2,1,0:T(8,128)(2,1)S(1)} %shard_map.397.refs_17_.refs_0_), channel_id=1, source_target_pairs={{0,4},{4,0},{8,12},{12,8},{16,20},{20,16},{24,28},{28,24},{1,5},{5... | collective-permute-start | bytes 884744 | tf_op jit(solution)/shard_map/ppermute | solution.py:745
  341.0 27.0 %collective-permute-start.63 = (bf16[192,768]{1,0:T(8,128)(2,1)S(1)}, bf16[192,768]{1,0:T(8,128)(2,1)S(1)}, u32[]{:S(2)}, u32[]{:S(2)}) collective-permute-start(bf16[192,768]{1,0:T(8,128)(2,1)S(1)} %get-tuple-element.472.refs_19_), channel_id=1, source_target_pairs={{0,4},{4,0},{8,12},{12,8},{16,20},{20,16},{24,28},{28,24},{1,5},{5... | collective-permute-start | bytes 884744 | tf_op jit(solution)/shard_map/ppermute | solution.py:737
  392.7 32.9 %collective-permute-start.77 = (bf16[4,96,768]{2,1,0:T(8,128)(2,1)S(1)}, bf16[4,96,768]{2,1,0:T(8,128)(2,1)S(1)}, u32[]{:S(2)}, u32[]{:S(2)}) collective-permute-start(bf16[4,96,768]{2,1,0:T(8,128)(2,1)S(1)} %copy-done.33), channel_id=1, source_target_pairs={{0,8},{4,12},{8,0},{12,4},{16,24},{20,28},{24,16},{28,20},{1,9},{5... | collective-permute-start | bytes 1769480 | tf_op jit(solution)/shard_map/ppermute | solution.py:745
  397.3 27.0 %collective-permute-start.70 = (bf16[320,768]{1,0:T(8,128)(2,1)S(1)}, bf16[320,768]{1,0:T(8,128)(2,1)S(1)}, u32[]{:S(2)}, u32[]{:S(2)}) collective-permute-start(bf16[320,768]{1,0:T(8,128)(2,1)S(1)} %get-tuple-element.514), channel_id=1, source_target_pairs={{0,8},{4,12},{8,0},{12,4},{16,24},{20,28},{24,16},{28,20},{1,9},{5... | collective-permute-start | bytes 1474568 | tf_op jit(solution)/shard_map/ppermute | solution.py:737
  400.7 24.2 %collective-permute-start.69 = (bf16[192,768]{1,0:T(8,128)(2,1)S(1)}, bf16[192,768]{1,0:T(8,128)(2,1)S(1)}, u32[]{:S(2)}, u32[]{:S(2)}) collective-permute-start(bf16[192,768]{1,0:T(8,128)(2,1)S(1)} %get-tuple-element.512.refs_2_), channel_id=1, source_target_pairs={{0,4},{4,0},{8,12},{12,8},{16,20},{20,16},{24,28},{28,24},{1,5},{5... | collective-permute-start | bytes 884744 | tf_op jit(solution)/shard_map/ppermute | solution.py:737
  449.1 43.0 %collective-permute-start.66 = (bf16[384,768]{1,0:T(8,128)(2,1)S(1)}, bf16[384,768]{1,0:T(8,128)(2,1)S(1)}, u32[]{:S(2)}, u32[]{:S(2)}) collective-permute-start(bf16[384,768]{1,0:T(8,128)(2,1)S(1)} %shard_map.412), channel_id=1, source_target_pairs={{0,2},{2,0},{1,3},{3,1},{4,6},{6,4},{5,7},{7,5},{8,10},{10,8},{9,1... | collective-permute-start | bytes 1769480 | tf_op jit(solution)/shard_map/ppermute | solution.py:29
  460.8 33.2 %collective-permute-start.86 = (bf16[4,96,768]{2,1,0:T(8,128)(2,1)S(1)}, bf16[4,96,768]{2,1,0:T(8,128)(2,1)S(1)}, u32[]{:S(2)}, u32[]{:S(2)}) collective-permute-start(bf16[4,96,768]{2,1,0:T(8,128)(2,1)S(1)} %shard_map.428.refs_2_.refs_1_), channel_id=1, source_target_pairs={{0,8},{4,12},{8,0},{12,4},{16,24},{20,28},{24,16},{28,20},{1,9},{5... | collective-permute-start | bytes 1769480 | tf_op jit(solution)/shard_map/ppermute | solution.py:745
  491.5 23.9 %collective-permute-start.90 = (bf16[4,96,768]{2,1,0:T(8,128)(2,1)S(1)}, bf16[4,96,768]{2,1,0:T(8,128)(2,1)S(1)}, u32[]{:S(2)}, u32[]{:S(2)}) collective-permute-start(bf16[4,96,768]{2,1,0:T(8,128)(2,1)S(1)} %shard_map.424.refs_2_.refs_1_), channel_id=1, source_target_pairs={{0,4},{4,0},{8,12},{12,8},{16,20},{20,16},{24,28},{28,24},{1,5},{5... | collective-permute-start | bytes 1769480 | tf_op jit(solution)/shard_map/ppermute | solution.py:745
  (189 other events, 1608.2 us)
